TPU v7x, 32 devices: a whole 2x2x4 slice. The times are simulated.
32 devices in a mesh: grp: 4 (over z), seq: 8 (over y, x, core).
Axes of the slice: x: 2, y: 2, z: 4, core: 2. Of those that a mesh axis runs over, the one named last changes fastest.
Arguments:
- tokens: bfloat16 [16384, 1024], P(('grp', 'seq')), may hold values from -6 to 6
- lengths: int32 [4], replicated, may hold values from 1024 to 4096, as said below
- mixer_gain: bfloat16 [1024], P('seq'), may hold values from 0.5 to 1.5
- gelu_weight: bfloat16 [1024, 1536], P('seq'), may hold values from -0.1875 to 0.1875
- input_weight: bfloat16 [1024, 1536], P('seq'), may hold values from -0.1875 to 0.1875
- conv_taps: bfloat16 [1536, 4], P('seq'), may hold values from -3 to 3
- conv_bias: bfloat16 [1536], P('seq'), may hold values from -2 to 2
- rgate_weight: bfloat16 [1536, 128], P('seq'), may hold values from -0.5 to 0.5
- rgate_bias: bfloat16 [1536], P('seq'), may hold values from -3 to 3
- igate_weight: bfloat16 [1536, 128], P('seq'), may hold values from -0.5 to 0.5
- igate_bias: bfloat16 [1536], P('seq'), may hold values from -3 to 3
- decay_param: bfloat16 [1536], P('seq')
- output_weight: bfloat16 [1536, 1024], P('seq'), may hold values from -0.625 to 0.625
- mlp_gain: bfloat16 [1024], P('seq'), may hold values from 0.5 to 1.5
- mlp_gate: bfloat16 [1024, 3072], P('seq'), may hold values from -0.1875 to 0.1875
- mlp_value: bfloat16 [1024, 3072], P('seq'), may hold values from -0.1875 to 0.1875
- mlp_down: bfloat16 [3072, 1024], P('seq'), may hold values from -0.21875 to 0.21875
- cotangent: bfloat16 [16384, 1024], P(('grp', 'seq')), may hold values from -6 to 6
Outputs:
- mixed: bfloat16 [16384, 1024], P(('grp', 'seq'))
- tokens_grad: float32 [16384, 1024], P(('grp', 'seq'))
- mixer_grad: float32 [1024], P('seq')
- gelu_grad: float32 [1024, 1536], P('seq')
- input_grad: float32 [1024, 1536], P('seq')
- taps_grad: float32 [1536, 4], P('seq')
- cbias_grad: float32 [1536], P('seq')
- rgate_grad: float32 [1536, 128], P('seq')
- rbias_grad: float32 [1536], P('seq')
- igate_grad: float32 [1536, 128], P('seq')
- ibias_grad: float32 [1536], P('seq')
- decay_grad: float32 [1536], P('seq')
- output_grad: float32 [1536, 1024], P('seq')
- mlpgain_grad: float32 [1024], P('seq')
- mlpgate_grad: float32 [1024, 3072], P('seq')
- mlpvalue_grad: float32 [1024, 3072], P('seq')
- mlpdown_grad: float32 [3072, 1024], P('seq')
Inputs may be any that keep to these rules, and one draw needn't show every extreme that they name: `lengths`: valid tokens of each slot, from its start; the rest of the slot is padding. Some slot has exactly 4096 and some exactly 1024.
All inputs are finite; a program needn't handle non-finite values.
Results may differ from a plain program's by a relative error of at most 0.0091.
Values may be sent and summed in bfloat16 or wider, within the bound.
A program may use at most 192 MiB of HBM per device.

v0:
```python
import jax
import jax.numpy as jnp
from jax import lax
from jax.sharding import PartitionSpec as P

epsilon = 1e-06
cfactor = 8.0


def passed_along(value, axis, steps):
    count = lax.axis_size(axis)
    leading, last = (max(0, -steps), min(count, count - steps))
    return lax.ppermute(value, axis, [(source, source + steps) for source in range(leading, last)])


def carried_in(value, axis, join, neutral, backward):
    count, mine = (lax.axis_size(axis), lax.axis_index(axis))
    pieces = jax.tree.map(lambda part: lax.all_gather(part, axis), value)
    if backward:
        pieces = jax.tree.map(lambda part: part[::-1], pieces)
        mine = count - 1 - mine
    so_far = jax.tree.map(
        lambda part, zero: jnp.full_like(part, 0) + jnp.asarray(zero, part.dtype), value, neutral
    )

    def step(position, so_far):
        longer = join(so_far, jax.tree.map(lambda part: part[position], pieces))
        return jax.tree.map(lambda new, old: jnp.where(position < mine, new, old), longer, so_far)

    return lax.fori_loop(0, count - 1, step, so_far)


def rms_norm(rows_in, gain):
    return rows_in * lax.rsqrt(jnp.mean(rows_in * rows_in, axis=-1, keepdims=True) + epsilon) * gain


def gelu_tanh(values):
    return jax.nn.gelu(values, approximate=True)


def matmul(left, right):
    return jnp.dot(left, right, preferred_element_type=jnp.float32)


def inner_rows(left, right):
    return lax.dot_general(
        left, right, (((0,), (0,)), ((), ())), preferred_element_type=jnp.float32
    )


def outer_cols(left, right):
    return lax.dot_general(
        left, right, (((1,), (1,)), ((), ())), preferred_element_type=jnp.float32
    )


def block_apply(values, weight, heads):
    count = values.shape[0]
    width = weight.shape[1]
    parts = values.reshape(count, heads, width)
    blocks = weight.reshape(heads, width, width)
    return jnp.einsum("rhi,hij->rhj", parts, blocks, preferred_element_type=jnp.float32).reshape(
        count, heads * width
    )


def block_back(grads, weight, heads):
    count = grads.shape[0]
    width = weight.shape[1]
    parts = grads.reshape(count, heads, width)
    blocks = weight.reshape(heads, width, width)
    return jnp.einsum("rhj,hij->rhi", parts, blocks, preferred_element_type=jnp.float32).reshape(
        count, heads * width
    )


def block_grad(values, grads, heads):
    count = values.shape[0]
    width = values.shape[1] // heads
    left = values.reshape(count, heads, width)
    right = grads.reshape(count, heads, width)
    return jnp.einsum("rhi,rhj->hij", left, right, preferred_element_type=jnp.float32).reshape(
        heads * width, width
    )


def chain_combine(earlier, later):
    return (earlier[0] * later[0], later[0] * earlier[1] + later[1])


def recurrence_gates(rgate_pre, igate_pre, conv_in, decay_in):
    rgate = jax.nn.sigmoid(rgate_pre)
    igate = jax.nn.sigmoid(igate_pre)
    log_decay = -cfactor * jax.nn.softplus(-decay_in) * rgate
    return (jnp.exp(log_decay), jnp.sqrt(-jnp.expm1(2.0 * log_decay)) * igate * conv_in)


def local(
    tokens,
    lengths,
    mixer_gain,
    gelu_weight,
    input_weight,
    conv_taps,
    conv_bias,
    rgate_weight,
    rgate_bias,
    igate_weight,
    igate_bias,
    decay_param,
    output_weight,
    mlp_gain,
    mlp_gate,
    mlp_value,
    mlp_down,
    cotangent,
):
    count = tokens.shape[0]
    width_lru = input_weight.shape[1]
    block = rgate_weight.shape[1]
    heads = width_lru // block
    taps_count = conv_taps.shape[1]
    rim = taps_count - 1
    seq_count = lax.axis_size("seq")
    slot_length = count * seq_count
    first_row = (lax.axis_index("grp") * seq_count + lax.axis_index("seq")) * count
    global_row = first_row + jnp.arange(count, dtype=jnp.int32)
    position = global_row % slot_length
    slot_of = global_row // slot_length
    slot_ids = jnp.arange(lengths.shape[0], dtype=jnp.int32)
    slot_len = jnp.sum(
        jnp.where(slot_of[:, None] == slot_ids[None, :], lengths[None, :], 0), axis=1
    )
    valid = (position < slot_len).astype(jnp.float32)[:, None]
    starts = (position > 0).astype(jnp.float32)[:, None]
    lag_masks = [(position >= lag).astype(jnp.float32)[:, None] for lag in range(taps_count)]
    zeros_lru = jnp.zeros((width_lru,), jnp.float32)
    ones_lru = jnp.ones((width_lru,), jnp.float32)
    (
        gain_one,
        gelu_full,
        input_full,
        taps_full,
        cbias_full,
        rgate_full,
        rbias_full,
        igate_full,
        ibias_full,
        decay_full,
        output_full,
        gain_two,
        mgate_full,
        mvalue_full,
        mdown_full,
    ) = (
        lax.all_gather(mixer_gain, "seq", axis=0, tiled=True),
        lax.all_gather(gelu_weight, "seq", axis=0, tiled=True),
        lax.all_gather(input_weight, "seq", axis=0, tiled=True),
        lax.all_gather(conv_taps, "seq", axis=0, tiled=True),
        lax.all_gather(conv_bias, "seq", axis=0, tiled=True),
        lax.all_gather(rgate_weight, "seq", axis=0, tiled=True),
        lax.all_gather(rgate_bias, "seq", axis=0, tiled=True),
        lax.all_gather(igate_weight, "seq", axis=0, tiled=True),
        lax.all_gather(igate_bias, "seq", axis=0, tiled=True),
        lax.all_gather(decay_param, "seq", axis=0, tiled=True),
        lax.all_gather(output_weight, "seq", axis=0, tiled=True),
        lax.all_gather(mlp_gain, "seq", axis=0, tiled=True),
        lax.all_gather(mlp_gate, "seq", axis=0, tiled=True),
        lax.all_gather(mlp_value, "seq", axis=0, tiled=True),
        lax.all_gather(mlp_down, "seq", axis=0, tiled=True),
    )
    inputs = tokens.astype(jnp.float32)
    normed_one, norm_one_back = jax.vjp(rms_norm, inputs, gain_one.astype(jnp.float32))
    normed_one = normed_one.astype(jnp.bfloat16)
    gate_pre = matmul(normed_one, gelu_full)
    gate_act, gate_back = jax.vjp(gelu_tanh, gate_pre)
    linear = matmul(normed_one, input_full)
    rim_in = passed_along(linear[count - rim :], "seq", 1)
    extended = jnp.concatenate([rim_in, linear], axis=0)
    taps_fwd = taps_full.astype(jnp.float32)
    conv = cbias_full.astype(jnp.float32) + taps_fwd[:, 0] * linear
    for lag in range(1, taps_count):
        conv = conv + taps_fwd[:, lag] * (extended[rim - lag : rim - lag + count] * lag_masks[lag])
    conv_low = conv.astype(jnp.bfloat16)
    conv_value = conv_low.astype(jnp.float32)
    rgate_pre = block_apply(conv_low, rgate_full, heads) + rbias_full.astype(jnp.float32)
    igate_pre = block_apply(conv_low, igate_full, heads) + ibias_full.astype(jnp.float32)
    (decay, inject), gates_back = jax.vjp(
        recurrence_gates, rgate_pre, igate_pre, conv_value, decay_full.astype(jnp.float32)
    )
    decay_used = decay * starts
    cum_decay, state_zero = lax.associative_scan(chain_combine, (decay_used, inject), axis=0)
    scanned = carried_in(
        (cum_decay[-1], state_zero[-1]), "seq", chain_combine, (ones_lru, zeros_lru), False
    )
    carry_in = scanned[1]
    state = state_zero + cum_decay * carry_in
    mixed_rec = (state * gate_act).astype(jnp.bfloat16)
    resid = inputs + matmul(mixed_rec, output_full)
    normed_two, norm_two_back = jax.vjp(rms_norm, resid, gain_two.astype(jnp.float32))
    normed_two = normed_two.astype(jnp.bfloat16)
    mgate_pre = matmul(normed_two, mgate_full)
    mvalue_pre = matmul(normed_two, mvalue_full)
    mgate_act, mgate_back = jax.vjp(gelu_tanh, mgate_pre)
    hidden = (mgate_act * mvalue_pre).astype(jnp.bfloat16)
    mixed = ((resid + matmul(hidden, mdown_full)) * valid).astype(jnp.bfloat16)
    (
        gain_one,
        gelu_full,
        input_full,
        taps_full,
        cbias_full,
        rgate_full,
        rbias_full,
        igate_full,
        ibias_full,
        decay_full,
        output_full,
        gain_two,
        mgate_full,
        mvalue_full,
        mdown_full,
    ) = (
        lax.all_gather(mixer_gain, "seq", axis=0, tiled=True),
        lax.all_gather(gelu_weight, "seq", axis=0, tiled=True),
        lax.all_gather(input_weight, "seq", axis=0, tiled=True),
        lax.all_gather(conv_taps, "seq", axis=0, tiled=True),
        lax.all_gather(conv_bias, "seq", axis=0, tiled=True),
        lax.all_gather(rgate_weight, "seq", axis=0, tiled=True),
        lax.all_gather(rgate_bias, "seq", axis=0, tiled=True),
        lax.all_gather(igate_weight, "seq", axis=0, tiled=True),
        lax.all_gather(igate_bias, "seq", axis=0, tiled=True),
        lax.all_gather(decay_param, "seq", axis=0, tiled=True),
        lax.all_gather(output_weight, "seq", axis=0, tiled=True),
        lax.all_gather(mlp_gain, "seq", axis=0, tiled=True),
        lax.all_gather(mlp_gate, "seq", axis=0, tiled=True),
        lax.all_gather(mlp_value, "seq", axis=0, tiled=True),
        lax.all_gather(mlp_down, "seq", axis=0, tiled=True),
    )
    taps_back = taps_full.astype(jnp.float32)
    grad_out = cotangent.astype(jnp.float32) * valid
    grad_out_low = grad_out.astype(jnp.bfloat16)
    down_grad = inner_rows(hidden, grad_out_low)
    grad_hidden = outer_cols(grad_out_low, mdown_full)
    grad_mgate = mgate_back(grad_hidden * mvalue_pre)[0].astype(jnp.bfloat16)
    grad_mvalue = (grad_hidden * mgate_act).astype(jnp.bfloat16)
    mgate_grad = inner_rows(normed_two, grad_mgate)
    mvalue_grad = inner_rows(normed_two, grad_mvalue)
    grad_ntwo = outer_cols(grad_mgate, mgate_full) + outer_cols(grad_mvalue, mvalue_full)
    grad_resid_norm, gain_two_grad = norm_two_back(grad_ntwo)
    grad_resid = grad_out + grad_resid_norm
    grad_mix = grad_resid.astype(jnp.bfloat16)
    output_grad = inner_rows(mixed_rec, grad_mix)
    grad_rec = outer_cols(grad_mix, output_full)
    grad_state = grad_rec * gate_act
    grad_gate = gate_back(grad_rec * state)[0].astype(jnp.bfloat16)
    decay_next = jnp.concatenate([decay_used[1:], jnp.ones((1, width_lru), jnp.float32)], axis=0)
    rev_prod, rev_adjoint = lax.associative_scan(
        chain_combine, (jnp.flip(decay_next, 0), jnp.flip(grad_state, 0)), axis=0
    )
    tail_prod = jnp.flip(rev_prod, 0)
    adjoint_zero = jnp.flip(rev_adjoint, 0)
    summary_decay = decay_used[0] * tail_prod[0]
    summary_adjoint = decay_used[0] * adjoint_zero[0]
    scanned_back = carried_in(
        (summary_decay, summary_adjoint), "seq", chain_combine, (ones_lru, zeros_lru), True
    )
    incoming = scanned_back[1]
    adjoint = adjoint_zero + tail_prod * incoming
    state_prev = jnp.concatenate([carry_in[None, :], state[:-1]], axis=0)
    grad_decay = adjoint * state_prev * starts
    grad_rpre, grad_ipre, grad_direct, decay_grad = gates_back((grad_decay, adjoint))
    rbias_grad = jnp.sum(grad_rpre, axis=0)
    ibias_grad = jnp.sum(grad_ipre, axis=0)
    grad_rlow = grad_rpre.astype(jnp.bfloat16)
    grad_ilow = grad_ipre.astype(jnp.bfloat16)
    rgate_grad = block_grad(conv_low, grad_rlow, heads)
    igate_grad = block_grad(conv_low, grad_ilow, heads)
    grad_conv = (
        grad_direct
        + block_back(grad_rlow, rgate_full, heads)
        + block_back(grad_ilow, igate_full, heads)
    )
    cbias_grad = jnp.sum(grad_conv, axis=0)
    taps_columns = []
    grad_extended = jnp.zeros((count + rim, width_lru), jnp.float32)
    for lag in range(taps_count):
        masked_term = grad_conv * lag_masks[lag]
        taps_columns.append(jnp.sum(masked_term * extended[rim - lag : rim - lag + count], axis=0))
        grad_extended = grad_extended + jnp.pad(
            taps_back[:, lag] * masked_term, ((rim - lag, lag), (0, 0))
        )
    taps_grad = jnp.stack(taps_columns, axis=1)
    rim_back = passed_along(grad_extended[:rim], "seq", -1)
    grad_linear = grad_extended[rim:] + jnp.pad(rim_back, ((count - rim, 0), (0, 0)))
    grad_lin = grad_linear.astype(jnp.bfloat16)
    input_grad = inner_rows(normed_one, grad_lin)
    gelu_grad = inner_rows(normed_one, grad_gate)
    grad_none = outer_cols(grad_lin, input_full) + outer_cols(grad_gate, gelu_full)
    grad_inputs_norm, gain_one_grad = norm_one_back(grad_none)
    tokens_grad = grad_resid + grad_inputs_norm
    partials = (
        gain_one_grad,
        gelu_grad,
        input_grad,
        taps_grad,
        cbias_grad,
        rgate_grad,
        rbias_grad,
        igate_grad,
        ibias_grad,
        decay_grad,
        output_grad,
        gain_two_grad,
        mgate_grad,
        mvalue_grad,
        down_grad,
    )
    summed_seq = (
        lax.psum_scatter(partials[0], "seq", scatter_dimension=0, tiled=True),
        lax.psum_scatter(partials[1], "seq", scatter_dimension=0, tiled=True),
        lax.psum_scatter(partials[2], "seq", scatter_dimension=0, tiled=True),
        lax.psum_scatter(partials[3], "seq", scatter_dimension=0, tiled=True),
        lax.psum_scatter(partials[4], "seq", scatter_dimension=0, tiled=True),
        lax.psum_scatter(partials[5], "seq", scatter_dimension=0, tiled=True),
        lax.psum_scatter(partials[6], "seq", scatter_dimension=0, tiled=True),
        lax.psum_scatter(partials[7], "seq", scatter_dimension=0, tiled=True),
        lax.psum_scatter(partials[8], "seq", scatter_dimension=0, tiled=True),
        lax.psum_scatter(partials[9], "seq", scatter_dimension=0, tiled=True),
        lax.psum_scatter(partials[10], "seq", scatter_dimension=0, tiled=True),
        lax.psum_scatter(partials[11], "seq", scatter_dimension=0, tiled=True),
        lax.psum_scatter(partials[12], "seq", scatter_dimension=0, tiled=True),
        lax.psum_scatter(partials[13], "seq", scatter_dimension=0, tiled=True),
        lax.psum_scatter(partials[14], "seq", scatter_dimension=0, tiled=True),
    )
    totals = lax.psum(tuple(summed_seq), "grp")
    return (
        mixed,
        tokens_grad,
        totals[0],
        totals[1],
        totals[2],
        totals[3],
        totals[4],
        totals[5],
        totals[6],
        totals[7],
        totals[8],
        totals[9],
        totals[10],
        totals[11],
        totals[12],
        totals[13],
        totals[14],
    )


def solution(mesh):
    placed = (
        P(("grp", "seq"), None),
        P(),
        P("seq"),
        P("seq", None),
        P("seq", None),
        P("seq", None),
        P("seq"),
        P("seq", None),
        P("seq"),
        P("seq", None),
        P("seq"),
        P("seq"),
        P("seq", None),
        P("seq"),
        P("seq", None),
        P("seq", None),
        P("seq", None),
        P(("grp", "seq"), None),
    )
    return jax.shard_map(
        local,
        mesh=mesh,
        in_specs=placed,
        out_specs=(
            P(("grp", "seq"), None),
            P(("grp", "seq"), None),
            P("seq"),
            P("seq", None),
            P("seq", None),
            P("seq", None),
            P("seq"),
            P("seq", None),
            P("seq"),
            P("seq", None),
            P("seq"),
            P("seq"),
            P("seq", None),
            P("seq"),
            P("seq", None),
            P("seq", None),
            P("seq", None),
        ),
        check_vma=False,
    )
```

profile of v0, /device:TPU:0, one launch (start us, length us, event | category | flops | bytes accessed | tf_op | source)
XLA Modules:
  0.0 1853.3 jit_solution(4062831445635098114)
XLA Ops:
  12.3 10.2 all-gather.1
  22.5 8.9 all-gather
  31.6 10.3 all_gather.73
  44.2 23.7 %all-reduce.92 = (bf16[1536]{0:T(1024)(128)(2,1)S(1)}, bf16[1536]{0:T(1024)(128)(2,1)S(1)}, bf16[1536]{0:T(1024)(128)(2,1)S(1)}, bf16[1536]{0:T(1024)(128)(2,1)S(1)}) all-reduce(bf16[1536]{0:T(1024)(128)(2,1)S(1)} %dynamic-update-slice, bf16[1536]{0:T(1024)(128)(2,1)S(1)} %dynamic-update-slice.1, ...), channel_id=1, replica_groups=mesh['grp'=4,'seq'=8] {'seq'}, use_global_device_ids=true, to_apply=%add.79 | all-reduce | flops 6144 | bytes 24576
  75.5 11.6 all_gather.75
  88.3 8.7 all-gather.4
  98.2 7.8 add_convert_fusion
  275.8 7.3 slice.671
  400.9 9.7 pad.258
  410.6 9.6 pad.259
  421.1 8.9 all-gather.3
  432.7 9.7 pad.276
  442.4 9.6 pad.277
  452.8 8.7 all-gather.2
  461.6 13.2 slice.696
  474.8 12.8 slice.703
  487.6 13.1 slice.694
  501.9 11.8 multiply_convert_fusion.2
  520.7 9.1 fusion.106
  529.8 9.2 fusion.107
  539.1 14.2 multiply_convert_fusion
  553.3 7.9 fusion.108
  588.8 12.8 slice.698
  601.6 12.8 slice.700
  810.0 9.7 pad.313
  835.3 9.7 pad.295
  845.0 13.1 slice.764
  865.4 9.6 pad.294
  877.8 9.7 pad.312
  895.8 9.0 all-gather.5
  905.0 8.7 all-gather.6
  914.6 15.8 rev.16
  930.3 24.9 %rev.15 = f32[512,1536]{1,0:T(8,128)} reverse(f32[512,1536]{1,0:T(8,128)} %add.753), dimensions={0} | reverse | bytes 6291456 | tf_op jit(solution)/shard_map/jit(_flip)/rev | solution.py:262
  955.3 8.3 fusion.89
  1013.6 12.2 multiply_reduce_fusion.3
  1037.8 8.3 fusion.112
  1046.4 8.4 fusion.113
  1056.1 9.3 fusion.43
  1066.9 50.7 %reduce-scatter.20.cloned.1.call-done = f32[192,1024]{1,0:T(8,128)} async-done(((f32[1536,1024]{1,0:T(8,128)}), f32[192,1024]{1,0:T(8,128)}) %reduce-scatter.20.cloned.1.call-update) | async-done | bytes 786448 | tf_op jit(solution)/shard_map/reduce_scatter | solution.py:330
  1117.6 65.4 %reduce-scatter.12.cloned.1.call-done = f32[128,1536]{1,0:T(8,128)} async-done(((f32[1024,1536]{1,0:T(8,128)}), f32[128,1536]{1,0:T(8,128)}) %reduce-scatter.12.cloned.1.call-update) | async-done | bytes 786448 | tf_op jit(solution)/shard_map/reduce_scatter | solution.py:321
  1183.0 65.1 %reduce-scatter.14.cloned.1.call-done = f32[128,1536]{1,0:T(8,128)} async-done(((f32[1024,1536]{1,0:T(8,128)}), f32[128,1536]{1,0:T(8,128)}) %reduce-scatter.14.cloned.1.call-update) | async-done | bytes 786448 | tf_op jit(solution)/shard_map/reduce_scatter | solution.py:322
  1248.2 96.2 %reduce-scatter.22.cloned.1.call-done = f32[128,3072]{1,0:T(8,128)} async-done(((f32[1024,3072]{1,0:T(8,128)}), f32[128,3072]{1,0:T(8,128)}) %reduce-scatter.22.cloned.1.call-update) | async-done | bytes 1572880 | tf_op jit(solution)/shard_map/reduce_scatter | solution.py:332
  1344.3 96.3 %reduce-scatter.24.cloned.1.call-done = f32[128,3072]{1,0:T(8,128)} async-done(((f32[1024,3072]{1,0:T(8,128)}), f32[128,3072]{1,0:T(8,128)}) %reduce-scatter.24.cloned.1.call-update) | async-done | bytes 1572880 | tf_op jit(solution)/shard_map/reduce_scatter | solution.py:333
  1440.7 96.2 %reduce-scatter.26.cloned.1.call-done = f32[384,1024]{1,0:T(8,128)} async-done(((f32[3072,1024]{1,0:T(8,128)}), f32[384,1024]{1,0:T(8,128)}) %reduce-scatter.26.cloned.1.call-update) | async-done | bytes 1572880 | tf_op jit(solution)/shard_map/reduce_scatter | solution.py:334
  1542.3 7.4 multiply_convert_fusion.3
  1553.2 23.7 %all-reduce.89 = (f32[1024]{0:T(1024)S(1)}, f32[1536]{0:T(1024)S(1)}, f32[1536]{0:T(1024)S(1)}, f32[1536]{0:T(1024)S(1)}, f32[1536]{0:T(1024)S(1)}, /*index=5*/f32[1024]{0:T(1024)S(1)}) all-reduce(f32[1024]{0:T(1024)S(1)} %get-tuple-element.252, f32[1536]{0:T(1024)S(1)} %get-tuple-element.251, ...), channel_id=2, replica_groups=mesh['grp'=4,'seq'=8] {'seq'}, use_global_device_ids=true, to_apply=%region_10.11.clone | all-reduce | flops 8192 | bytes 65536
  1581.8 13.4 all-reduce.90
  1595.2 241.3 %all-reduce.95.cloned.1.call-done = (f32[128,1536]{1,0:T(8,128)}, f32[128,1536]{1,0:T(8,128)}, f32[192,128]{1,0:T(8,128)}, f32[192,128]{1,0:T(8,128)}, f32[192,1...) async-done(((f32[128,1536]{1,0:T(8,128)}, f32[128,1536]{1,0:T(8,128)}, f32[192,128]{1,0:T(8,128)}, f32[192,128]{1,0:T(8,128)}, ...) | async-done | bytes 7274512 | tf_op jit(solution)/shard_map/psum | solution.py:336
  (759 shorter events, 661.6 us)
Async XLA Ops:
  7.2 34.7 %copy-start.141 = (u32[32]{0:T(128)S(1)}, u32[32]{0:T(128)}, u32[]{:S(2)}) copy-start(u32[32]{0:T(128)} %constant.295) | copy-start | bytes 388
  7.2 24.3 %copy-start.83 = (bf16[192,128]{1,0:T(8,128)(2,1)S(1)}, bf16[192,128]{1,0:T(8,128)(2,1)}, u32[]{:S(2)}) copy-start(bf16[192,128]{1,0:T(8,128)(2,1)} %param.29) | copy-start | bytes 147460
  7.2 36.0 %copy-start.148 = (bf16[192]{0:T(256)(128)(2,1)S(1)}, bf16[192]{0:T(256)(128)(2,1)}, u32[]{:S(2)}) copy-start(bf16[192]{0:T(256)(128)(2,1)} %param.33) | copy-start | bytes 1156
  7.3 36.2 %copy-start.149 = (bf16[192]{0:T(256)(128)(2,1)S(1)}, bf16[192]{0:T(256)(128)(2,1)}, u32[]{:S(2)}) copy-start(bf16[192]{0:T(256)(128)(2,1)} %param.28) | copy-start | bytes 1156
  7.3 36.5 %copy-start.150 = (bf16[192]{0:T(256)(128)(2,1)S(1)}, bf16[192]{0:T(256)(128)(2,1)}, u32[]{:S(2)}) copy-start(bf16[192]{0:T(256)(128)(2,1)} %param.30) | copy-start | bytes 1156
  7.3 36.7 %copy-start.151 = (bf16[192]{0:T(256)(128)(2,1)S(1)}, bf16[192]{0:T(256)(128)(2,1)}, u32[]{:S(2)}) copy-start(bf16[192]{0:T(256)(128)(2,1)} %param.32) | copy-start | bytes 1156
  7.3 60.7 %copy-start.143 = (s32[4]{0:T(128)S(1)}, s32[4]{0:T(128)}, u32[]{:S(2)}) copy-start(s32[4]{0:T(128)} %param.23) | copy-start | bytes 52
  7.3 61.4 %all-gather.14.cloned.1.call-start = ((), (), s32[]{:S(2)}) async-start(), calls=%async_computation.9 | async-start | bytes 3538944 | tf_op jit(solution)/shard_map/all_gather | solution.py:158
  8.0 493.8 %all-gather.16.cloned.1.call-start = ((), (), s32[]{:S(2)}) async-start(), calls=%async_computation.10 | async-start | bytes 3538944 | tf_op jit(solution)/shard_map/all_gather | solution.py:157
  8.8 504.9 %all-gather.18.cloned.1.call-start = ((), (), s32[]{:S(2)}) async-start(), calls=%async_computation.11 | async-start | bytes 3538944 | tf_op jit(solution)/shard_map/all_gather | solution.py:166
  9.5 511.2 %all-gather.20.cloned.1.call-start = ((), (), s32[]{:S(2)}) async-start(), calls=%async_computation.12 | async-start | bytes 7077888 | tf_op jit(solution)/shard_map/all_gather | solution.py:168
  10.1 519.7 %all-gather.22.cloned.1.call-start = ((), (), s32[]{:S(2)}) async-start(), calls=%async_computation.13 | async-start | bytes 7077888 | tf_op jit(solution)/shard_map/all_gather | solution.py:169
  10.7 528.4 %all-gather.24.cloned.1.call-start = ((), (), s32[]{:S(2)}) async-start(), calls=%async_computation.14 | async-start | bytes 7077888 | tf_op jit(solution)/shard_map/all_gather | solution.py:170
  11.3 1055.6 %reduce-scatter.16.cloned.1.call-start = ((), (), s32[]{:S(2)}) async-start(), calls=%async_computation.17 | async-start | bytes 884736 | tf_op jit(solution)/shard_map/reduce_scatter | solution.py:325
  11.3 86.3 %copy-start.98 = (f32[512]{0:T(512)}, f32[512]{0:T(512)S(1)}, u32[]{:S(2)}) copy-start(f32[512]{0:T(512)S(1)} %get-tuple-element.410) | copy-start | bytes 6148
  11.3 86.3 %copy-start.100 = (f32[512]{0:T(512)}, f32[512]{0:T(512)S(1)}, u32[]{:S(2)}) copy-start(f32[512]{0:T(512)S(1)} %get-tuple-element.411) | copy-start | bytes 6148
  11.4 86.2 %copy-start.96 = (f32[512]{0:T(512)}, f32[512]{0:T(512)S(1)}, u32[]{:S(2)}) copy-start(f32[512]{0:T(512)S(1)} %compare_convert_fusion.5) | copy-start | bytes 6148
  12.3 60.2 %copy-start.128 = (f32[512]{0:T(512)}, f32[512]{0:T(512)S(1)}, u32[]{:S(2)}) copy-start(f32[512]{0:T(512)S(1)} %fusion.77) | copy-start | bytes 6148
  22.5 50.0 %copy-start.89 = (f32[8,1,128]{2,1,0:T(1,128)}, f32[8,1,128]{2,1,0:T(1,128)S(1)}, u32[]{:S(2)}) copy-start(f32[8,1,128]{2,1,0:T(1,128)S(1)} %convert_element_type.156) | copy-start | bytes 12292
  31.6 66.0 %copy-start.75 = (f32[1536]{0:T(1024)}, f32[1536]{0:T(1024)S(1)}, u32[]{:S(2)}) copy-start(f32[1536]{0:T(1024)S(1)} %get-tuple-element.254) | copy-start | bytes 18436
  31.6 66.0 %copy-start.77 = (f32[1536]{0:T(1024)}, f32[1536]{0:T(1024)S(1)}, u32[]{:S(2)}) copy-start(f32[1536]{0:T(1024)S(1)} %get-tuple-element.255) | copy-start | bytes 18436
  31.6 66.0 %copy-start.79 = (f32[1536]{0:T(1024)}, f32[1536]{0:T(1024)S(1)}, u32[]{:S(2)}) copy-start(f32[1536]{0:T(1024)S(1)} %get-tuple-element.256) | copy-start | bytes 18436
  31.6 66.0 %copy-start.81 = (f32[1536]{0:T(1024)}, f32[1536]{0:T(1024)S(1)}, u32[]{:S(2)}) copy-start(f32[1536]{0:T(1024)S(1)} %get-tuple-element.257) | copy-start | bytes 18436
  41.9 64.9 %copy-start.35 = (bf16[1536,128]{1,0:T(8,128)(2,1)}, bf16[1536,128]{1,0:T(8,128)(2,1)S(1)}, u32[]{:S(2)}) copy-start(bf16[1536,128]{1,0:T(8,128)(2,1)S(1)} %all_gather.73) | copy-start | bytes 1179652
  68.0 51.9 %copy-start.55 = (f32[1536]{0:T(1024)}, f32[1536]{0:T(1024)S(1)}, u32[]{:S(2)}) copy-start(f32[1536]{0:T(1024)S(1)} %fusion.64) | copy-start | bytes 18436
  74.2 23.4 %collective-permute-start = (f32[3,1536]{1,0:T(4,128)S(1)}, f32[3,1536]{1,0:T(4,128)S(1)}, u32[]{:S(2)}, u32[]{:S(2)}) collective-permute-start(f32[3,1536]{1,0:T(4,128)S(1)} %slice.788), channel_id=1, source_target_pairs={{0,1},{1,2},{2,3},{3,4},{4,5},{5,6},{6,7},{8,9},{9,10},{10,11},{11... | collective-permute-start | bytes 55304 | tf_op jit(solution)/shard_map/ppermute | solution.py:13
  474.8 27.1 %copy-start.90 = (f32[8,1,128]{2,1,0:T(1,128)S(1)}, f32[8,1,128]{2,1,0:T(1,128)}, u32[]{:S(2)}) copy-start(f32[8,1,128]{2,1,0:T(1,128)} %copy-done.89) | copy-start | bytes 12292
  474.8 27.1 %copy-start.129 = (f32[512]{0:T(512)S(1)}, f32[512]{0:T(512)}, u32[]{:S(2)}) copy-start(f32[512]{0:T(512)} %copy-done.128) | copy-start | bytes 6148
  720.5 20.4 %copy-start.71 = (f32[3,1536]{1,0:T(4,128)S(1)}, f32[3,1536]{1,0:T(4,128)}, u32[]{:S(2)}) copy-start(f32[3,1536]{1,0:T(4,128)} %slice.734) | copy-start | bytes 55300
  720.5 20.4 %copy-start.72 = (f32[3,1536]{1,0:T(4,128)S(1)}, f32[3,1536]{1,0:T(4,128)}, u32[]{:S(2)}) copy-start(f32[3,1536]{1,0:T(4,128)} %slice.751) | copy-start | bytes 55300
  720.6 20.4 %copy-start.114 = (f32[1,1536]{1,0:T(1,128)S(1)}, f32[1,1536]{1,0:T(1,128)}, u32[]{:S(2)}) copy-start(f32[1,1536]{1,0:T(1,128)} %slice.860) | copy-start | bytes 18436
  893.6 21.0 %copy-start.19 = (f32[512,1536]{1,0:T(8,128)S(1)}, f32[512,1536]{1,0:T(8,128)}, u32[]{:S(2)}) copy-start(f32[512,1536]{1,0:T(8,128)} %add.762) | copy-start | bytes 9437188
  930.3 24.9 %copy-start.1 = (f32[512,1536]{1,0:T(8,128)S(1)}, f32[512,1536]{1,0:T(8,128)}, u32[]{:S(2)}) copy-start(f32[512,1536]{1,0:T(8,128)} %copy-done) | copy-start | bytes 9437188
  930.3 24.9 %copy-start.56 = (f32[1536]{0:T(1024)S(1)}, f32[1536]{0:T(1024)}, u32[]{:S(2)}) copy-start(f32[1536]{0:T(1024)} %copy-done.55) | copy-start | bytes 18436
  930.3 24.9 %copy-start.58 = (f32[1536]{0:T(1024)S(1)}, f32[1536]{0:T(1024)}, u32[]{:S(2)}) copy-start(f32[1536]{0:T(1024)} %convert_element_type.135) | copy-start | bytes 18436
  930.3 25.0 %copy-start.61 = (f32[1536]{0:T(1024)S(1)}, f32[1536]{0:T(1024)}, u32[]{:S(2)}) copy-start(f32[1536]{0:T(1024)} %convert_element_type.136) | copy-start | bytes 18436
  978.4 88.5 %reduce-scatter.18.cloned.1.call-start = ((), (), s32[]{:S(2)}) async-start(), calls=%async_computation.18 | async-start | bytes 884736 | tf_op jit(solution)/shard_map/reduce_scatter | solution.py:327
  984.4 133.2 %reduce-scatter.20.cloned.1.call-start = ((), (), s32[]{:S(2)}) async-start(), calls=%async_computation.19 | async-start | bytes 7077888 | tf_op jit(solution)/shard_map/reduce_scatter | solution.py:330
  991.0 192.0 %reduce-scatter.12.cloned.1.call-start = ((), (), s32[]{:S(2)}) async-start(), calls=%async_computation.15 | async-start | bytes 7077888 | tf_op jit(solution)/shard_map/reduce_scatter | solution.py:321
  998.0 250.1 %reduce-scatter.14.cloned.1.call-start = ((), (), s32[]{:S(2)}) async-start(), calls=%async_computation.16 | async-start | bytes 7077888 | tf_op jit(solution)/shard_map/reduce_scatter | solution.py:322
  1027.2 3.2 collective-permute-start.1
  1036.5 307.8 %reduce-scatter.22.cloned.1.call-start = ((), (), s32[]{:S(2)}) async-start(), calls=%async_computation.20 | async-start | bytes 14155776 | tf_op jit(solution)/shard_map/reduce_scatter | solution.py:332
  1046.1 394.5 %reduce-scatter.24.cloned.1.call-start = ((), (), s32[]{:S(2)}) async-start(), calls=%async_computation.21 | async-start | bytes 14155776 | tf_op jit(solution)/shard_map/reduce_scatter | solution.py:333
  1054.9 482.0 %reduce-scatter.26.cloned.1.call-start = ((), (), s32[]{:S(2)}) async-start(), calls=%async_computation.22 | async-start | bytes 14155776 | tf_op jit(solution)/shard_map/reduce_scatter | solution.py:334
  1065.4 515.4 %reduce-scatter.28.cloned.1.call-start = ((), (), s32[]{:S(2)}) async-start(), calls=%async_computation.23 | async-start | bytes 884736
  1066.8 769.7 %all-reduce.95.cloned.1.call-start = ((), (), s32[]{:S(2)}) async-start(), calls=%async_computation.24 | async-start | bytes 14548992 | tf_op jit(solution)/shard_map/psum | solution.py:336
  1549.7 27.7 %copy-start.133 = (f32[512]{0:T(512)S(1)}, f32[512]{0:T(512)}, u32[]{:S(2)}) copy-start(f32[512]{0:T(512)} %copy-done.132) | copy-start | bytes 6148
  1549.7 27.7 %copy-start.9 = (f32[512,1024]{1,0:T(8,128)S(1)}, f32[512,1024]{1,0:T(8,128)}, u32[]{:S(2)}) copy-start(f32[512,1024]{1,0:T(8,128)} %copy-done.8) | copy-start | bytes 6291460
  (126 other events, 937.9 us)
Sparse Core Ops, SparseCore 0:
  10.0 36.5 all-gather.13
  48.5 32.3 all-gather.15
  82.9 32.4 all-gather.17
  117.1 45.5 all-gather.19
  164.4 45.5 all-gather.21
  211.7 45.5 all-gather.23
  978.5 35.1 reduce-scatter.15
  1017.4 34.9 reduce-scatter.17
  1055.8 61.7 reduce-scatter.19
  1121.2 61.7 reduce-scatter.11
  1186.4 61.7 reduce-scatter.13
  1251.9 92.3 reduce-scatter.21
  1348.2 92.3 reduce-scatter.23
  1444.4 92.3 reduce-scatter.25
  1540.7 35.1 reduce-scatter.27
  1579.0 257.3 all-reduce.94
where the time goes:
time: 1880 us; the launch traced here: 1850 us
  waiting for transfers between devices  715 us (38%)
  local copies, waits for them, and re-layouts  624 us (33%)
  other arithmetic  196 us (10%)
  matrix products  150 us (8%)
  blocking collectives  146 us (8%)
    psum x1, waiting for transfers between devices, local(): totals = lax.psum(tuple(summed_seq), 'grp')  241 us
    slice x65, local copies, waits for them, and re-layouts, local(): lax.associative_scan(chain_combine, (jnp.flip(decay_next, 0), jnp.flip(gr...  220 us
    slice x60, local copies, waits for them, and re-layouts, local(): lax.associative_scan(chain_combine, (decay_used, inject), axis=0)  137 us
    reduce_scatter x1, waiting for transfers between devices, local(): lax.psum_scatter(partials[13], 'seq', scatter_dimension=0, tiled=True)  96.3 us
    reduce_scatter x1, waiting for transfers between devices, local(): lax.psum_scatter(partials[14], 'seq', scatter_dimension=0, tiled=True)  96.2 us
    reduce_scatter x1, waiting for transfers between devices, local(): lax.psum_scatter(partials[12], 'seq', scatter_dimension=0, tiled=True)  96.2 us
    pad x32, local copies, waits for them, and re-layouts, local(): lax.associative_scan(chain_combine, (decay_used, inject), axis=0)  87.1 us
    pad x32, local copies, waits for them, and re-layouts, local(): lax.associative_scan(chain_combine, (jnp.flip(decay_next, 0), jnp.flip(gr...  86 us
  transfers between devices with their start and end apart: 18, of which 8 were waited for; matrix products, arithmetic and copies ran while one was open for 29% of the time, Pallas kernels for 0%

commit v1 on v0

--- a/solution.py
+++ b/solution.py
@@ -1,6 +1,10 @@
+import functools
+
 import jax
 import jax.numpy as jnp
 from jax import lax
+from jax.experimental import pallas as pl
+from jax.experimental.pallas import tpu as pltpu
 from jax.sharding import PartitionSpec as P
 
 epsilon = 1e-06
@@ -93,6 +97,569 @@
     igate = jax.nn.sigmoid(igate_pre)
     log_decay = -cfactor * jax.nn.softplus(-decay_in) * rgate
     return (jnp.exp(log_decay), jnp.sqrt(-jnp.expm1(2.0 * log_decay)) * igate * conv_in)
+
+
+MESH = pl.DeviceIdType.MESH
+
+
+class Place:
+    def __init__(self):
+        self.z = lax.axis_index("grp")
+        seq = lax.axis_index("seq")
+        self.core = seq % 2
+        self.x = (seq // 2) % 2
+        self.y = seq // 4
+        self.seq = seq
+        self.sib = (self.z, self.at(self.y, self.x, 1 - self.core))
+        self.xnb = (self.z, self.at(self.y, 1 - self.x, self.core))
+        self.ynb = (self.z, self.at(1 - self.y, self.x, self.core))
+
+    def at(self, y, x, core):
+        return (y * 2 + x) * 2 + core
+
+    def level(self, z):
+        return (z, self.seq)
+
+
+def meet(peers):
+    barrier = pltpu.get_barrier_semaphore()
+    for peer in peers:
+        pl.semaphore_signal(barrier, inc=1, device_id=peer, device_id_type=MESH)
+    pl.semaphore_wait(barrier, len(peers))
+
+
+def when(cond, body):
+    if cond is None:
+        body()
+    else:
+        pl.when(cond)(body)
+
+
+GOT = ("X", "Y", "D1", "D2", "SO", "SX", "SY", "S1", "S2")
+SENT = ("ox", "oy", "os", "fy", "fx", "zX", "zY", "zD1", "zD2", "SX", "SY", "S1", "S2")
+
+
+class Gather:
+    def __init__(self, place, shards, fulls, kinds, send, recv, own):
+        self.p, self.shards, self.fulls = place, shards, fulls
+        self.send, self.recv, self.own = send, recv, own
+        even = place.z % 2 == 0
+        odd = place.z % 2 == 1
+        self.fetch = [(None, even, odd)[kind] for kind in kinds]
+        self.shared = [kind > 0 for kind in kinds]
+        self.znb = place.level(place.z + 1 - 2 * (place.z % 2))
+
+    def part(self, i, name):
+        p = self.p
+        n = self.shards[i].shape[0]
+        spot = {
+            "O": (p.y, p.x, p.core), "X": (p.y, 1 - p.x, p.core), "Y": (1 - p.y, p.x, p.core),
+            "D1": (1 - p.y, 1 - p.x, p.core), "D2": (1 - p.y, 1 - p.x, p.core),
+            "SO": (p.y, p.x, 1 - p.core), "SX": (p.y, 1 - p.x, 1 - p.core), "SY": (1 - p.y, p.x, 1 - p.core),
+            "S1": (1 - p.y, 1 - p.x, 1 - p.core), "S2": (1 - p.y, 1 - p.x, 1 - p.core),
+        }[name]
+        first = pl.multiple_of(p.at(*spot) * n, n)
+        if name in ("D1", "S1"):
+            return pl.ds(first, n // 2)
+        if name in ("D2", "S2"):
+            return pl.ds(pl.multiple_of(first + n // 2, n // 2), n // 2)
+        return pl.ds(first, n)
+
+    def half(self, i, name, which):
+        n = self.shards[i].shape[0]
+        first = self.part(i, name).start
+        return pl.ds(pl.multiple_of(first + which * (n // 2), n // 2), n // 2)
+
+    def copy(self, i, how, got, peer, rows, src=None):
+        full = self.fulls[i]
+        return pltpu.make_async_remote_copy(
+            src_ref=full.at[rows] if src is None else src,
+            dst_ref=full.at[rows],
+            send_sem=self.send.at[i, SENT.index(how)],
+            recv_sem=self.recv.at[i, GOT.index(got)],
+            device_id=peer,
+            device_id_type=MESH,
+        )
+
+    def wait(self, i, name):
+        self.copy(i, "ox", name, self.p.sib, self.part(i, name)).wait_recv()
+
+    def own_far(self, i):
+        p, mine = self.p, self.part(i, "O")
+        return [self.copy(i, "ox", "X", p.xnb, mine, self.shards[i]), self.copy(i, "oy", "Y", p.ynb, mine, self.shards[i])]
+
+    def own_near(self, i):
+        return self.copy(i, "os", "SO", self.p.sib, self.part(i, "O"), self.shards[i])
+
+    def own_kept(self, i):
+        return pltpu.make_async_copy(self.shards[i], self.fulls[i].at[self.part(i, "O")], self.own.at[i])
+
+    def start(self, i):
+        def far():
+            for c in self.own_far(i):
+                c.start()
+
+        when(self.fetch[i], far)
+        self.own_near(i).start()
+        self.own_kept(i).start()
+
+    def onward_far(self, i, name):
+        p = self.p
+        far = []
+        if name == "X":
+            far.append(self.copy(i, "fy", "D1", p.ynb, self.half(i, "X", 0)))
+        if name == "Y":
+            far.append(self.copy(i, "fx", "D2", p.xnb, self.half(i, "Y", 1)))
+        if self.shared[i]:
+            far.append(self.copy(i, "z" + name, name, self.znb, self.part(i, name)))
+        return far
+
+    def onward_near(self, i, name):
+        to_sib = {"X": "SX", "Y": "SY", "D1": "S1", "D2": "S2"}[name]
+        return self.copy(i, to_sib, to_sib, self.p.sib, self.part(i, name))
+
+    def relay(self, i, names):
+        for name in names:
+            self.wait(i, name)
+
+            def far(name=name):
+                for c in self.onward_far(i, name):
+                    c.start()
+
+            if name in ("X", "Y") or self.shared[i]:
+                when(self.fetch[i], far)
+            self.onward_near(i, name).start()
+
+    def arrive(self, i):
+        for name in ("SO", "SX", "SY", "S1", "S2"):
+            self.wait(i, name)
+        self.own_kept(i).wait()
+
+    def drain(self, i):
+        self.own_near(i).wait_send()
+        for name in ("X", "Y", "D1", "D2"):
+            self.onward_near(i, name).wait_send()
+
+        def far():
+            for c in self.own_far(i):
+                c.wait_send()
+            for name in ("X", "Y", "D1", "D2"):
+                for c in self.onward_far(i, name):
+                    c.wait_send()
+
+        when(self.fetch[i], far)
+
+    def peers(self):
+        return [self.p.sib, self.p.xnb, self.p.ynb, self.znb]
+
+
+def rows_loop(total, body, step=16):
+    @pl.loop(0, total // step)
+    def _(k):
+        body(pl.ds(pl.multiple_of(k * step, step), step))
+
+
+def wide(value):
+    return value.astype(jnp.float32)
+
+
+class Reduce:
+    def __init__(self, place, slots, sems):
+        self.p = place
+        self.slots = slots
+        self.send, self.recv = sems
+        z = place.z
+        self.inner = (z == 1) | (z == 2)
+        self.outer = (z == 0) | (z == 3)
+        self.mine = jnp.where(z == 2, 1, 0)
+        self.peer = place.level(jnp.where(self.inner, 3 - z, z))
+        self.out = place.level(jnp.where(z < 2, 1 - z, 5 - z))
+
+    def copy(self, i, tag, src, dst, peer, got=None):
+        return pltpu.make_async_remote_copy(
+            src_ref=src,
+            dst_ref=dst,
+            send_sem=self.send.at[i, tag],
+            recv_sem=self.recv.at[i, tag if got is None else got],
+            device_id=peer,
+            device_id_type=MESH,
+        )
+
+    def to_sib(self, i, j, src, dst):
+        return self.copy(i, j, src, dst, self.p.sib)
+
+    def first(self, i):
+        p, s = self.p, self.slots[i]
+        return [
+            self.copy(i, 4, s["a"].at[1 - p.x], s["xr"].at[0], p.xnb),
+            self.copy(i, 5, s["a"].at[2 + 1 - p.x], s["xr"].at[1], p.xnb),
+            self.copy(i, 6, s["b"].at[2 * (1 - p.y)], s["yr"].at[0], p.ynb),
+            self.copy(i, 7, s["b"].at[2 * (1 - p.y) + 1], s["yr"].at[1], p.ynb),
+        ]
+
+    def second(self, i):
+        p, s = self.p, self.slots[i]
+        return [
+            self.copy(i, 8, s["a"].at[2 * (1 - p.y) + p.x], s["yr2"], p.ynb),
+            self.copy(i, 9, s["b"].at[2 * p.y + 1 - p.x], s["xr2"], p.xnb),
+        ]
+
+    def add_first(self, i):
+        p, s = self.p, self.slots[i]
+        n = s["n"]
+        for k, cp in enumerate(self.first(i)):
+            cp.wait_recv()
+        for q in range(2):
+            ja, jb = 2 * q + p.x, 2 * p.y + q
+
+            def body(rows, q=q, ja=ja, jb=jb):
+                s["a"][ja, rows, :] = (wide(s["a"][ja, rows, :]) + wide(s["xr"][q, rows, :])).astype(jnp.bfloat16)
+                s["b"][jb, rows, :] = (wide(s["b"][jb, rows, :]) + wide(s["yr"][q, rows, :])).astype(jnp.bfloat16)
+
+            rows_loop(n, body)
+        for cp in self.second(i):
+            cp.start()
+
+    def up(self, i):
+        s = self.slots[i]
+        return [self.copy(i, 10 + k, s["u"].at[k], s["zo"].at[k], self.out) for k in range(2)]
+
+    def across(self, i):
+        s = self.slots[i]
+        return self.copy(i, 12, s["u"].at[1 - self.mine], s["zp"], self.peer)
+
+    def total_out(self, i):
+        s = self.slots[i]
+        res = s["res"].at[self.mine]
+        return [self.copy(i, 13, res, res, self.out), self.copy(i, 14, res, res, self.peer)]
+
+    def total_on(self, i):
+        s = self.slots[i]
+        res = s["res"].at[1 - self.mine]
+        return self.copy(i, 15, res, res, self.out)
+
+    def add_second(self, i):
+        p, s = self.p, self.slots[i]
+        me = 2 * p.y + p.x
+        for cp in self.second(i):
+            cp.wait_recv()
+
+        def body(rows):
+            s["u"][0, rows, :] = (wide(s["a"][me, rows, :]) + wide(s["yr2"][rows, :])).astype(jnp.bfloat16)
+            s["u"][1, rows, :] = (wide(s["b"][me, rows, :]) + wide(s["xr2"][rows, :])).astype(jnp.bfloat16)
+
+        rows_loop(s["n"], body)
+
+        @pl.when(self.outer)
+        def _():
+            for cp in self.up(i):
+                cp.start()
+
+    def add_outer(self, i):
+        s = self.slots[i]
+
+        @pl.when(self.inner)
+        def _():
+            for cp in self.up(i):
+                cp.wait_recv()
+
+            def body(rows):
+                for k in range(2):
+                    s["u"][k, rows, :] = (wide(s["u"][k, rows, :]) + wide(s["zo"][k, rows, :])).astype(jnp.bfloat16)
+
+            rows_loop(s["n"], body)
+            self.across(i).start()
+
+    def add_peer(self, i):
+        s = self.slots[i]
+
+        @pl.when(self.inner)
+        def _():
+            self.across(i).wait_recv()
+            mine = self.mine
+
+            def body(rows):
+                s["res"][mine, rows, :] = (wide(s["u"][mine, rows, :]) + wide(s["zp"][rows, :])).astype(jnp.bfloat16)
+
+            rows_loop(s["n"], body)
+            for cp in self.total_out(i):
+                cp.start()
+
+    def pass_on(self, i):
+        @pl.when(self.inner)
+        def _():
+            s = self.slots[i]
+            other = s["res"].at[1 - self.mine]
+            self.copy(i, 14, other, other, self.peer).wait_recv()
+            self.total_on(i).start()
+
+    def finish(self, i):
+        s = self.slots[i]
+
+        @pl.when(self.outer)
+        def _():
+            near = jnp.where(self.p.z == 3, 1, 0)
+            self.copy(i, 13, s["res"].at[near], s["res"].at[near], self.out).wait_recv()
+            self.copy(i, 15, s["res"].at[1 - near], s["res"].at[1 - near], self.out).wait_recv()
+            for cp in self.up(i):
+                cp.wait_send()
+
+        @pl.when(self.inner)
+        def _():
+            for cp in [self.across(i), self.total_on(i)] + self.total_out(i):
+                cp.wait_send()
+
+        for cp in self.first(i) + self.second(i):
+            cp.wait_send()
+
+    def peers(self):
+        p = self.p
+        return [p.sib, p.xnb, p.ynb] + [p.level((p.z + d) % 4) for d in (1, 2, 3)]
+
+
+class Small:
+    def __init__(self, place, total, slots, sems):
+        p = place
+        self.total, self.slots = total, slots
+        self.send, self.recv = sems
+        z = p.z
+        self.order = [p.sib, p.xnb, p.ynb, p.level(z + 1 - 2 * (z % 2)), p.level((z + 2) % 4)]
+
+    def copy(self, k):
+        return pltpu.make_async_remote_copy(
+            src_ref=self.slots.at[0, k],
+            dst_ref=self.slots.at[1, k],
+            send_sem=self.send.at[k],
+            recv_sem=self.recv.at[k],
+            device_id=self.order[k],
+            device_id_type=MESH,
+        )
+
+    def begin(self):
+        self.slots[0, 0] = self.total[...]
+        self.copy(0).start()
+
+    def step(self, k):
+        self.copy(k).wait_recv()
+        both = self.slots[0, k] + self.slots[1, k]
+        if k < 4:
+            self.slots[0, k + 1] = both
+            self.copy(k + 1).start()
+        else:
+            self.total[...] = both
+
+    def drain(self):
+        for k in range(5):
+            self.copy(k).wait_send()
+
+
+def gather_call(shards):
+    kinds = (0, 2, 1, 0, 0, 1, 2, 0)
+    count = len(shards)
+
+    def kernel(*refs):
+        ins, outs = refs[:count], refs[count : 2 * count]
+        send, recv, own = refs[2 * count :]
+        place = Place()
+        gather = Gather(place, ins, outs, kinds, send, recv, own)
+        meet(gather.peers())
+        for i in range(3):
+            gather.start(i)
+        for i in range(count):
+            gather.relay(i, ("X", "Y"))
+            if i + 3 < count:
+                gather.start(i + 3)
+            if i >= 1:
+                gather.relay(i - 1, ("D1", "D2"))
+        gather.relay(count - 1, ("D1", "D2"))
+        for i in range(count):
+            gather.arrive(i)
+            gather.drain(i)
+
+    return pl.pallas_call(
+        kernel,
+        out_shape=[jax.ShapeDtypeStruct((8 * s.shape[0], s.shape[1]), s.dtype) for s in shards],
+        in_specs=[pl.BlockSpec(memory_space=pl.ANY)] * count,
+        out_specs=[pl.BlockSpec(memory_space=pl.ANY)] * count,
+        scratch_shapes=[
+            pltpu.SemaphoreType.DMA((count, len(SENT))),
+            pltpu.SemaphoreType.DMA((count, len(GOT))),
+            pltpu.SemaphoreType.DMA((count,)),
+        ],
+        compiler_params=pltpu.CompilerParams(collective_id=1, has_side_effects=True),
+        name="gather_weights",
+    )(*shards)
+
+
+def slot_shapes(rows, columns):
+    n, h = rows // 8, columns // 2
+    bf = jnp.bfloat16
+    return [
+        ("a", pltpu.VMEM((4, n, h), bf)), ("b", pltpu.VMEM((4, n, h), bf)),
+        ("xr", pltpu.VMEM((2, n, h), bf)), ("yr", pltpu.VMEM((2, n, h), bf)),
+        ("yr2", pltpu.VMEM((n, h), bf)), ("xr2", pltpu.VMEM((n, h), bf)),
+        ("u", pltpu.VMEM((2, n, h), bf)), ("zo", pltpu.VMEM((2, n, h), bf)),
+        ("zp", pltpu.VMEM((n, h), bf)), ("res", pltpu.VMEM((2, n, h), bf)),
+    ]
+
+
+def reduce_call(partials, small):
+    count = len(partials)
+    shapes = [part.shape for part in partials]
+    names = [name for name, _ in slot_shapes(*shapes[0])]
+
+    def kernel(*refs):
+        refs = list(refs)
+        parts = refs[:count]
+        small_in = refs[count]
+        outs = refs[count + 1 : 2 * count + 1]
+        small_out = refs[2 * count + 1]
+        landed = refs[2 * count + 2 : 3 * count + 2]
+        rest = refs[3 * count + 2 :]
+        slots = []
+        for i in range(count):
+            s = dict(zip(names, rest[i * len(names) : (i + 1) * len(names)]))
+            s["n"], s["h"] = shapes[i][0] // 8, shapes[i][1] // 2
+            slots.append(s)
+        send, recv, small_slots, small_send, small_recv, done = rest[count * len(names) :]
+        place = Place()
+        red = Reduce(place, slots, (send, recv))
+        tot = Small(place, small_out, small_slots, (small_send, small_recv))
+        meet(red.peers())
+        small_out[...] = small_in[...]
+        tot.begin()
+
+        def block(i, j, core):
+            n = slots[i]["n"]
+            return pl.ds(pl.multiple_of((2 * j + core) * n, n), n)
+
+        def sib(i, j):
+            return red.to_sib(i, j, parts[i].at[block(i, j, 1 - place.core)], landed[i].at[j])
+
+        for i in range(count):
+            for j in range(4):
+                sib(i, j).start()
+
+        def fold(i):
+            s = slots[i]
+            n, h = s["n"], s["h"]
+            for j in range(4):
+                sib(i, j).wait_recv()
+
+            def body(own, came):
+                j = pl.program_id(0)
+
+                def add(rows):
+                    both = wide(own[rows, :]) + wide(came[rows, :])
+                    s["a"][j, rows, :] = both[:, :h].astype(jnp.bfloat16)
+                    s["b"][j, rows, :] = both[:, h:].astype(jnp.bfloat16)
+
+                rows_loop(n, add)
+
+            pltpu.emit_pipeline(
+                body,
+                grid=(4,),
+                in_specs=[
+                    pl.BlockSpec((n, 2 * h), lambda j: (2 * j + place.core, 0)),
+                    pl.BlockSpec((None, n, 2 * h), lambda j: (j, 0, 0)),
+                ],
+            )(parts[i], landed[i])
+            for cp in red.first(i):
+                cp.start()
+
+        def keep(i):
+            red.finish(i)
+            s = slots[i]
+            return [
+                pltpu.make_async_copy(s["res"].at[k], outs[i].at[:, pl.ds(k * s["h"], s["h"])], done.at[i, k]) for k in range(2)
+            ]
+
+        stages = [fold, red.add_first, red.add_second, red.add_outer, red.add_peer, red.pass_on]
+        for t in range(count + len(stages) - 1):
+            for k, stage in enumerate(stages):
+                if 0 <= t - k < count:
+                    stage(t - k)
+            if t < 5:
+                tot.step(t)
+        copies = []
+        for i in range(count):
+            more = keep(i)
+            for cp in more:
+                cp.start()
+            copies += more
+            for j in range(4):
+                sib(i, j).wait_send()
+        for cp in copies:
+            cp.wait()
+        tot.drain()
+
+    hbm = pl.BlockSpec(memory_space=pl.ANY)
+    vmem = pl.BlockSpec(memory_space=pltpu.VMEM)
+    bf = jnp.bfloat16
+    result = pl.pallas_call(
+        kernel,
+        out_shape=[jax.ShapeDtypeStruct((r // 8, c), bf) for r, c in shapes]
+        + [jax.ShapeDtypeStruct(small.shape, jnp.float32)]
+        + [jax.ShapeDtypeStruct((4, r // 8, c), bf) for r, c in shapes],
+        in_specs=[hbm] * count + [vmem],
+        out_specs=[hbm] * count + [vmem] + [hbm] * count,
+        scratch_shapes=[shape for r, c in shapes for _, shape in slot_shapes(r, c)]
+        + [
+            pltpu.SemaphoreType.DMA((count, 16)),
+            pltpu.SemaphoreType.DMA((count, 16)),
+            pltpu.VMEM((2, 5) + small.shape, jnp.float32),
+            pltpu.SemaphoreType.DMA((5,)),
+            pltpu.SemaphoreType.DMA((5,)),
+            pltpu.SemaphoreType.DMA((count, 2)),
+        ],
+        compiler_params=pltpu.CompilerParams(collective_id=2, has_side_effects=True, vmem_limit_bytes=60 << 20),
+        name="reduce_gradients",
+    )(*partials, small)
+    return result[:count], result[count]
+
+
+def scan_call(decay, value, backward):
+    rows, width = decay.shape
+    lanes = 128
+    segments, span, tiles = 8, rows // 8, width // lanes
+
+    def kernel(decay_ref, value_ref, prod_ref, sum_ref):
+        def step(k, carry):
+            prod, total = carry
+            t = span - 1 - k if backward else k
+            spot = pl.ds(t, segments, stride=span)
+            new_prod, new_total = [], []
+            for c in range(tiles):
+                d = decay_ref[c, spot, :]
+                new_prod.append(prod[c] * d)
+                new_total.append(total[c] * d + value_ref[c, spot, :])
+                prod_ref[c, spot, :] = new_prod[c]
+                sum_ref[c, spot, :] = new_total[c]
+            return new_prod, new_total
+
+        ones = [jnp.ones((segments, lanes), jnp.float32)] * tiles
+        zeros = [jnp.zeros((segments, lanes), jnp.float32)] * tiles
+        lax.fori_loop(0, span, step, (ones, zeros), unroll=2)
+        order = list(range(segments))[::-1] if backward else list(range(segments))
+        edge = order[0] * span + (0 if backward else span - 1)
+        for seg in order[1:]:
+            base = seg * span
+            for c in range(tiles):
+                prod, total = prod_ref[c, edge : edge + 1, :], sum_ref[c, edge : edge + 1, :]
+                here = prod_ref[c, base : base + span, :]
+                sum_ref[c, base : base + span, :] = sum_ref[c, base : base + span, :] + here * total
+                prod_ref[c, base : base + span, :] = here * prod
+            edge = base + (0 if backward else span - 1)
+
+    shape = jax.ShapeDtypeStruct((tiles, rows, lanes), jnp.float32)
+    fold = lambda v: v.reshape(rows, tiles, lanes).transpose(1, 0, 2)
+    out = pl.pallas_call(
+        kernel,
+        out_shape=[shape, shape],
+        compiler_params=pltpu.CompilerParams(vmem_limit_bytes=48 << 20),
+        name="scan_rows",
+    )(fold(decay), fold(value))
+    return [v.transpose(1, 0, 2).reshape(rows, width) for v in out]
 
 
 def local(
@@ -355,6 +922,194 @@
     )
 
 
+def local_fast(
+    tokens,
+    lengths,
+    mixer_gain,
+    gelu_weight,
+    input_weight,
+    conv_taps,
+    conv_bias,
+    rgate_weight,
+    rgate_bias,
+    igate_weight,
+    igate_bias,
+    decay_param,
+    output_weight,
+    mlp_gain,
+    mlp_gate,
+    mlp_value,
+    mlp_down,
+    cotangent,
+):
+    count = tokens.shape[0]
+    width_lru = input_weight.shape[1]
+    block = rgate_weight.shape[1]
+    heads = width_lru // block
+    taps_count = conv_taps.shape[1]
+    rim = taps_count - 1
+    seq_count = lax.axis_size("seq")
+    slot_length = count * seq_count
+    first_row = (lax.axis_index("grp") * seq_count + lax.axis_index("seq")) * count
+    global_row = first_row + jnp.arange(count, dtype=jnp.int32)
+    position = global_row % slot_length
+    slot_of = global_row // slot_length
+    slot_ids = jnp.arange(lengths.shape[0], dtype=jnp.int32)
+    slot_len = jnp.sum(
+        jnp.where(slot_of[:, None] == slot_ids[None, :], lengths[None, :], 0), axis=1
+    )
+    valid = (position < slot_len).astype(jnp.float32)[:, None]
+    starts = (position > 0).astype(jnp.float32)[:, None]
+    lag_masks = [(position >= lag).astype(jnp.float32)[:, None] for lag in range(taps_count)]
+    zeros_lru = jnp.zeros((width_lru,), jnp.float32)
+    ones_lru = jnp.ones((width_lru,), jnp.float32)
+    lru_rows = jnp.concatenate(
+        [conv_taps.T, conv_bias[None], rgate_bias[None], igate_bias[None], decay_param[None]], axis=0
+    ).astype(jnp.float32)
+    model_rows = jnp.stack([mixer_gain, mlp_gain]).astype(jnp.float32)
+    mine = lax.axis_index("seq")
+    small = jnp.zeros((16, width_lru), jnp.float32)
+    small = lax.dynamic_update_slice(small, lru_rows, (0, mine * lru_rows.shape[1]))
+    small = lax.dynamic_update_slice(small, model_rows, (8, mine * model_rows.shape[1]))
+    gathered = gather_call(
+        [small, gelu_weight, input_weight, jnp.concatenate([rgate_weight, igate_weight], axis=1), output_weight, mlp_gate, mlp_value, mlp_down]
+    )
+    small_full = gathered[0].reshape(seq_count, 16, width_lru).sum(axis=0)
+    gelu_full, input_full, gates_full, output_full, mgate_full, mvalue_full, mdown_full = gathered[1:]
+    rgate_full, igate_full = gates_full[:, :block], gates_full[:, block:]
+    taps_full = small_full[:4].T
+    cbias_full, rbias_full, ibias_full, decay_full = small_full[4], small_full[5], small_full[6], small_full[7]
+    gain_one, gain_two = small_full[8, : tokens.shape[1]], small_full[9, : tokens.shape[1]]
+    inputs = tokens.astype(jnp.float32)
+    normed_one, norm_one_back = jax.vjp(rms_norm, inputs, gain_one.astype(jnp.float32))
+    normed_one = normed_one.astype(jnp.bfloat16)
+    gate_pre = matmul(normed_one, gelu_full)
+    gate_act, gate_back = jax.vjp(gelu_tanh, gate_pre)
+    linear = matmul(normed_one, input_full)
+    rim_in = passed_along(linear[count - rim :], "seq", 1)
+    extended = jnp.concatenate([rim_in, linear], axis=0)
+    taps_fwd = taps_full.astype(jnp.float32)
+    conv = cbias_full.astype(jnp.float32) + taps_fwd[:, 0] * linear
+    for lag in range(1, taps_count):
+        conv = conv + taps_fwd[:, lag] * (extended[rim - lag : rim - lag + count] * lag_masks[lag])
+    conv_low = conv.astype(jnp.bfloat16)
+    conv_value = conv_low.astype(jnp.float32)
+    rgate_pre = block_apply(conv_low, rgate_full, heads) + rbias_full.astype(jnp.float32)
+    igate_pre = block_apply(conv_low, igate_full, heads) + ibias_full.astype(jnp.float32)
+    (decay, inject), gates_back = jax.vjp(
+        recurrence_gates, rgate_pre, igate_pre, conv_value, decay_full.astype(jnp.float32)
+    )
+    decay_used = decay * starts
+    cum_decay, state_zero = scan_call(decay_used, inject, False)
+    scanned = carried_in(
+        (cum_decay[-1], state_zero[-1]), "seq", chain_combine, (ones_lru, zeros_lru), False
+    )
+    carry_in = scanned[1]
+    state = state_zero + cum_decay * carry_in
+    mixed_rec = (state * gate_act).astype(jnp.bfloat16)
+    resid = inputs + matmul(mixed_rec, output_full)
+    normed_two, norm_two_back = jax.vjp(rms_norm, resid, gain_two.astype(jnp.float32))
+    normed_two = normed_two.astype(jnp.bfloat16)
+    mgate_pre = matmul(normed_two, mgate_full)
+    mvalue_pre = matmul(normed_two, mvalue_full)
+    mgate_act, mgate_back = jax.vjp(gelu_tanh, mgate_pre)
+    hidden = (mgate_act * mvalue_pre).astype(jnp.bfloat16)
+    mixed = ((resid + matmul(hidden, mdown_full)) * valid).astype(jnp.bfloat16)
+    taps_back = taps_full.astype(jnp.float32)
+    grad_out = cotangent.astype(jnp.float32) * valid
+    grad_out_low = grad_out.astype(jnp.bfloat16)
+    down_grad = inner_rows(hidden, grad_out_low)
+    grad_hidden = outer_cols(grad_out_low, mdown_full)
+    grad_mgate = mgate_back(grad_hidden * mvalue_pre)[0].astype(jnp.bfloat16)
+    grad_mvalue = (grad_hidden * mgate_act).astype(jnp.bfloat16)
+    mgate_grad = inner_rows(normed_two, grad_mgate)
+    mvalue_grad = inner_rows(normed_two, grad_mvalue)
+    grad_ntwo = outer_cols(grad_mgate, mgate_full) + outer_cols(grad_mvalue, mvalue_full)
+    grad_resid_norm, gain_two_grad = norm_two_back(grad_ntwo)
+    grad_resid = grad_out + grad_resid_norm
+    grad_mix = grad_resid.astype(jnp.bfloat16)
+    output_grad = inner_rows(mixed_rec, grad_mix)
+    grad_rec = outer_cols(grad_mix, output_full)
+    grad_state = grad_rec * gate_act
+    grad_gate = gate_back(grad_rec * state)[0].astype(jnp.bfloat16)
+    decay_next = jnp.concatenate([decay_used[1:], jnp.ones((1, width_lru), jnp.float32)], axis=0)
+    tail_prod, adjoint_zero = scan_call(decay_next, grad_state, True)
+    summary_decay = decay_used[0] * tail_prod[0]
+    summary_adjoint = decay_used[0] * adjoint_zero[0]
+    scanned_back = carried_in(
+        (summary_decay, summary_adjoint), "seq", chain_combine, (ones_lru, zeros_lru), True
+    )
+    incoming = scanned_back[1]
+    adjoint = adjoint_zero + tail_prod * incoming
+    state_prev = jnp.concatenate([carry_in[None, :], state[:-1]], axis=0)
+    grad_decay = adjoint * state_prev * starts
+    grad_rpre, grad_ipre, grad_direct, decay_grad = gates_back((grad_decay, adjoint))
+    rbias_grad = jnp.sum(grad_rpre, axis=0)
+    ibias_grad = jnp.sum(grad_ipre, axis=0)
+    grad_rlow = grad_rpre.astype(jnp.bfloat16)
+    grad_ilow = grad_ipre.astype(jnp.bfloat16)
+    rgate_grad = block_grad(conv_low, grad_rlow, heads)
+    igate_grad = block_grad(conv_low, grad_ilow, heads)
+    grad_conv = (
+        grad_direct
+        + block_back(grad_rlow, rgate_full, heads)
+        + block_back(grad_ilow, igate_full, heads)
+    )
+    cbias_grad = jnp.sum(grad_conv, axis=0)
+    taps_columns = []
+    grad_extended = jnp.zeros((count + rim, width_lru), jnp.float32)
+    for lag in range(taps_count):
+        masked_term = grad_conv * lag_masks[lag]
+        taps_columns.append(jnp.sum(masked_term * extended[rim - lag : rim - lag + count], axis=0))
+        grad_extended = grad_extended + jnp.pad(
+            taps_back[:, lag] * masked_term, ((rim - lag, lag), (0, 0))
+        )
+    taps_grad = jnp.stack(taps_columns, axis=1)
+    rim_back = passed_along(grad_extended[:rim], "seq", -1)
+    grad_linear = grad_extended[rim:] + jnp.pad(rim_back, ((count - rim, 0), (0, 0)))
+    grad_lin = grad_linear.astype(jnp.bfloat16)
+    input_grad = inner_rows(normed_one, grad_lin)
+    gelu_grad = inner_rows(normed_one, grad_gate)
+    grad_none = outer_cols(grad_lin, input_full) + outer_cols(grad_gate, gelu_full)
+    grad_inputs_norm, gain_one_grad = norm_one_back(grad_none)
+    tokens_grad = grad_resid + grad_inputs_norm
+    low = lambda value: value.astype(jnp.bfloat16)
+    lru_out = jnp.concatenate([taps_grad.T, cbias_grad[None], rbias_grad[None], ibias_grad[None], decay_grad[None]], axis=0)
+    model_out = jnp.stack([gain_one_grad, gain_two_grad])
+    small_part = jnp.concatenate(
+        [lru_out, jnp.pad(model_out, ((0, 6), (0, width_lru - model_out.shape[1])))], axis=0
+    )
+    big, small_sum = reduce_call(
+        [
+            low(down_grad), low(mgate_grad), low(mvalue_grad), low(output_grad),
+            jnp.concatenate([low(rgate_grad), low(igate_grad)], axis=1), low(input_grad), low(gelu_grad),
+        ],
+        small_part,
+    )
+    down, mgate, mvalue, out_w, gates, input_w, gelu_w = [value.astype(jnp.float32) for value in big]
+    lru_own = lax.dynamic_slice(small_sum, (0, mine * conv_bias.shape[0]), (8, conv_bias.shape[0]))
+    model_own = lax.dynamic_slice(small_sum, (8, mine * mixer_gain.shape[0]), (2, mixer_gain.shape[0]))
+    return (
+        mixed,
+        tokens_grad,
+        model_own[0],
+        gelu_w,
+        input_w,
+        lru_own[:4].T,
+        lru_own[4],
+        gates[:, :block],
+        lru_own[5],
+        gates[:, block:],
+        lru_own[6],
+        lru_own[7],
+        out_w,
+        model_own[1],
+        mgate,
+        mvalue,
+        down,
+    )
+
+
 def solution(mesh):
     placed = (
         P(("grp", "seq"), None),
@@ -376,8 +1131,9 @@
         P("seq", None),
         P(("grp", "seq"), None),
     )
+    fits = mesh.shape["grp"] == 4 and mesh.shape["seq"] == 8
     return jax.shard_map(
-        local,
+        local_fast if fits else local,
         mesh=mesh,
         in_specs=placed,
         out_specs=(

time: 1880 us -> 766 us (0.41); the launches traced: 1850 us -> 760 us
  waiting for transfers between devices: 715 us -> 0.01 us
  local copies, waits for them, and re-layouts: 624 us -> 124 us
  Pallas kernels: 0 us -> 389 us
  other arithmetic: 196 us -> 81.8 us
  blocking collectives: 146 us -> 40.5 us
  matrix products: 150 us -> 119 us
    reduce_scatter x8 -> x0, waiting for transfers between devices: 470 us -> none  [the longest x1 96.3 us: local(): lax.psum_scatter(partials[13], 'seq', scatter_dimension=0, tiled=True)]
    pallas_call x0 -> x4, Pallas kernels: none -> 389 us  [the longest x1 199 us: reduce_call(): pl.pallas_call(kernel, out_shape=[jax.ShapeDtypeStruct((r // 8, c), bf) f...]
    slice x128 -> x7, local copies, waits for them, and re-layouts: 357 us -> 5.7 us  [the longest x1 2.03 us: local_fast(): decay_used[1:]]
    psum x1 -> x0, waiting for transfers between devices: 241 us -> none  [local(): totals = lax.psum(tuple(summed_seq), 'grp')]
    pad x64 -> x0, local copies, waits for them, and re-layouts: 173 us -> none  [the longest x32 87.1 us: local(): lax.associative_scan(chain_combine, (decay_used, inject), axis=0)]
    add x52 -> x3, other arithmetic: 80 us -> 4.09 us  [the longest x1 1.89 us: local_fast(): tokens_grad = grad_resid + grad_inputs_norm]
    all_gather x5 -> x0, blocking collectives: 49.7 us -> none  [the longest x1 11.6 us: local(): lax.all_gather(igate_weight, 'seq', axis=0, tiled=True)]
    unnamed x2 -> x0, blocking collectives: 47.4 us -> none
  transfers between devices with their start and end apart: 18 -> 2, of which waited for: 8 -> 0; matrix products, arithmetic and copies ran while one was open for 29% -> 1% of each run, Pallas kernels for 0% -> 0%
where the time goes in v1:
time: 766 us; the launch traced here: 760 us
  Pallas kernels  389 us (51%)
  local copies, waits for them, and re-layouts  124 us (16%)
  matrix products  119 us (16%)
  other arithmetic  81.8 us (11%)
  blocking collectives  40.5 us (5%)
    pallas_call x1, Pallas kernels, reduce_call(): pl.pallas_call(kernel, out_shape=[jax.ShapeDtypeStruct((r // 8, c), bf) f...  199 us
    pallas_call x1, Pallas kernels, gather_call(): pl.pallas_call(kernel, out_shape=[jax.ShapeDtypeStruct((8 * s.shape[0], s...  161 us
    all_gather x4, blocking collectives, carried_in(): pieces = jax.tree.map(lambda part: lax.all_gather(part, axis), value)  40.5 us
    dot_general x6, matrix products, outer_cols(): lax.dot_general(left, right, (((1,), (1,)), ((), ())), preferred_element_...  40.4 us
    dot_general x6, matrix products, inner_rows(): lax.dot_general(left, right, (((0,), (0,)), ((), ())), preferred_element_...  29.6 us
    pallas_call x2, Pallas kernels, scan_call(): pl.pallas_call(kernel, out_shape=[shape, shape], compiler_params=pltpu.Co...  29.3 us
    dot_general x6, matrix products, matmul(): return jnp.dot(left, right, preferred_element_type=jnp.float32)  26.9 us
    unnamed x202, local copies, waits for them, and re-layouts  16 us
  transfers between devices with their start and end apart: 2, of which 0 were waited for; matrix products, arithmetic and copies ran while one was open for 1% of the time, Pallas kernels for 0%

profile of v1, /device:TPU:0, one launch (start us, length us, event | category | flops | bytes accessed | tf_op | source)
XLA Modules:
  0.0 760.5 jit_solution(17794593193980413279)
XLA Ops:
  7.5 160.7 %gather_weights.1 = (f32[128,1536]{1,0:T(8,128)}, bf16[1024,1536]{1,0:T(8,128)(2,1)}, bf16[1024,1536]{1,0:T(8,128)(2,1)}, bf16[1536,256]{1,0:T(8,128)(2,1)}, bf1...) custom-call(f32[16,1536]{1,0:T(8,128)} %copy-done.42, ...), custom_call_target="tpu_custom_call" | custom-call | tf_op jit(solution)/shard_map/gather_weights/pallas_call | solution.py:479
  170.9 3.9 fusion.59
  183.3 7.6 %add_convert_fusion = bf16[512,1536]{1,0:T(8,128)(2,1)S(1)} fusion(f32[512,1536]{1,0:T(8,128)} %copy-done.11, f32[3,1536]{1,0:T(4,128)S(1)} %collective-permute-done, f32[512]{0:T(512)S(1)} %get-tuple-element.370, f32[1536]{0:T(1024)S(1)} %get-tuple-element.297, f32[512]{0:T(512)S(1)} %get-tuple-element.371, f32[1536]{0:T(1024)S(1)} %get-tuple-element.298, ...), kind=kLoop, calls=%fused_computation.73 | loop fusion | flops 11796480 | bytes 4773888 | tf_op jit(solution)/shard_map/convert_element_type | solution.py:995
  191.7 3.6 convolution_bitcast_fusion.2
  195.3 3.5 copy.140
  198.9 3.6 copy.141
  204.7 3.7 copy.135
  210.8 8.2 %exponential_multiply_fusion = (f32[512,1536]{1,0:T(8,128)}, f32[512,1536]{1,0:T(8,128)}) fusion(f32[512]{0:T(512)} %get-tuple-element.369, f32[1536]{0:T(1024)S(1)} %get-tuple-element.327, f32[512,1536]{1,0:T(8,128)S(1)} %copy.136, f32[1536]{0:T(1024)} %get-tuple-element.357, bf16[512,1536]{1,0:T(8,128)(2,1)} %copy-done.6, f32[512,1536]{1,0:T(8,128)} %copy.141, ...), kind=kLoop, calls=%fused_computation.78 | loop fusion | flops 11796480 | bytes 14176256 | tf_op jit(solution)/shard_map/mul | solution.py:1002
  219.0 3.5 copy.142
  222.5 3.8 copy.143
  226.4 3.6 multiply_bitcast_fusion.decay_ref
  230.0 14.5 %scan_rows.2 = (f32[12,512,128]{2,1,0:T(8,128)S(1)}, f32[12,512,128]{2,1,0:T(8,128)}) custom-call(f32[12,512,128]{2,1,0:T(8,128)} %multiply_bitcast_fusion.decay_ref, f32[12,512,128]{2,1,0:T(8,128)} %bitcast.157), custom_call_target="tpu_custom_call" | custom-call | tf_op jit(solution)/shard_map/scan_rows/pallas_call | solution.py:656
  247.6 3.7 copy.144
  251.3 14.2 %all-gather.1 = f32[8,1,1536]{2,1,0:T(1,128)S(1)} all-gather(f32[1,1,1536]{2,1,0:T(1,128)S(1)} %slice_bitcast_fusion.3), channel_id=1, replica_groups=mesh['grp'=4,'seq'=8] {'seq'}, dimensions={0}, use_global_device_ids=true | all-gather | bytes 55296 | tf_op jit(solution)/shard_map/all_gather | solution.py:22
  265.5 9.0 %all-gather = f32[8,1,1536]{2,1,0:T(1,128)S(1)} all-gather(f32[1,1,1536]{2,1,0:T(1,128)S(1)} %slice_bitcast_fusion.4), channel_id=1, replica_groups=mesh['grp'=4,'seq'=8] {'seq'}, dimensions={0}, use_global_device_ids=true | all-gather | bytes 55296 | tf_op jit(solution)/shard_map/all_gather | solution.py:22
  277.5 3.6 copy.147
  281.0 6.0 multiply_convert_fusion.2
  292.7 5.3 fusion.70
  298.1 5.3 fusion.69
  303.4 15.7 %multiply_convert_fusion = (bf16[512,3072]{1,0:T(8,128)(2,1)S(1)}, bf16[512,3072]{1,0:T(8,128)(2,1)}, bf16[512,3072]{1,0:T(8,128)(2,1)}) fusion(f32[512,3072]{1,0:T(8,128)} %fusion.69, f32[512,3072]{1,0:T(8,128)} %fusion.70, bf16[3072,1024]{1,0:T(8,128)(2,1)} %get-tuple-element.235, bf16[512,1024]{1,0:T(8,128)(2,1)S(1)} %copy-done.29, f32[512]{0:T(512)S(1)} %copy-done.78), kind=kOutput, calls=%fused_computation.15 | convolution fusion | flops 3263692800 | bytes 29362176 | tf_op jit(solution)/shard_map/dot_general | solution.py:56
  319.1 7.6 %fusion.71 = f32[512,1024]{1,0:T(8,128)S(1)} fusion(bf16[512,3072]{1,0:T(8,128)(2,1)} %get-tuple-element.334, bf16[1024,3072]{1,0:T(8,128)(2,1)} %get-tuple-element.233), kind=kOutput, calls=%fused_computation.186 | convolution fusion | flops 3221225472 | bytes 11534336 | tf_op jit(solution)/shard_map/dot_general | solution.py:56
  326.8 6.9 multiply_reduce_fusion.5
  336.3 4.9 fusion.32
  343.6 3.7 copy.151
  353.7 3.5 copy.149
  357.2 14.8 %scan_rows.3 = (f32[12,512,128]{2,1,0:T(8,128)S(1)}, f32[12,512,128]{2,1,0:T(8,128)}) custom-call(f32[12,512,128]{2,1,0:T(8,128)} %bitcast.158, f32[12,512,128]{2,1,0:T(8,128)} %bitcast.156), custom_call_target="tpu_custom_call" | custom-call | tf_op jit(solution)/shard_map/scan_rows/pallas_call | solution.py:656
  375.7 3.6 copy.152
  379.9 8.5 %all-gather.2 = f32[8,1,1536]{2,1,0:T(1,128)S(1)} all-gather(f32[1,1,1536]{2,1,0:T(1,128)} %get-tuple-element.345), channel_id=1, replica_groups=mesh['grp'=4,'seq'=8] {'seq'}, dimensions={0}, use_global_device_ids=true | all-gather | bytes 55296 | tf_op jit(solution)/shard_map/all_gather | solution.py:22
  389.1 5.8 rev.6
  394.9 8.8 %all-gather.3 = f32[8,1,1536]{2,1,0:T(1,128)S(1)} all-gather(f32[1,1,1536]{2,1,0:T(1,128)S(1)} %get-tuple-element.344), channel_id=1, replica_groups=mesh['grp'=4,'seq'=8] {'seq'}, dimensions={0}, use_global_device_ids=true | all-gather | bytes 55296 | tf_op jit(solution)/shard_map/all_gather | solution.py:22
  404.3 6.2 rev.7
  410.5 14.5 %while.29 = (s32[]{:T(128)}, f32[1536]{0:T(1024)}, s32[]{:T(128)}, f32[8,1536]{1,0:T(8,128)}, f32[8,1536]{1,0:T(8,128)}, /*index=5*/s32[]{:T(128)}, s32[]{:T(128)}) while((s32[]{:T(128)}, f32[1536]{0:T(1024)}, s32[]{:T(128)}, f32[8,1536]{1,0:T(8,128)}, f32[8,1536]{1,0:T(8,128)}, /*index=5*/s32[]{:T(128)}, s32[]{:T(128)}) %tuple.117), condition=%wide.region_8.9_spmd.clone, body=%wide.region_7.8_spmd.clone.sunk | while | flops 6148 | bytes 49253 | solution.py:34
  425.0 3.6 copy.154
  428.5 3.5 copy.155
  432.1 8.7 %fusion.61 = (f32[1536]{0:T(1024)}, bf16[512,1536]{1,0:T(8,128)(2,1)}, f32[512,1536]{1,0:T(8,128)S(1)}) fusion(f32[512,1536]{1,0:T(8,128)} %copy.141, f32[1536]{0:T(1024)} %get-tuple-element.358, bf16[512,1536]{1,0:T(8,128)(2,1)} %copy-done.6, f32[512,1536]{1,0:T(8,128)} %copy-done, f32[1536]{0:T(1024)S(1)} %copy-done.37, f32[1536]{0:T(1024)S(1)} %copy-done.36, ...), kind=kLoop, calls=%fused_computation.178 | loop fusion | flops 16513536 | bytes 18905088 | tf_op jit(solution)/shard_map/reduce_sum | solution.py:1048
  440.9 6.6 multiply_reduce_fusion
  452.3 3.7 convolution_bitcast_fusion.1
  458.6 3.6 copy.159
  462.2 11.2 %add_reduce_fusion = (f32[12,128]{1,0:T(8,128)}, f32[512,12,128]{2,0,1:T(8,128)}) fusion(f32[512,12,128]{2,0,1:T(8,128)} %convolution_bitcast_fusion.1, f32[512,12,128]{2,0,1:T(8,128)} %convolution_bitcast_fusion.2, f32[12,128]{1,0:T(8,128)} %bitcast.182, f32[12,128]{1,0:T(8,128)} %bitcast.183, f32[12,128]{1,0:T(8,128)S(1)} %bitcast.181, ...), kind=kOutput, calls=%fused_computation.58 | convolution fusion | flops 215480832 | bytes 20871168 | tf_op jit(solution)/shard_map/rhj,hij->rhi/dot_general | solution.py:76
  478.4 3.7 copy.160
  482.2 12.1 %multiply_reduce_fusion.3 = (f32[1536]{0:T(1024)S(1)}, f32[1536]{0:T(1024)S(1)}, f32[1536]{0:T(1024)S(1)}, f32[1536]{0:T(1024)S(1)}, f32[512,1536]{1,0:T(8,128)S(1)}) fusion(f32[512]{0:T(512)S(1)} %copy-done.67, f32[512,1536]{1,0:T(8,128)} %copy-done.11, f32[3,1536]{1,0:T(4,128)S(1)} %copy-done.47, f32[512]{0:T(512)S(1)} %copy-done.65, ...), kind=kLoop, calls=%fused_computation.61 | loop fusion | flops 23586816 | bytes 22089728 | tf_op jit(solution)/shard_map/reduce_sum | solution.py:1063
  504.3 5.5 convolution_convert_fusion.refs_2_
  509.7 5.8 convolution_convert_fusion.1.refs_1_
  517.5 3.7 convolution_convert_fusion.3.refs_6_
  521.1 5.6 convolution_convert_fusion.2.refs_0_
  526.8 4.4 multiply_convert_fusion.3
  539.6 5.5 convolution_convert_fusion.4.refs_5_
  545.2 199.1 %reduce_gradients.1 = (bf16[384,1024]{1,0:T(8,128)(2,1)}, bf16[128,3072]{1,0:T(8,128)(2,1)}, bf16[128,3072]{1,0:T(8,128)(2,1)}, bf16[192,1024]{1,0:T(8,128)(2,1)...) custom-call(bf16[3072,1024]{1,0:T(8,128)(2,1)} %convolution_convert_, ...), custom_call_target="tpu_custom_call" | custom-call | tf_op jit(solution)/shard_map/reduce_gradients/pallas_call | solution.py:599
  (319 shorter events, 115.1 us)
Async XLA Ops:
  0.7 169.3 %copy-start.15 = (bf16[512,1024]{1,0:T(8,128)(2,1)S(1)}, bf16[512,1024]{1,0:T(8,128)(2,1)}, u32[]{:S(2)}) copy-start(bf16[512,1024]{1,0:T(8,128)(2,1)} %param.22) | copy-start | bytes 3145732
  169.4 9.8 %copy-start.43 = (f32[16,1536]{1,0:T(8,128)}, f32[16,1536]{1,0:T(8,128)S(1)}, u32[]{:S(2)}) copy-start(f32[16,1536]{1,0:T(8,128)S(1)} %reduce_sum.140) | copy-start | bytes 294916
  170.9 10.3 %copy-start.33 = (bf16[1536,256]{1,0:T(8,128)(2,1)S(1)}, bf16[1536,256]{1,0:T(8,128)(2,1)}, u32[]{:S(2)}) copy-start(bf16[1536,256]{1,0:T(8,128)(2,1)} %get-tuple-element.226) | copy-start | bytes 2359300
  170.9 11.1 %copy-start.82 = (s32[4]{0:T(128)S(1)}, s32[4]{0:T(128)}, u32[]{:S(2)}) copy-start(s32[4]{0:T(128)} %param.23) | copy-start | bytes 52
  176.4 6.4 collective-permute-start
  180.4 45.9 %copy-start.35 = (f32[1536]{0:T(1024)}, f32[1536]{0:T(1024)S(1)}, u32[]{:S(2)}) copy-start(f32[1536]{0:T(1024)S(1)} %get-tuple-element.327) | copy-start | bytes 18436
  191.7 10.7 %copy-start.4 = (bf16[512,1536]{0,1:T(8,128)(2,1)}, bf16[512,1536]{0,1:T(8,128)(2,1)S(1)}, u32[]{:S(2)}) copy-start(bf16[512,1536]{0,1:T(8,128)(2,1)S(1)} %copy.130) | copy-start | bytes 4718596
  210.8 8.2 %copy-start = (f32[512,1536]{1,0:T(8,128)}, f32[512,1536]{1,0:T(8,128)S(1)}, u32[]{:S(2)}) copy-start(f32[512,1536]{1,0:T(8,128)S(1)} %copy.136) | copy-start | bytes 9437188
  281.0 6.1 copy-start.16
  281.0 6.1 copy-start.84
  287.1 47.3 %copy-start.13 = (f32[512,1536]{1,0:T(8,128)}, f32[512,1536]{1,0:T(8,128)S(1)}, u32[]{:S(2)}) copy-start(f32[512,1536]{1,0:T(8,128)S(1)} %get-tuple-element.326) | copy-start | bytes 9437188
  287.1 5.6 slice-start.3
  289.0 44.7 %copy-start.18 = (f32[512,1024]{1,0:T(8,128)}, f32[512,1024]{1,0:T(8,128)S(1)}, u32[]{:S(2)}) copy-start(f32[512,1024]{1,0:T(8,128)S(1)} %get-tuple-element.363) | copy-start | bytes 6291460
  289.1 9.0 %slice-start.4 = ((s8[6291456]{0:T(1024)(128)(4,1)}), s8[4194304]{0:T(1024)(128)(4,1)S(1)}, s32[]{:S(2)}) async-start(s8[6291456]{0:T(1024)(128)(4,1)} %bitcast.212), calls=%async_computation.4 | async-start | bytes 8388608
  289.3 8.7 %copy-start.31 = (bf16[512,1024]{1,0:T(8,128)(2,1)}, bf16[512,1024]{1,0:T(8,128)(2,1)S(1)}, u32[]{:S(2)}) copy-start(bf16[512,1024]{1,0:T(8,128)(2,1)S(1)} %multiply_convert_fusion.4) | copy-start | bytes 3145732
  319.1 7.7 %copy-start.87 = (bf16[512,3072]{1,0:T(8,128)(2,1)}, bf16[512,3072]{1,0:T(8,128)(2,1)S(1)}, u32[]{:S(2)}) copy-start(bf16[512,3072]{1,0:T(8,128)(2,1)S(1)} %get-tuple-element.333) | copy-start | bytes 9437188
  334.4 6.8 copy-start.20
  432.0 8.7 %copy-start.1 = (f32[512,1536]{1,0:T(8,128)S(1)}, f32[512,1536]{1,0:T(8,128)}, u32[]{:S(2)}) copy-start(f32[512,1536]{1,0:T(8,128)} %copy-done) | copy-start | bytes 9437188
  432.0 8.7 %copy-start.3 = (f32[512,1536]{1,0:T(8,128)S(1)}, f32[512,1536]{1,0:T(8,128)}, u32[]{:S(2)}) copy-start(f32[512,1536]{1,0:T(8,128)} %copy.141) | copy-start | bytes 9437188
  432.1 8.7 %copy-start.7 = (bf16[512,1536]{1,0:T(8,128)(2,1)S(1)}, bf16[512,1536]{1,0:T(8,128)(2,1)}, u32[]{:S(2)}) copy-start(bf16[512,1536]{1,0:T(8,128)(2,1)} %copy-done.6) | copy-start | bytes 4718596
  432.1 8.9 %copy-start.14 = (f32[512,1536]{1,0:T(8,128)S(1)}, f32[512,1536]{1,0:T(8,128)}, u32[]{:S(2)}) copy-start(f32[512,1536]{1,0:T(8,128)} %copy-done.13) | copy-start | bytes 9437188
  432.1 8.9 %copy-start.44 = (f32[1536]{0:T(1024)S(1)}, f32[1536]{0:T(1024)}, u32[]{:S(2)}) copy-start(f32[1536]{0:T(1024)} %get-tuple-element.358) | copy-start | bytes 18436
  432.1 8.8 %copy-start.68 = (f32[512]{0:T(512)S(1)}, f32[512]{0:T(512)}, u32[]{:S(2)}) copy-start(f32[512]{0:T(512)} %get-tuple-element.369) | copy-start | bytes 6148
  432.1 8.8 %copy-start.70 = (f32[1,1536]{1,0:T(1,128)S(1)}, f32[1,1536]{1,0:T(1,128)}, u32[]{:S(2)}) copy-start(f32[1,1536]{1,0:T(1,128)} %broadcast_in_dim.70) | copy-start | bytes 18436
  440.8 6.8 copy-start.9
  482.1 12.1 %copy-start.49 = (f32[1536]{0:T(1024)S(1)}, f32[1536]{0:T(1024)}, u32[]{:S(2)}) copy-start(f32[1536]{0:T(1024)} %copy-done.48) | copy-start | bytes 18436
  482.1 12.1 %copy-start.51 = (f32[1536]{0:T(1024)S(1)}, f32[1536]{0:T(1024)}, u32[]{:S(2)}) copy-start(f32[1536]{0:T(1024)} %copy-done.50) | copy-start | bytes 18436
  482.1 12.1 %copy-start.53 = (f32[1536]{0:T(1024)S(1)}, f32[1536]{0:T(1024)}, u32[]{:S(2)}) copy-start(f32[1536]{0:T(1024)} %copy-done.52) | copy-start | bytes 18436
  482.2 12.1 %copy-start.55 = (f32[1536]{0:T(1024)S(1)}, f32[1536]{0:T(1024)}, u32[]{:S(2)}) copy-start(f32[1536]{0:T(1024)} %copy-done.54) | copy-start | bytes 18436
  497.5 37.4 %copy-start.23 = (f32[515,1536]{1,0:T(8,128)}, f32[515,1536]{1,0:T(8,128)S(1)}, u32[]{:S(2)}) copy-start(f32[515,1536]{1,0:T(8,128)S(1)} %pad_add_fusion) | copy-start | bytes 9492484
  504.3 5.5 copy-start.89
  509.7 5.8 copy-start.24
  509.7 5.8 copy-start.86
  517.4 9.3 %slice-start = ((s8[6291456]{0:T(1024)(128)(4,1)}), s8[4194304]{0:T(1024)(128)(4,1)S(1)}, s32[]{:S(2)}) async-start(s8[6291456]{0:T(1024)(128)(4,1)} %bitcast.208), calls=%async_computation | async-start | bytes 8388608
  521.1 5.7 copy-start.19
  521.1 5.6 slice-start.1
  526.8 6.1 copy-start.61
  526.8 6.1 copy-start.71
  526.8 7.9 %copy-start.80 = (f32[12,128]{1,0:T(8,128)S(1)}, f32[12,128]{1,0:T(8,128)}, u32[]{:S(2)}) copy-start(f32[12,128]{1,0:T(8,128)} %get-tuple-element.366) | copy-start | bytes 18436
  526.8 7.9 %copy-start.60 = (f32[1536]{0:T(1024)S(1)}, f32[1536]{0:T(1024)}, u32[]{:S(2)}) copy-start(f32[1536]{0:T(1024)} %get-tuple-element.287) | copy-start | bytes 18436
  526.8 7.9 %copy-start.69 = (f32[1536]{0:T(1024)S(1)}, f32[1536]{0:T(1024)}, u32[]{:S(2)}) copy-start(f32[1536]{0:T(1024)} %get-tuple-element.320) | copy-start | bytes 18436
  526.8 8.0 %copy-start.83 = (bf16[1024,1536]{1,0:T(8,128)(2,1)S(1)}, bf16[1024,1536]{1,0:T(8,128)(2,1)}, u32[]{:S(2)}) copy-start(bf16[1024,1536]{1,0:T(8,128)(2,1)} %get-tuple-element.227) | copy-start | bytes 9437188
  531.3 3.5 collective-permute-start.1
  744.2 7.1 copy-start.34
  746.4 6.3 copy-start.41
  748.9 5.8 copy-start.39
  751.4 5.4 copy-start.77
  751.4 5.4 copy-start.25
  (51 other events, 156.1 us)

commit v2 on v0

--- a/solution.py
+++ b/solution.py
@@ -1,6 +1,11 @@
+import math
+from types import SimpleNamespace
+
 import jax
 import jax.numpy as jnp
 from jax import lax
+from jax.experimental import pallas as pl
+from jax.experimental.pallas import tpu as pltpu
 from jax.sharding import PartitionSpec as P
 
 epsilon = 1e-06
@@ -93,6 +98,1215 @@
     igate = jax.nn.sigmoid(igate_pre)
     log_decay = -cfactor * jax.nn.softplus(-decay_in) * rgate
     return (jnp.exp(log_decay), jnp.sqrt(-jnp.expm1(2.0 * log_decay)) * igate * conv_in)
+
+
+MESH = pl.DeviceIdType.MESH
+
+
+class Place:
+    def __init__(self):
+        self.z = lax.axis_index("grp")
+        seq = lax.axis_index("seq")
+        self.core = seq % 2
+        self.x = (seq // 2) % 2
+        self.y = seq // 4
+        self.seq = seq
+        self.sib = (self.z, self.at(self.y, self.x, 1 - self.core))
+        self.xnb = (self.z, self.at(self.y, 1 - self.x, self.core))
+        self.ynb = (self.z, self.at(1 - self.y, self.x, self.core))
+
+    def at(self, y, x, core):
+        return (y * 2 + x) * 2 + core
+
+    def level(self, z):
+        return (z, self.seq)
+
+
+def meet(peers):
+    barrier = pltpu.get_barrier_semaphore()
+    for peer in peers:
+        pl.semaphore_signal(barrier, inc=1, device_id=peer, device_id_type=MESH)
+    pl.semaphore_wait(barrier, len(peers))
+
+
+def when(cond, body):
+    if cond is None:
+        body()
+    else:
+        pl.when(cond)(body)
+
+
+GOT = ("X", "Y", "D1", "D2", "SO", "SX", "SY", "S1", "S2")
+SENT = ("ox", "oy", "os", "fy", "fx", "zX", "zY", "zD1", "zD2", "SX", "SY", "S1", "S2")
+
+
+class Gather:
+    def __init__(self, place, shards, fulls, kinds, send, recv, own):
+        self.p, self.shards, self.fulls = place, shards, fulls
+        self.send, self.recv, self.own = send, recv, own
+        even = place.z % 2 == 0
+        odd = place.z % 2 == 1
+        self.fetch = [(None, even, odd)[kind] for kind in kinds]
+        self.shared = [kind > 0 for kind in kinds]
+        self.znb = place.level(place.z + 1 - 2 * (place.z % 2))
+
+    def part(self, i, name):
+        p = self.p
+        n = self.shards[i].shape[0]
+        spot = {
+            "O": (p.y, p.x, p.core), "X": (p.y, 1 - p.x, p.core), "Y": (1 - p.y, p.x, p.core),
+            "D1": (1 - p.y, 1 - p.x, p.core), "D2": (1 - p.y, 1 - p.x, p.core),
+            "SO": (p.y, p.x, 1 - p.core), "SX": (p.y, 1 - p.x, 1 - p.core), "SY": (1 - p.y, p.x, 1 - p.core),
+            "S1": (1 - p.y, 1 - p.x, 1 - p.core), "S2": (1 - p.y, 1 - p.x, 1 - p.core),
+        }[name]
+        first = pl.multiple_of(p.at(*spot) * n, n)
+        if name in ("D1", "S1"):
+            return pl.ds(first, n // 2)
+        if name in ("D2", "S2"):
+            return pl.ds(pl.multiple_of(first + n // 2, n // 2), n // 2)
+        return pl.ds(first, n)
+
+    def half(self, i, name, which):
+        n = self.shards[i].shape[0]
+        first = self.part(i, name).start
+        return pl.ds(pl.multiple_of(first + which * (n // 2), n // 2), n // 2)
+
+    def copy(self, i, how, got, peer, rows, src=None):
+        full = self.fulls[i]
+        return pltpu.make_async_remote_copy(
+            src_ref=full.at[rows] if src is None else src,
+            dst_ref=full.at[rows],
+            send_sem=self.send.at[i, SENT.index(how)],
+            recv_sem=self.recv.at[i, GOT.index(got)],
+            device_id=peer,
+            device_id_type=MESH,
+        )
+
+    def wait(self, i, name):
+        self.copy(i, "ox", name, self.p.sib, self.part(i, name)).wait_recv()
+
+    def own_far(self, i):
+        p, mine = self.p, self.part(i, "O")
+        return [self.copy(i, "ox", "X", p.xnb, mine, self.shards[i]), self.copy(i, "oy", "Y", p.ynb, mine, self.shards[i])]
+
+    def own_near(self, i):
+        return self.copy(i, "os", "SO", self.p.sib, self.part(i, "O"), self.shards[i])
+
+    def own_kept(self, i):
+        return pltpu.make_async_copy(self.shards[i], self.fulls[i].at[self.part(i, "O")], self.own.at[i])
+
+    def start(self, i):
+        def far():
+            for c in self.own_far(i):
+                c.start()
+
+        when(self.fetch[i], far)
+        self.own_near(i).start()
+        self.own_kept(i).start()
+
+    def onward_far(self, i, name):
+        p = self.p
+        far = []
+        if name == "X":
+            far.append(self.copy(i, "fy", "D1", p.ynb, self.half(i, "X", 0)))
+        if name == "Y":
+            far.append(self.copy(i, "fx", "D2", p.xnb, self.half(i, "Y", 1)))
+        if self.shared[i]:
+            far.append(self.copy(i, "z" + name, name, self.znb, self.part(i, name)))
+        return far
+
+    def onward_near(self, i, name):
+        to_sib = {"X": "SX", "Y": "SY", "D1": "S1", "D2": "S2"}[name]
+        return self.copy(i, to_sib, to_sib, self.p.sib, self.part(i, name))
+
+    def relay(self, i, names):
+        for name in names:
+            self.wait(i, name)
+
+            def far(name=name):
+                for c in self.onward_far(i, name):
+                    c.start()
+
+            if name in ("X", "Y") or self.shared[i]:
+                when(self.fetch[i], far)
+            self.onward_near(i, name).start()
+
+    def arrive(self, i):
+        for name in ("SO", "SX", "SY", "S1", "S2"):
+            self.wait(i, name)
+        self.own_kept(i).wait()
+
+    def drain(self, i):
+        self.own_near(i).wait_send()
+        for name in ("X", "Y", "D1", "D2"):
+            self.onward_near(i, name).wait_send()
+
+        def far():
+            for c in self.own_far(i):
+                c.wait_send()
+            for name in ("X", "Y", "D1", "D2"):
+                for c in self.onward_far(i, name):
+                    c.wait_send()
+
+        when(self.fetch[i], far)
+
+    def peers(self):
+        return [self.p.sib, self.p.xnb, self.p.ynb, self.znb]
+
+
+def rows_loop(total, body, step=16):
+    @pl.loop(0, total // step)
+    def _(k):
+        body(pl.ds(pl.multiple_of(k * step, step), step))
+
+
+def wide(value):
+    return value.astype(jnp.float32)
+
+class Reduce:
+    def __init__(self, place, slots, sems):
+        self.p = place
+        self.slots = slots
+        self.send, self.recv = sems
+        z = place.z
+        self.inner = (z == 1) | (z == 2)
+        self.outer = (z == 0) | (z == 3)
+        self.mine = jnp.where(z == 2, 1, 0)
+        self.peer = place.level(jnp.where(self.inner, 3 - z, z))
+        self.out = place.level(jnp.where(z < 2, 1 - z, 5 - z))
+        self.me = 2 * place.y + place.x
+
+    def copy(self, i, tag, src, dst, peer):
+        return pltpu.make_async_remote_copy(
+            src_ref=src, dst_ref=dst, send_sem=self.send.at[i, tag], recv_sem=self.recv.at[i, tag], device_id=peer, device_id_type=MESH
+        )
+
+    def to_sib(self, i):
+        s = self.slots[i]
+        return self.copy(i, 0, s.stage, s.landed, self.p.sib)
+
+    def first(self, i):
+        p, s = self.p, self.slots[i]
+        return [
+            self.copy(i, 4, s.ab.at[0, 1 - p.x], s.xr.at[0], p.xnb),
+            self.copy(i, 5, s.ab.at[0, 2 + 1 - p.x], s.xr.at[1], p.xnb),
+            self.copy(i, 6, s.ab.at[1, 2 * (1 - p.y)], s.yr.at[0], p.ynb),
+            self.copy(i, 7, s.ab.at[1, 2 * (1 - p.y) + 1], s.yr.at[1], p.ynb),
+        ]
+
+    def second(self, i):
+        p, s = self.p, self.slots[i]
+        return [
+            self.copy(i, 8, s.ab.at[0, 2 * (1 - p.y) + p.x], s.yr2, p.ynb),
+            self.copy(i, 9, s.ab.at[1, 2 * p.y + 1 - p.x], s.xr2, p.xnb),
+        ]
+
+    def start_first(self, i):
+        for cp in self.first(i):
+            cp.start()
+
+    def add_first(self, i):
+        p, s = self.p, self.slots[i]
+        for cp in self.first(i):
+            cp.wait_recv()
+        for q in range(2):
+            ja, jb = 2 * q + p.x, 2 * p.y + q
+
+            def body(rows, q=q, ja=ja, jb=jb):
+                s.ab[0, ja, rows, :] = low(wide(s.ab[0, ja, rows, :]) + wide(s.xr[q, rows, :]))
+                s.ab[1, jb, rows, :] = low(wide(s.ab[1, jb, rows, :]) + wide(s.yr[q, rows, :]))
+
+            rows_loop(s.n, body)
+        for cp in self.second(i):
+            cp.start()
+
+    def up(self, i):
+        s = self.slots[i]
+        return [self.copy(i, 10 + k, s.ab.at[k, self.me], s.zo.at[k], self.out) for k in range(2)]
+
+    def across(self, i):
+        s = self.slots[i]
+        return self.copy(i, 12, s.ab.at[1 - self.mine, self.me], s.zp, self.peer)
+
+    def total_out(self, i):
+        res = self.slots[i].res.at[self.mine]
+        return [self.copy(i, 13, res, res, self.out), self.copy(i, 14, res, res, self.peer)]
+
+    def total_on(self, i):
+        res = self.slots[i].res.at[1 - self.mine]
+        return self.copy(i, 15, res, res, self.out)
+
+    def add_second(self, i):
+        s, me = self.slots[i], self.me
+        for cp in self.second(i):
+            cp.wait_recv()
+
+        def body(rows):
+            s.ab[0, me, rows, :] = low(wide(s.ab[0, me, rows, :]) + wide(s.yr2[rows, :]))
+            s.ab[1, me, rows, :] = low(wide(s.ab[1, me, rows, :]) + wide(s.xr2[rows, :]))
+
+        rows_loop(s.n, body)
+
+        @pl.when(self.outer)
+        def _():
+            for cp in self.up(i):
+                cp.start()
+
+    def add_outer(self, i):
+        s, me = self.slots[i], self.me
+
+        @pl.when(self.inner)
+        def _():
+            for cp in self.up(i):
+                cp.wait_recv()
+
+            def body(rows):
+                for k in range(2):
+                    s.ab[k, me, rows, :] = low(wide(s.ab[k, me, rows, :]) + wide(s.zo[k, rows, :]))
+
+            rows_loop(s.n, body)
+            self.across(i).start()
+
+    def add_peer(self, i):
+        s, me, mine = self.slots[i], self.me, self.mine
+
+        @pl.when(self.inner)
+        def _():
+            self.across(i).wait_recv()
+
+            def body(rows):
+                s.res[mine, rows, :] = low(wide(s.ab[mine, me, rows, :]) + wide(s.zp[rows, :]))
+
+            rows_loop(s.n, body)
+            for cp in self.total_out(i):
+                cp.start()
+
+    def pass_on(self, i):
+        @pl.when(self.inner)
+        def _():
+            other = self.slots[i].res.at[1 - self.mine]
+            self.copy(i, 14, other, other, self.peer).wait_recv()
+            self.total_on(i).start()
+
+    def arrive(self, i):
+        res = self.slots[i].res
+
+        @pl.when(self.outer)
+        def _():
+            near = jnp.where(self.p.z == 3, 1, 0)
+            self.copy(i, 13, res.at[near], res.at[near], self.out).wait_recv()
+            self.copy(i, 15, res.at[1 - near], res.at[1 - near], self.out).wait_recv()
+
+    def drain(self, i):
+        @pl.when(self.outer)
+        def _():
+            for cp in self.up(i):
+                cp.wait_send()
+
+        @pl.when(self.inner)
+        def _():
+            for cp in [self.across(i), self.total_on(i)] + self.total_out(i):
+                cp.wait_send()
+
+        for cp in [self.to_sib(i)] + self.first(i) + self.second(i):
+            cp.wait_send()
+
+
+class Small:
+    def __init__(self, place, total, slots, sems):
+        p = place
+        self.total, self.slots = total, slots
+        self.send, self.recv = sems
+        z = p.z
+        self.order = [p.sib, p.xnb, p.ynb, p.level(z + 1 - 2 * (z % 2)), p.level((z + 2) % 4)]
+
+    def copy(self, k):
+        return pltpu.make_async_remote_copy(
+            src_ref=self.slots.at[0, k],
+            dst_ref=self.slots.at[1, k],
+            send_sem=self.send.at[k],
+            recv_sem=self.recv.at[k],
+            device_id=self.order[k],
+            device_id_type=MESH,
+        )
+
+    def begin(self):
+        self.slots[0, 0] = self.total[...]
+        self.copy(0).start()
+
+    def step(self, k):
+        self.copy(k).wait_recv()
+        both = self.slots[0, k] + self.slots[1, k]
+        if k < 4:
+            self.slots[0, k + 1] = both
+            self.copy(k + 1).start()
+        else:
+            self.total[...] = both
+
+    def drain(self):
+        for k in range(5):
+            self.copy(k).wait_send()
+
+ROOT = math.sqrt(2.0 / math.pi)
+CUBE = 0.044715
+LANES = 128
+
+
+def low(value):
+    return value.astype(jnp.bfloat16)
+
+
+def gelu_parts(v):
+    square = v * v
+    t = jnp.tanh(ROOT * (v + CUBE * v * square))
+    half = 0.5 * (1.0 + t)
+    return v * half, half + 0.5 * v * (1.0 - t * t) * (ROOT * (1.0 + 3.0 * CUBE * square))
+
+
+def gelu_value(v):
+    return 0.5 * v * (1.0 + jnp.tanh(ROOT * (v + CUBE * v * (v * v))))
+
+
+def dot(left, right):
+    return jnp.dot(left, right, preferred_element_type=jnp.float32)
+
+
+def dot_t(left, right):
+    return lax.dot_general(left, right, (((1,), (1,)), ((), ())), preferred_element_type=jnp.float32)
+
+
+def sigmoid(v):
+    return 1.0 / (1.0 + jnp.exp(-v))
+
+
+def minus_expm1(twice, half_of):
+    t = jnp.tanh(half_of)
+    return -2.0 * t / (1.0 - t)
+
+
+def softplus_minus(v):
+    return jnp.maximum(-v, 0.0) + jnp.log1p(jnp.exp(-jnp.abs(v)))
+
+
+def strided_scan(decay_ref, value_ref, prod_ref, sum_ref, backward, rows):
+    tiles, _, lanes = sum_ref.shape
+    span = rows // 8
+
+    def step(k, carry):
+        prod, total = carry
+        t = span - 1 - k if backward else k
+        spot = pl.ds(t, 8, stride=span)
+        new_prod, new_total = [], []
+        for c in range(tiles):
+            d, v = decay_ref[c, spot, :], value_ref[c, spot, :]
+            if backward:
+                seen = total[c] + v
+                sum_ref[c, spot, :] = seen
+                prod_ref[c, spot, :] = prod[c]
+                new_prod.append(prod[c] * d)
+                new_total.append(seen * d)
+            else:
+                new_prod.append(prod[c] * d)
+                new_total.append(total[c] * d + v)
+                prod_ref[c, spot, :] = new_prod[c]
+                sum_ref[c, spot, :] = new_total[c]
+        return new_prod, new_total
+
+    ones = [jnp.ones((8, lanes), jnp.float32)] * tiles
+    zeros = [jnp.zeros((8, lanes), jnp.float32)] * tiles
+    return lax.fori_loop(0, span, step, (ones, zeros), unroll=2)
+
+
+def segment_ends(ends, backward):
+    before, whole = [], []
+    order = range(7, -1, -1) if backward else range(8)
+    for prod, total in zip(*ends):
+        p = jnp.ones((1, prod.shape[1]), jnp.float32)
+        s = jnp.zeros((1, prod.shape[1]), jnp.float32)
+        ps, ss = [None] * 8, [None] * 8
+        for k in order:
+            ps[k], ss[k] = p, s
+            d, v = prod[k : k + 1], total[k : k + 1]
+            p, s = p * d, s * d + v
+        before.append((jnp.concatenate(ps, axis=0), jnp.concatenate(ss, axis=0)))
+        whole.append((p, s))
+    return before, whole
+
+
+class Ends:
+    def __init__(self, place, slots, sems, backward):
+        self.p, self.slots, self.backward = place, slots, backward
+        self.send, self.recv = sems
+
+    def copy(self, d):
+        to = (self.p.seq + d) % 8
+        return pltpu.make_async_remote_copy(
+            src_ref=self.slots.at[self.p.seq], dst_ref=self.slots.at[self.p.seq], send_sem=self.send.at[d - 1],
+            recv_sem=self.recv.at[d - 1], device_id=(self.p.z, to), device_id_type=MESH,
+        )
+
+    def come(self, d):
+        src = (self.p.seq + 8 - d) % 8
+        return pltpu.make_async_remote_copy(
+            src_ref=self.slots.at[src], dst_ref=self.slots.at[src], send_sem=self.send.at[d - 1],
+            recv_sem=self.recv.at[d - 1], device_id=(self.p.z, src), device_id_type=MESH,
+        )
+
+    def tell(self, whole):
+        for c, (prod, total) in enumerate(whole):
+            self.slots[self.p.seq, 0, c : c + 1, :] = prod
+            self.slots[self.p.seq, 1, c : c + 1, :] = total
+        for d in range(1, 8):
+            self.copy(d).start()
+
+    def joined(self):
+        for d in range(1, 8):
+            self.come(d).wait_recv()
+        carry = jnp.zeros(self.slots.shape[2:], jnp.float32)
+        for k in range(7, 0, -1) if self.backward else range(7):
+            further = self.slots[k, 0] * carry + self.slots[k, 1]
+            counts = k > self.p.seq if self.backward else k < self.p.seq
+            carry = jnp.where(counts, further, carry)
+        return carry
+
+    def drain(self):
+        for d in range(1, 8):
+            self.copy(d).wait_send()
+
+
+def named(keys, refs):
+    return SimpleNamespace(**dict(zip(keys, refs)))
+
+
+HBM = pl.BlockSpec(memory_space=pl.ANY)
+VMEM = pl.BlockSpec(memory_space=pltpu.VMEM)
+
+
+def forward_call(lengths, tokens, shards):
+    rows, width = tokens.shape
+    lru = shards[1].shape[1]
+    ff = shards[5].shape[1]
+    tiles = lru // LANES
+    kinds = (0,) * 8
+    count = len(shards)
+    f32, bf = jnp.float32, jnp.bfloat16
+    shape = jax.ShapeDtypeStruct
+    wholes = [shape((8 * s.shape[0], s.shape[1]), s.dtype) for s in shards]
+    saved = dict(
+        mixed=shape((rows, width), bf),
+        small=shape((16, lru), f32),
+        n1t=shape((width, rows), bf),
+        pre=shape((tiles, rows, LANES), f32),
+        lin=shape((tiles, rows + 8, LANES), f32),
+        conv=shape((tiles, rows, LANES), bf),
+        convt=shape((tiles, LANES, rows), bf),
+        rgate=shape((tiles, rows, LANES), f32),
+        igate=shape((tiles, rows, LANES), f32),
+        state=shape((tiles, rows + 8, LANES), f32),
+        rect=shape((lru, rows), bf),
+        resid=shape((rows, width), f32),
+        n2t=shape((width, rows), bf),
+        mg=shape((rows, ff), f32),
+        mv=shape((rows, ff), f32),
+        hidt=shape((ff, rows), bf),
+    )
+    names = list(saved)
+    scratch = dict(
+        x=pltpu.VMEM((rows, width), bf),
+        n1=pltpu.VMEM((rows, width), bf),
+        n1t=pltpu.VMEM((width, rows), bf),
+        parts=pltpu.VMEM((8 * 16, lru), f32),
+        small=pltpu.VMEM((16, lru), f32),
+        pre=pltpu.VMEM((tiles, rows, LANES), f32),
+        lin=pltpu.VMEM((tiles, rows + 8, LANES), f32),
+        conv=pltpu.VMEM((tiles, rows, LANES), bf),
+        convt=pltpu.VMEM((tiles, LANES, rows), bf),
+        rgate=pltpu.VMEM((tiles, rows, LANES), f32),
+        igate=pltpu.VMEM((tiles, rows, LANES), f32),
+        prod=pltpu.VMEM((tiles, rows, LANES), f32),
+        state=pltpu.VMEM((tiles, rows + 8, LANES), f32),
+        total=pltpu.VMEM((tiles, rows, LANES), f32),
+        rec=pltpu.VMEM((rows, lru), bf),
+        rect=pltpu.VMEM((lru, rows), bf),
+        resid=pltpu.VMEM((rows, width), f32),
+        n2=pltpu.VMEM((rows, width), bf),
+        n2t=pltpu.VMEM((width, rows), bf),
+        hidden=pltpu.VMEM((rows, ff), bf),
+        ends=pltpu.VMEM((8, 2, tiles, LANES), f32),
+        gsend=pltpu.SemaphoreType.DMA((count, len(SENT))),
+        grecv=pltpu.SemaphoreType.DMA((count, len(GOT))),
+        gown=pltpu.SemaphoreType.DMA((count,)),
+        esend=pltpu.SemaphoreType.DMA((7,)),
+        erecv=pltpu.SemaphoreType.DMA((7,)),
+        hsend=pltpu.SemaphoreType.DMA(()),
+        hrecv=pltpu.SemaphoreType.DMA(()),
+        load=pltpu.SemaphoreType.DMA((2,)),
+        keep=pltpu.SemaphoreType.DMA((len(names),)),
+    )
+    keys = list(scratch)
+    R = 128
+
+    def kernel(lengths_ref, tokens_ref, *refs):
+        ins, outs = refs[:count], refs[count : 2 * count]
+        out = named(names, refs[2 * count : 2 * count + len(names)])
+        v = named(keys, refs[2 * count + len(names) :])
+        gelu_w, input_w, gates_w, output_w, mgate_w, mvalue_w, mdown_w = outs[1:]
+        place = Place()
+        gather = Gather(place, ins, outs, kinds, v.gsend, v.grecv, v.gown)
+        ends = Ends(place, v.ends, (v.esend, v.erecv), False)
+        z, seq = place.z, place.seq
+        meet([(z, (seq + d) % 8) for d in range(1, 8)])
+        kept = []
+
+        def keep(src, dst):
+            cp = pltpu.make_async_copy(src, dst, v.keep.at[len(kept)])
+            cp.start()
+            kept.append(cp)
+
+        load = pltpu.make_async_copy(tokens_ref, v.x, v.load.at[0])
+        load.start()
+        for i in range(4):
+            gather.start(i)
+        load.wait()
+        gather.relay(0, ("X", "Y"))
+        gather.start(4)
+        gather.relay(0, ("D1", "D2"))
+        gather.arrive(0)
+        load = pltpu.make_async_copy(outs[0], v.parts, v.load.at[1])
+        load.start()
+        gather.relay(1, ("X", "Y"))
+        load.wait()
+        small = v.small
+        total = v.parts[0:16, :]
+        for k in range(1, 8):
+            total = total + v.parts[16 * k : 16 * (k + 1), :]
+        small[...] = total
+        keep(v.small, out.small)
+
+        def norm_one(at):
+            x = wide(v.x[at, :])
+            scale = lax.rsqrt(jnp.mean(x * x, axis=-1, keepdims=True) + epsilon)
+            v.n1[at, :] = low(x * scale * small[8:9, :width])
+
+        rows_loop(rows, norm_one, 64)
+        gather.relay(2, ("X", "Y"))
+        gather.start(5)
+        gather.relay(1, ("D1", "D2"))
+
+        def turn(src, dst, at):
+            dst[at, :] = src[:, at].T
+
+        @pl.loop(0, width // 256)
+        def _(k):
+            turn(v.n1, v.n1t, pl.ds(pl.multiple_of(k * 256, 256), 256))
+
+        keep(v.n1t, out.n1t)
+        gather.relay(3, ("X", "Y"))
+        gather.relay(2, ("D1", "D2"))
+        gather.arrive(1)
+
+        def project(weight, dst, first):
+            def body(w):
+                t = pl.program_id(0)
+                both = dot(v.n1[...], w[...])
+                dst[2 * t, pl.ds(first, rows), :] = both[:, :LANES]
+                dst[2 * t + 1, pl.ds(first, rows), :] = both[:, LANES:]
+
+            pltpu.emit_pipeline(body, grid=(tiles // 2,), in_specs=[pl.BlockSpec((width, 2 * LANES), lambda t: (0, t))])(weight)
+
+        project(gelu_w, v.pre, 0)
+        keep(v.pre, out.pre)
+        gather.relay(4, ("X", "Y"))
+        gather.start(6)
+        gather.relay(3, ("D1", "D2"))
+        gather.arrive(2)
+        project(input_w, v.lin, 8)
+
+        def halo():
+            return pltpu.make_async_remote_copy(
+                src_ref=v.lin.at[:, pl.ds(rows, 8)], dst_ref=v.lin.at[:, pl.ds(0, 8)], send_sem=v.hsend, recv_sem=v.hrecv,
+                device_id=(z, (seq + 1) % 8), device_id_type=MESH,
+            )
+
+        @pl.when(seq < 7)
+        def _():
+            halo().start()
+
+        gather.relay(5, ("X", "Y"))
+        gather.relay(4, ("D1", "D2"))
+        gather.start(7)
+        gather.arrive(3)
+
+        @pl.when(seq == 0)
+        def _():
+            v.lin[:, 0:8, :] = jnp.zeros((tiles, 8, LANES), f32)
+
+        @pl.when(seq > 0)
+        def _():
+            halo().wait_recv()
+
+        keep(v.lin, out.lin)
+
+        def gates(w):
+            h = pl.program_id(0)
+            lane = pl.ds(pl.multiple_of(h * LANES, LANES), LANES)
+            taps = [small[k : k + 1, lane] for k in range(4)]
+            cb, rb, ib, dp = [small[k : k + 1, lane] for k in range(4, 8)]
+            rate = -cfactor * softplus_minus(dp)
+            for r in range(0, rows, R):
+                acc = cb + taps[0] * v.lin[h, 8 + r : 8 + r + R, :]
+                for k in range(1, 4):
+                    acc = acc + taps[k] * v.lin[h, 8 + r - k : 8 + r - k + R, :]
+                cl = low(acc)
+                v.conv[h, r : r + R, :] = cl
+                v.convt[h, :, r : r + R] = cl.T
+                both = dot(cl, w[...])
+                rg = sigmoid(both[:, :LANES] + rb)
+                ig = sigmoid(both[:, LANES:] + ib)
+                v.rgate[h, r : r + R, :] = rg
+                v.igate[h, r : r + R, :] = ig
+                log_decay = rate * rg
+                v.prod[h, r : r + R, :] = jnp.exp(log_decay)
+                v.total[h, r : r + R, :] = jnp.sqrt(minus_expm1(2.0 * log_decay, log_decay)) * ig * wide(cl)
+
+        pltpu.emit_pipeline(gates, grid=(tiles,), in_specs=[pl.BlockSpec((LANES, 2 * LANES), lambda h: (h, 0))])(gates_w)
+        for src, dst in ((v.conv, out.conv), (v.convt, out.convt), (v.rgate, out.rgate), (v.igate, out.igate)):
+            keep(src, dst)
+        gather.relay(6, ("X", "Y"))
+        gather.relay(5, ("D1", "D2"))
+        tails = strided_scan(v.prod, v.total, v.prod, v.total, False, rows)
+        before, whole = segment_ends(tails, False)
+        ends.tell(whole)
+        gather.relay(7, ("X", "Y"))
+        gather.relay(6, ("D1", "D2"))
+        carry = ends.joined()
+        span = rows // 8
+        for c in range(tiles):
+            v.state[c, 0:8, :] = jnp.broadcast_to(carry[c : c + 1, :], (8, LANES))
+            into = before[c][0] * carry[c : c + 1, :] + before[c][1]
+            v.parts[8 * c : 8 * c + 8, 0:LANES] = into
+
+        @pl.loop(0, tiles)
+        def _(c):
+            lane = pl.ds(pl.multiple_of(c * LANES, LANES), LANES)
+            into = v.parts[pl.ds(pl.multiple_of(c * 8, 8), 8), 0:LANES]
+            for s in range(8):
+                at = slice(s * span, (s + 1) * span)
+                state = v.total[c, at, :] + v.prod[c, at, :] * into[s : s + 1, :]
+                v.state[c, 8 + s * span : 8 + (s + 1) * span, :] = state
+                v.rec[at, lane] = low(state * gelu_value(v.pre[c, at, :]))
+            v.rect[lane, :] = v.rec[:, lane].T
+
+        keep(v.state, out.state)
+        keep(v.rect, out.rect)
+        gather.arrive(4)
+
+        def back_to_width(w):
+            t = pl.program_id(0)
+            at = pl.ds(pl.multiple_of(t * 256, 256), 256)
+            v.resid[:, at] = wide(v.x[:, at]) + dot(v.rec[...], w[...])
+
+        pltpu.emit_pipeline(back_to_width, grid=(width // 256,), in_specs=[pl.BlockSpec((lru, 256), lambda t: (0, t))])(output_w)
+        keep(v.resid, out.resid)
+        gather.relay(7, ("D1", "D2"))
+
+        def norm_two(at):
+            x = v.resid[at, :]
+            scale = lax.rsqrt(jnp.mean(x * x, axis=-1, keepdims=True) + epsilon)
+            v.n2[at, :] = low(x * scale * small[9:10, :width])
+
+        rows_loop(rows, norm_two, 64)
+
+        @pl.loop(0, width // 256)
+        def _(k):
+            turn(v.n2, v.n2t, pl.ds(pl.multiple_of(k * 256, 256), 256))
+
+        keep(v.n2t, out.n2t)
+        gather.arrive(5)
+        gather.arrive(6)
+
+        def mlp(wg, wv, mg, mv, hidt):
+            t = pl.program_id(0)
+            at = pl.ds(pl.multiple_of(t * 256, 256), 256)
+            mg[...] = dot(v.n2[...], wg[...])
+            mv[...] = dot(v.n2[...], wv[...])
+
+            def act(rs):
+                v.hidden[rs, at] = low(gelu_value(mg[rs, :]) * mv[rs, :])
+
+            rows_loop(rows, act, 64)
+            hidt[...] = v.hidden[:, at].T
+
+        wide_tile = pl.BlockSpec((width, 256), lambda t: (0, t))
+        pltpu.emit_pipeline(
+            mlp,
+            grid=(ff // 256,),
+            in_specs=[wide_tile, wide_tile],
+            out_specs=[pl.BlockSpec((rows, 256), lambda t: (0, t))] * 2 + [pl.BlockSpec((256, rows), lambda t: (t, 0))],
+        )(mgate_w, mvalue_w, out.mg, out.mv, out.hidt)
+        gather.arrive(7)
+        valid_rows = lengths_ref[z] - seq * rows
+
+        def down(w, mixed):
+            t = pl.program_id(0)
+            at = pl.ds(pl.multiple_of(t * 256, 256), 256)
+            valid = (lax.broadcasted_iota(jnp.int32, (rows, 256), 0) < valid_rows).astype(f32)
+            mixed[...] = low((v.resid[:, at] + dot(v.hidden[...], w[...])) * valid)
+
+        pltpu.emit_pipeline(
+            down,
+            grid=(width // 256,),
+            in_specs=[pl.BlockSpec((ff, 256), lambda t: (0, t))],
+            out_specs=[pl.BlockSpec((rows, 256), lambda t: (0, t))],
+        )(mdown_w, out.mixed)
+        for cp in kept:
+            cp.wait()
+        for i in range(count):
+            gather.drain(i)
+        ends.drain()
+
+        @pl.when(seq < 7)
+        def _():
+            halo().wait_send()
+
+    result = pl.pallas_call(
+        kernel,
+        out_shape=wholes + [saved[name] for name in names],
+        in_specs=[pl.BlockSpec(memory_space=pltpu.SMEM), HBM] + [HBM] * count,
+        out_specs=[HBM] * (count + len(names)),
+        scratch_shapes=[scratch[key] for key in keys],
+        compiler_params=pltpu.CompilerParams(collective_id=1, has_side_effects=True, vmem_limit_bytes=60 << 20),
+        name="forward",
+    )(lengths, tokens, *shards)
+    return result[:count], named(names, result[count:])
+
+def slot_scratch(rows, columns):
+    n, h = rows // 8, columns // 2
+    bf = jnp.bfloat16
+    return dict(
+        ab=pltpu.VMEM((2, 4, n, h), bf),
+        xr=pltpu.VMEM((2, n, h), bf),
+        yr=pltpu.VMEM((2, n, h), bf),
+        yr2=pltpu.VMEM((n, h), bf),
+        xr2=pltpu.VMEM((n, h), bf),
+        zo=pltpu.VMEM((2, n, h), bf),
+        zp=pltpu.VMEM((n, h), bf),
+        res=pltpu.VMEM((2, n, h), bf),
+    )
+
+
+def backward_call(lengths, tokens, cotangent, weights, saved):
+    rows, width = tokens.shape
+    gelu_full, input_full, gates_full, output_full, mgate_full, mvalue_full, mdown_full = weights
+    lru, ff = gelu_full.shape[1], mgate_full.shape[1]
+    tiles = lru // LANES
+    f32, bf = jnp.float32, jnp.bfloat16
+    shape = jax.ShapeDtypeStruct
+    DOWN, MGATE, MVALUE, OUTPUT, GELU, INPUT, GATES = range(7)
+    full = [mdown_full, mgate_full, mvalue_full, output_full, gelu_full, input_full, gates_full]
+    extents = [w.shape for w in full]
+    tile_of = [256, 512, 512, 256, 256, 256, None]
+    count = len(full)
+    split = lambda v: v.reshape(4, 2, v.shape[0] // 8, v.shape[1])
+    inputs = dict(
+        tokens=tokens, cot=cotangent, gelu_w=gelu_full, input_w=input_full, gates_w=gates_full, output_w=output_full, mgate_w=mgate_full,
+        mvalue_w=mvalue_full, mdown_w=mdown_full, small=saved.small, n1t=split(saved.n1t), pre=saved.pre, lin=saved.lin, conv=saved.conv,
+        convt=saved.convt, rgate=saved.rgate, igate=saved.igate, state=saved.state, rect=split(saved.rect), resid=saved.resid,
+        n2t=split(saved.n2t), mg=saved.mg, mv=saved.mv, hidt=split(saved.hidt),
+    )
+    slot_keys = list(slot_scratch(8, 256))
+    scratch = dict(
+        go=pltpu.VMEM((rows, width), bf),
+        gm=pltpu.VMEM((rows, width), bf),
+        gn=pltpu.VMEM((rows, width), f32),
+        x=pltpu.VMEM((rows, width), bf),
+        resid=pltpu.VMEM((rows, width), f32),
+        gh=pltpu.VMEM((rows, 256), f32),
+        small=pltpu.VMEM((16, lru), f32),
+        part=pltpu.VMEM((16, lru), f32),
+        gain=pltpu.VMEM((8, width), f32),
+        adj=pltpu.VMEM((tiles, rows + 8, LANES), f32),
+        prod=pltpu.VMEM((tiles, rows, LANES), f32),
+        into=pltpu.VMEM((tiles, 8, LANES), f32),
+        gg=pltpu.VMEM((rows, lru), bf),
+        gl=pltpu.VMEM((rows, lru), bf),
+        gri=pltpu.VMEM((rows, 2 * LANES), bf),
+        direct=pltpu.VMEM((rows, LANES), f32),
+        gstage=pltpu.VMEM((4, 2, lru // 8, 2 * LANES), bf),
+        glanded=pltpu.VMEM((4, lru // 8, 2 * LANES), bf),
+        ends=pltpu.VMEM((8, 2, tiles, LANES), f32),
+        sslots=pltpu.VMEM((2, 5, 16, lru), f32),
+        rsend=pltpu.SemaphoreType.DMA((count, 16)),
+        rrecv=pltpu.SemaphoreType.DMA((count, 16)),
+        esend=pltpu.SemaphoreType.DMA((7,)),
+        erecv=pltpu.SemaphoreType.DMA((7,)),
+        hsend=pltpu.SemaphoreType.DMA(()),
+        hrecv=pltpu.SemaphoreType.DMA(()),
+        ssend=pltpu.SemaphoreType.DMA((5,)),
+        srecv=pltpu.SemaphoreType.DMA((5,)),
+        load=pltpu.SemaphoreType.DMA((4,)),
+        keep=pltpu.SemaphoreType.DMA((count + 1, 2)),
+    )
+    keys = list(scratch)
+    outs = dict(
+        tokens_grad=shape((rows, width), f32),
+        small_sum=shape((16, lru), f32),
+        gmg=shape((rows, ff), bf),
+        gmv=shape((rows, ff), bf),
+    )
+    out_keys = list(outs)
+    stages = [shape((4, r // 8, c), bf) for r, c in extents[:-1]]
+    sums = [shape((r // 8, c), bf) for r, c in extents]
+
+    def kernel(lengths_ref, *refs):
+        refs = list(refs)
+
+        def take(k):
+            got = refs[:k]
+            del refs[:k]
+            return got
+
+        w = named(inputs, take(len(inputs)))
+        out = named(out_keys, take(len(out_keys)))
+        sum_refs = take(count)
+        staged, landed = take(count - 1), take(count - 1)
+        v = named(keys, take(len(keys)))
+        slots = []
+        for i, (r, c) in enumerate(extents):
+            s = named(slot_keys, take(len(slot_keys)))
+            s.n, s.h, s.columns, s.tile = r // 8, c // 2, c, tile_of[i]
+            slots.append(s)
+        place = Place()
+        z, seq, core = place.z, place.seq, place.core
+        for i in range(count - 1):
+            slots[i].stage, slots[i].landed = staged[i], landed[i]
+        slots[GATES].stage, slots[GATES].landed = v.gstage.at[:, 1 - core], v.glanded
+        red = Reduce(place, slots, (v.rsend, v.rrecv))
+        ends = Ends(place, v.ends, (v.esend, v.erecv), True)
+        tot = Small(place, v.part, v.sslots, (v.ssend, v.srecv))
+        loads = [
+            pltpu.make_async_copy(w.cot, v.go, v.load.at[0]),
+            pltpu.make_async_copy(w.small, v.small, v.load.at[1]),
+            pltpu.make_async_copy(w.resid, v.resid, v.load.at[2]),
+            pltpu.make_async_copy(w.tokens, v.x, v.load.at[3]),
+        ]
+        for cp in loads:
+            cp.start()
+        meet([(z, (seq + d) % 8) for d in range(1, 8)] + [((z + d) % 4, seq) for d in range(1, 4)])
+        loads[0].wait()
+        valid_rows = lengths_ref[z] - seq * rows
+
+        def mask(at):
+            here = lax.broadcasted_iota(jnp.int32, (64, width), 0) + at.start < valid_rows
+            v.go[at, :] = low(jnp.where(here, wide(v.go[at, :]), 0.0))
+
+        rows_loop(rows, mask, 64)
+
+        def spread(s, left, right):
+            return dot(left[...].reshape(4 * s.n, rows), right).reshape(4, s.n, s.tile)
+
+        def right_of(held, s):
+            t = pl.program_id(0)
+            return held[:, pl.ds(pl.multiple_of(t * s.tile, s.tile), s.tile)]
+
+        def weight_pass(i, left, right, streamed, own):
+            s = slots[i]
+            steps = s.columns // s.tile
+            in_specs = [pl.BlockSpec((4, None, s.n, rows), lambda t: (0, core if own else 1 - core, 0, 0))]
+            operands = [left]
+            if streamed:
+                in_specs.append(pl.BlockSpec((rows, s.tile), lambda t: (0, t)))
+                operands.append(right)
+            block = pl.BlockSpec((4, s.n, s.tile), lambda t: (0, 0, t))
+
+            def body(*args):
+                value = spread(s, args[0], args[1][...] if streamed else right_of(right, s))
+                if own:
+                    t = pl.program_id(0)
+                    half = steps // 2
+                    at = pl.ds(pl.multiple_of((t % half) * s.tile, s.tile), s.tile)
+                    s.ab[t // half, :, :, at] = low(value + wide(args[-1][...]))
+                else:
+                    args[-1][...] = low(value)
+
+            if own:
+                red.to_sib(i).wait_recv()
+                pltpu.emit_pipeline(body, grid=(steps,), in_specs=in_specs + [block])(*operands, s.landed)
+                red.start_first(i)
+            else:
+                pltpu.emit_pipeline(body, grid=(steps,), in_specs=in_specs, out_specs=[block])(*operands, s.stage)
+                red.to_sib(i).start()
+
+        weight_pass(DOWN, w.hidt, v.go, False, False)
+
+        def mlp(md, mg, mv, wg, wv, gmg, gmv):
+            v.gh[...] = dot_t(v.go[...], md[...])
+
+            def act(at):
+                value, slope = gelu_parts(mg[at, :])
+                gh = v.gh[at, :]
+                gmg[at, :] = low(gh * mv[at, :] * slope)
+                gmv[at, :] = low(gh * value)
+
+            rows_loop(rows, act, 64)
+            more = dot_t(gmg[...], wg[...]) + dot_t(gmv[...], wv[...])
+
+            @pl.when(pl.program_id(0) == 0)
+            def _():
+                v.gn[...] = more
+
+            @pl.when(pl.program_id(0) > 0)
+            def _():
+                v.gn[...] += more
+
+        across = pl.BlockSpec((rows, 256), lambda t: (0, t))
+        pltpu.emit_pipeline(
+            mlp,
+            grid=(ff // 256,),
+            in_specs=[pl.BlockSpec((256, width), lambda t: (t, 0)), across, across]
+            + [pl.BlockSpec((width, 256), lambda t: (0, t))] * 2,
+            out_specs=[across, across],
+        )(w.mdown_w, w.mg, w.mv, w.mgate_w, w.mvalue_w, out.gmg, out.gmv)
+        weight_pass(DOWN, w.hidt, v.go, False, True)
+        weight_pass(MGATE, w.n2t, out.gmg, True, False)
+        weight_pass(MVALUE, w.n2t, out.gmv, True, False)
+        for cp in loads[1:]:
+            cp.wait()
+        small, part = v.small, v.part
+        part[...] = jnp.zeros_like(part)
+
+        def eight(value):
+            return value.reshape(value.shape[0] // 8, 8, value.shape[1]).sum(axis=0)
+
+        def norm_back(read, gain, write):
+            v.gain[...] = jnp.zeros_like(v.gain)
+
+            def chunk(at):
+                x, grad, add = read(at)
+                scale = lax.rsqrt(jnp.mean(x * x, axis=-1, keepdims=True) + epsilon)
+                v.gain[...] += eight(grad * x * scale)
+                scaled = grad * gain
+                m = jnp.mean(scaled * x, axis=-1, keepdims=True)
+                write(at, add + scale * (scaled - x * (scale * scale * m)))
+
+            rows_loop(rows, chunk, 64)
+            return v.gain[...].sum(axis=0, keepdims=True)
+
+        def keep_resid(at, value):
+            v.gn[at, :] = value
+            v.gm[at, :] = low(value)
+
+        part[9:10, :width] = norm_back(lambda at: (v.resid[at, :], v.gn[at, :], wide(v.go[at, :])), small[9:10, :width], keep_resid)
+        weight_pass(MGATE, w.n2t, out.gmg, True, True)
+        weight_pass(MVALUE, w.n2t, out.gmv, True, True)
+        red.add_first(DOWN)
+
+        weight_pass(OUTPUT, w.rect, v.gm, False, False)
+
+        def into_branch(wo, pre, state, rgate):
+            t = pl.program_id(0)
+            v.gh[...] = dot_t(v.gm[...], wo[...])
+            for q in range(2):
+                c = 2 * t + q
+                lane = pl.ds(pl.multiple_of(c * LANES, LANES), LANES)
+                rate = -cfactor * softplus_minus(small[7:8, lane])
+
+                def chunk(at, q=q, c=c, lane=lane, rate=rate):
+                    grad = v.gh[at, q * LANES : (q + 1) * LANES]
+                    value, slope = gelu_parts(pre[q, at, :])
+                    v.adj[c, at, :] = grad * value
+                    v.gg[at, lane] = low(grad * state[q, pl.ds(pl.multiple_of(at.start + 8, 8), 64), :] * slope)
+                    v.prod[c, at, :] = jnp.exp(rate * rgate[q, at, :])
+
+                rows_loop(rows, chunk, 64)
+
+        pair = lambda t: (t, 0, 0)
+        pltpu.emit_pipeline(
+            into_branch,
+            grid=(tiles // 2,),
+            in_specs=[
+                pl.BlockSpec((256, width), lambda t: (t, 0)), pl.BlockSpec((2, rows, LANES), pair),
+                pl.BlockSpec((2, rows + 8, LANES), pair), pl.BlockSpec((2, rows, LANES), pair),
+            ],
+        )(w.output_w, w.pre, w.state, w.rgate)
+        weight_pass(OUTPUT, w.rect, v.gm, False, True)
+        tails = strided_scan(v.prod, v.adj, v.prod, v.adj, True, rows)
+        before, whole = segment_ends(tails, True)
+        ends.tell(whole)
+        weight_pass(GELU, w.n1t, v.gg, False, False)
+        red.add_first(MGATE)
+        carry = ends.joined()
+        for c in range(tiles):
+            v.into[c] = before[c][0] * carry[c : c + 1, :] + before[c][1]
+        span = rows // 8
+
+        def through_gates(rgate, igate, conv, convt, state, wg):
+            c = pl.program_id(0)
+            lane = pl.ds(pl.multiple_of(c * LANES, LANES), LANES)
+            dp = small[7:8, lane]
+            rate = -cfactor * softplus_minus(dp)
+            sums = [jnp.zeros((8, LANES), f32) for _ in range(3)]
+            for k in range(8):
+                at = slice(k * span, (k + 1) * span)
+                adj = v.adj[c, at, :] + v.prod[c, at, :] * v.into[c, k : k + 1, :]
+                rg, ig, cv = rgate[at, :], igate[at, :], wide(conv[at, :])
+                log_decay = rate * rg
+                decay = jnp.exp(log_decay)
+                mult = jnp.sqrt(minus_expm1(2.0 * log_decay, log_decay))
+                grad_decay = adj * state[7 + k * span : 7 + (k + 1) * span, :]
+                grad_log = grad_decay * decay - adj * ig * cv * (decay * decay) / mult
+                grad_r = grad_log * rate * rg * (1.0 - rg)
+                through = adj * mult
+                grad_i = through * cv * ig * (1.0 - ig)
+                v.direct[at, :] = through * ig
+                v.gri[at, :LANES] = low(grad_r)
+                v.gri[at, LANES:] = low(grad_i)
+                for q, value in enumerate((grad_log * rg, grad_r, grad_i)):
+                    sums[q] = sums[q] + eight(value)
+            part[7:8, lane] = sums[0].sum(axis=0, keepdims=True) * (cfactor * sigmoid(-dp))
+            part[5:6, lane] = sums[1].sum(axis=0, keepdims=True)
+            part[6:7, lane] = sums[2].sum(axis=0, keepdims=True)
+            product = low(dot(convt[...], v.gri[...]))
+            for q in range(2):
+                unit = 2 * c + q
+                block = unit // 3
+                at = pl.ds(pl.multiple_of((unit % 3) * 64, 64), 64)
+                v.gstage[block // 2, block % 2, at, :] = product[64 * q : 64 * (q + 1), :]
+            grad_conv = v.direct[...] + dot_t(v.gri[...], wg[...])
+            v.adj[c, pl.ds(0, rows), :] = grad_conv
+            part[4:5, lane] = eight(grad_conv).sum(axis=0, keepdims=True)
+
+        one = lambda t: (t, 0, 0)
+        pltpu.emit_pipeline(
+            through_gates,
+            grid=(tiles,),
+            in_specs=[
+                pl.BlockSpec((None, rows, LANES), one), pl.BlockSpec((None, rows, LANES), one), pl.BlockSpec((None, rows, LANES), one),
+                pl.BlockSpec((None, LANES, rows), one), pl.BlockSpec((None, rows + 8, LANES), one),
+                pl.BlockSpec((LANES, 2 * LANES), lambda t: (t, 0)),
+            ],
+        )(w.rgate, w.igate, w.conv, w.convt, w.state, w.gates_w)
+
+        def halo():
+            return pltpu.make_async_remote_copy(
+                src_ref=v.adj.at[:, pl.ds(0, 8)], dst_ref=v.adj.at[:, pl.ds(rows, 8)], send_sem=v.hsend, recv_sem=v.hrecv,
+                device_id=(z, (seq + 7) % 8), device_id_type=MESH,
+            )
+
+        @pl.when(seq > 0)
+        def _():
+            halo().start()
+
+        red.to_sib(GATES).start()
+        weight_pass(GELU, w.n1t, v.gg, False, True)
+        red.add_first(MVALUE)
+        red.add_second(DOWN)
+
+        @pl.when(seq == 7)
+        def _():
+            v.adj[:, pl.ds(rows, 8), :] = jnp.zeros((tiles, 8, LANES), f32)
+
+        @pl.when(seq < 7)
+        def _():
+            halo().wait_recv()
+
+        def through_conv(lin):
+            c = pl.program_id(0)
+            lane = pl.ds(pl.multiple_of(c * LANES, LANES), LANES)
+            taps = [small[k : k + 1, lane] for k in range(4)]
+            sums = [jnp.zeros((8, LANES), f32) for _ in range(4)]
+            for r in range(0, rows, 128):
+                here = v.adj[c, r : r + 128, :]
+                acc = taps[0] * here
+                for k in range(4):
+                    sums[k] = sums[k] + eight(here * lin[8 + r - k : 8 + r - k + 128, :])
+                    if k:
+                        acc = acc + taps[k] * v.adj[c, r + k : r + k + 128, :]
+                v.gl[r : r + 128, lane] = low(acc)
+            for k in range(4):
+                part[k : k + 1, lane] = sums[k].sum(axis=0, keepdims=True)
+
+        pltpu.emit_pipeline(through_conv, grid=(tiles,), in_specs=[pl.BlockSpec((None, rows + 8, LANES), one)])(w.lin)
+        weight_pass(INPUT, w.n1t, v.gl, False, False)
+
+        def gates_own():
+            s = slots[GATES]
+            red.to_sib(GATES).wait_recv()
+            for j in range(4):
+
+                def body(at, j=j):
+                    both = low(wide(v.gstage[j, core, at, :]) + wide(v.glanded[j, at, :]))
+                    s.ab[0, j, at, :] = both[:, : s.h]
+                    s.ab[1, j, at, :] = both[:, s.h :]
+
+                rows_loop(s.n, body)
+            red.start_first(GATES)
+
+        def into_norm(wi, wg):
+            t = pl.program_id(0)
+            at = pl.ds(pl.multiple_of(t * 256, 256), 256)
+            v.resid[:, at] = dot_t(v.gl[...], wi[...]) + dot_t(v.gg[...], wg[...])
+
+        pltpu.emit_pipeline(into_norm, grid=(width // 256,), in_specs=[pl.BlockSpec((256, lru), lambda t: (t, 0))] * 2)(w.input_w, w.gelu_w)
+        weight_pass(INPUT, w.n1t, v.gl, False, True)
+        gates_own()
+        red.add_first(OUTPUT)
+        red.add_second(MGATE)
+        red.add_outer(DOWN)
+
+        def keep_tokens(at, value):
+            v.gn[at, :] = value
+
+        part[8:9, :width] = norm_back(lambda at: (wide(v.x[at, :]), v.resid[at, :], v.gn[at, :]), small[8:9, :width], keep_tokens)
+        tot.begin()
+        kept = [pltpu.make_async_copy(v.gn, out.tokens_grad, v.keep.at[count, 0])]
+        kept[0].start()
+
+        def finish(i):
+            s = slots[i]
+            red.arrive(i)
+            for k in range(2):
+                cp = pltpu.make_async_copy(s.res.at[k], sum_refs[i].at[:, pl.ds(k * s.h, s.h)], v.keep.at[i, k])
+                cp.start()
+                kept.append(cp)
+
+        steps = [
+            (red.add_first, GELU), (red.add_second, MVALUE), (red.add_outer, MGATE), (red.add_peer, DOWN), (tot.step, 0),
+            (red.add_first, INPUT), (red.add_second, OUTPUT), (red.add_outer, MVALUE), (red.add_peer, MGATE), (red.pass_on, DOWN), (tot.step, 1),
+            (red.add_first, GATES), (red.add_second, GELU), (red.add_outer, OUTPUT), (red.add_peer, MVALUE), (red.pass_on, MGATE), (finish, DOWN),
+            (tot.step, 2),
+            (red.add_second, INPUT), (red.add_outer, GELU), (red.add_peer, OUTPUT), (red.pass_on, MVALUE), (finish, MGATE), (tot.step, 3),
+            (red.add_second, GATES), (red.add_outer, INPUT), (red.add_peer, GELU), (red.pass_on, OUTPUT), (finish, MVALUE), (tot.step, 4),
+            (red.add_outer, GATES), (red.add_peer, INPUT), (red.pass_on, GELU), (finish, OUTPUT),
+            (red.add_peer, GATES), (red.pass_on, INPUT), (finish, GELU), (red.pass_on, GATES), (finish, INPUT), (finish, GATES),
+        ]
+        for act, i in steps:
+            act(i)
+        cp = pltpu.make_async_copy(part, out.small_sum, v.keep.at[count, 1])
+        cp.start()
+        kept.append(cp)
+        for cp in kept:
+            cp.wait()
+        for i in range(count):
+            red.drain(i)
+        tot.drain()
+        ends.drain()
+
+        @pl.when(seq > 0)
+        def _():
+            halo().wait_send()
+
+    slot_list = [value for r, c in extents for value in slot_scratch(r, c).values()]
+    result = pl.pallas_call(
+        kernel,
+        out_shape=list(outs.values()) + sums + stages + stages,
+        in_specs=[pl.BlockSpec(memory_space=pltpu.SMEM)] + [HBM] * len(inputs),
+        out_specs=[HBM] * (len(outs) + count + 2 * (count - 1)),
+        scratch_shapes=list(scratch.values()) + slot_list,
+        compiler_params=pltpu.CompilerParams(collective_id=2, has_side_effects=True, vmem_limit_bytes=62 << 20),
+        name="backward",
+    )(lengths, *inputs.values())
+    return result[0], result[1], result[len(outs) : len(outs) + count]
 
 
 def local(
@@ -355,6 +1569,65 @@
     )
 
 
+def local_fast(
+    tokens,
+    lengths,
+    mixer_gain,
+    gelu_weight,
+    input_weight,
+    conv_taps,
+    conv_bias,
+    rgate_weight,
+    rgate_bias,
+    igate_weight,
+    igate_bias,
+    decay_param,
+    output_weight,
+    mlp_gain,
+    mlp_gate,
+    mlp_value,
+    mlp_down,
+    cotangent,
+):
+    block = rgate_weight.shape[1]
+    width_lru = input_weight.shape[1]
+    lru_rows = jnp.concatenate(
+        [conv_taps.T, conv_bias[None], rgate_bias[None], igate_bias[None], decay_param[None]], axis=0
+    ).astype(jnp.float32)
+    model_rows = jnp.stack([mixer_gain, mlp_gain]).astype(jnp.float32)
+    mine = lax.axis_index("seq")
+    small = jnp.zeros((16, width_lru), jnp.float32)
+    small = lax.dynamic_update_slice(small, lru_rows, (0, mine * lru_rows.shape[1]))
+    small = lax.dynamic_update_slice(small, model_rows, (8, mine * model_rows.shape[1]))
+    gates = jnp.concatenate([rgate_weight, igate_weight], axis=1)
+    weights, saved = forward_call(
+        lengths, tokens, [small, gelu_weight, input_weight, gates, output_weight, mlp_gate, mlp_value, mlp_down]
+    )
+    tokens_grad, small_sum, big = backward_call(lengths, tokens, cotangent, weights[1:], saved)
+    down, mgate, mvalue, out_w, gelu_w, input_w, gates = [value.astype(jnp.float32) for value in big]
+    lru_own = lax.dynamic_slice(small_sum, (0, mine * conv_bias.shape[0]), (8, conv_bias.shape[0]))
+    model_own = lax.dynamic_slice(small_sum, (8, mine * mixer_gain.shape[0]), (2, mixer_gain.shape[0]))
+    return (
+        saved.mixed,
+        tokens_grad,
+        model_own[0],
+        gelu_w,
+        input_w,
+        lru_own[:4].T,
+        lru_own[4],
+        gates[:, :block],
+        lru_own[5],
+        gates[:, block:],
+        lru_own[6],
+        lru_own[7],
+        out_w,
+        model_own[1],
+        mgate,
+        mvalue,
+        down,
+    )
+
+
 def solution(mesh):
     placed = (
         P(("grp", "seq"), None),
@@ -376,8 +1649,9 @@
         P("seq", None),
         P(("grp", "seq"), None),
     )
+    fits = mesh.shape["grp"] == 4 and mesh.shape["seq"] == 8
     return jax.shard_map(
-        local,
+        local_fast if fits else local,
         mesh=mesh,
         in_specs=placed,
         out_specs=(

time: 1880 us -> 461 us (0.25); the launches traced: 1850 us -> 458 us
  waiting for transfers between devices: 715 us -> 0 us
  local copies, waits for them, and re-layouts: 624 us -> 12 us
  Pallas kernels: 0 us -> 434 us
  other arithmetic: 196 us -> 12.1 us
  matrix products: 150 us -> 0 us
  blocking collectives: 146 us -> 0 us
    reduce_scatter x8 -> x0, waiting for transfers between devices: 470 us -> none  [the longest x1 96.3 us: local(): lax.psum_scatter(partials[13], 'seq', scatter_dimension=0, tiled=True)]
    pallas_call x0 -> x2, Pallas kernels: none -> 434 us  [the longest x1 276 us: backward_call(): pl.pallas_call(kernel, out_shape=list(outs.values()) + sums + stages + st...]
    slice x128 -> x2, local copies, waits for them, and re-layouts: 357 us -> 3.09 us  [the longest x1 1.58 us: local_fast(): gates[:, block:]]
    psum x1 -> x0, waiting for transfers between devices: 241 us -> none  [local(): totals = lax.psum(tuple(summed_seq), 'grp')]
    pad x64 -> x0, local copies, waits for them, and re-layouts: 173 us -> none  [the longest x32 87.1 us: local(): lax.associative_scan(chain_combine, (decay_used, inject), axis=0)]
    dot_general x24 -> x0, matrix products: 150 us -> none  [the longest x6 45.8 us: matmul(): return jnp.dot(left, right, preferred_element_type=jnp.float32)]
    all_gather x9 -> x0, blocking collectives: 85 us -> none  [the longest x4 35.3 us: carried_in(): pieces = jax.tree.map(lambda part: lax.all_gather(part, axis), value)]
    add x52 -> x0, other arithmetic: 80 us -> none  [the longest x18 27.5 us: local(): lax.associative_scan(chain_combine, (jnp.flip(decay_next, 0), jnp.flip(gr...]
  transfers between devices with their start and end apart: 18 -> 0, of which waited for: 8 -> 0; matrix products, arithmetic and copies ran while one was open for 29% -> 0% of each run, Pallas kernels for 0% -> 0%
where the time goes in v2:
time: 461 us; the launch traced here: 458 us
  Pallas kernels  434 us (94%)
  other arithmetic  12.1 us (3%)
  local copies, waits for them, and re-layouts  12 us (3%)
    pallas_call x1, Pallas kernels, backward_call(): pl.pallas_call(kernel, out_shape=list(outs.values()) + sums + stages + st...  276 us
    pallas_call x1, Pallas kernels, forward_call(): pl.pallas_call(kernel, out_shape=wholes + [saved[name] for name in names]...  157 us
    convert_element_type x6, other arithmetic, local_fast(): value.astype(jnp.float32)  9.85 us

profile of v2, /device:TPU:0, one launch (start us, length us, event | category | flops | bytes accessed | tf_op | source)
XLA Modules:
  0.0 458.3 jit_solution(4368638794328288893)
XLA Ops:
  0.7 0.7 broadcast_in_dim.16
  1.3 0.7 broadcast_in_dim.17
  2.0 0.7 broadcast_in_dim.18
  2.6 0.7 broadcast_in_dim.19
  3.3 0.7 concatenate.6
  4.0 0.6 dynamic_update_slice.6
  4.6 0.7 convert_dynamic-update-slice_fusion.refs_0_
  5.3 0.0 copy-start.5
  5.3 1.5 pad_maximum_fusion.refs_3_
  6.8 0.0 copy-done.5
  6.8 157.2 %forward.1 = (f32[128,1536]{1,0:T(8,128)}, bf16[1024,1536]{1,0:T(8,128)(2,1)}, bf16[1024,1536]{1,0:T(8,128)(2,1)}, bf16[1536,256]{1,0:T(8,128)(2,1)}, bf16[1536,...) custom-call(s32[4]{0:T(128)} %lengths_ref.3, ...), custom_call_target="tpu_custom_call" | custom-call | tf_op jit(solution)/shard_map/forward/pallas_call | solution.py:872
  164.1 276.3 %backward.1 = (f32[512,1024]{1,0:T(8,128)}, f32[16,1536]{1,0:T(8,128)}, bf16[512,3072]{1,0:T(8,128)(2,1)}, bf16[512,3072]{1,0:T(8,128)(2,1)}, bf16[384,1024]{1,0...) custom-call(s32[4]{0:T(128)} %lengths_ref.3, ...), custom_call_target="tpu_custom_call" | custom-call | tf_op jit(solution)/shard_map/backward/pallas_call | solution.py:1300
  440.4 0.0 copy-start.4
  440.4 0.8 constant_dynamic-slice_fusion
  441.2 0.5 slice_bitcast_fusion
  441.7 0.0 copy-start.3
  441.7 2.0 convert_element_type.29
  443.7 2.0 convert_element_type.30
  445.7 1.4 dynamic-slice_bitcast_fusion
  447.0 1.5 fusion
  448.6 0.0 copy-start.2
  448.6 1.6 fusion.1
  450.1 2.0 convert_element_type.32
  452.1 0.0 copy-done.4
  452.1 0.0 copy-start.1
  452.1 1.3 convert_element_type.33
  453.4 0.0 copy-done.3
  453.4 0.0 copy-start
  453.4 1.3 convert_element_type.34
  454.7 0.0 copy-done.2
  454.7 1.3 convert_element_type.35
  456.0 0.0 copy-done.1
  456.0 1.0 copy.39
  457.0 0.0 copy-done
  457.0 1.3 copy.40
  (2 shorter events, 0.0 us)
Async XLA Ops:
  5.3 1.5 copy-start.5
  440.4 11.7 %copy-start.4 = (bf16[128,3072]{1,0:T(8,128)(2,1)S(1)}, bf16[128,3072]{1,0:T(8,128)(2,1)}, u32[]{:S(2)}) copy-start(bf16[128,3072]{1,0:T(8,128)(2,1)} %get-tuple-element.78) | copy-start | bytes 2359300
  441.7 11.7 %copy-start.3 = (bf16[128,3072]{1,0:T(8,128)(2,1)S(1)}, bf16[128,3072]{1,0:T(8,128)(2,1)}, u32[]{:S(2)}) copy-start(bf16[128,3072]{1,0:T(8,128)(2,1)} %get-tuple-element.79) | copy-start | bytes 2359300
  448.6 6.1 %copy-start.2 = (bf16[384,1024]{1,0:T(8,128)(2,1)S(1)}, bf16[384,1024]{1,0:T(8,128)(2,1)}, u32[]{:S(2)}) copy-start(bf16[384,1024]{1,0:T(8,128)(2,1)} %get-tuple-element.80) | copy-start | bytes 2359300
  452.1 3.9 copy-start.1
  453.4 3.6 copy-start

commit v3 on v2

--- a/solution.py
+++ b/solution.py
@@ -141,8 +141,8 @@
 
 
 class Gather:
-    def __init__(self, place, shards, fulls, kinds, send, recv, own):
-        self.p, self.shards, self.fulls = place, shards, fulls
+    def __init__(self, place, shards, fulls, kinds, send, recv, own, bounce):
+        self.p, self.shards, self.fulls, self.bounce = place, shards, fulls, bounce
         self.send, self.recv, self.own = send, recv, own
         even = place.z % 2 == 0
         odd = place.z % 2 == 1
@@ -192,8 +192,10 @@
     def own_near(self, i):
         return self.copy(i, "os", "SO", self.p.sib, self.part(i, "O"), self.shards[i])
 
-    def own_kept(self, i):
-        return pltpu.make_async_copy(self.shards[i], self.fulls[i].at[self.part(i, "O")], self.own.at[i])
+    def own_kept(self, i, leg):
+        if leg == 0:
+            return pltpu.make_async_copy(self.shards[i], self.bounce[i], self.own.at[i, 0])
+        return pltpu.make_async_copy(self.bounce[i], self.fulls[i].at[self.part(i, "O")], self.own.at[i, 1])
 
     def start(self, i):
         def far():
@@ -202,7 +204,7 @@
 
         when(self.fetch[i], far)
         self.own_near(i).start()
-        self.own_kept(i).start()
+        self.own_kept(i, 0).start()
 
     def onward_far(self, i, name):
         p = self.p
@@ -230,11 +232,14 @@
             if name in ("X", "Y") or self.shared[i]:
                 when(self.fetch[i], far)
             self.onward_near(i, name).start()
+            if name == "X":
+                self.own_kept(i, 0).wait()
+                self.own_kept(i, 1).start()
 
     def arrive(self, i):
         for name in ("SO", "SX", "SY", "S1", "S2"):
             self.wait(i, name)
-        self.own_kept(i).wait()
+        self.own_kept(i, 1).wait()
 
     def drain(self, i):
         self.own_near(i).wait_send()
@@ -254,8 +259,8 @@
         return [self.p.sib, self.p.xnb, self.p.ynb, self.znb]
 
 
-def rows_loop(total, body, step=16):
-    @pl.loop(0, total // step)
+def rows_loop(total, body, step=16, start=0):
+    @pl.loop(start // step, total // step)
     def _(k):
         body(pl.ds(pl.multiple_of(k * step, step), step))
 
@@ -269,147 +274,144 @@
         self.slots = slots
         self.send, self.recv = sems
         z = place.z
-        self.inner = (z == 1) | (z == 2)
+        inner = (z == 1) | (z == 2)
+        self.inner = inner
         self.outer = (z == 0) | (z == 3)
-        self.mine = jnp.where(z == 2, 1, 0)
-        self.peer = place.level(jnp.where(self.inner, 3 - z, z))
+        self.peer = place.level(jnp.where(inner, 3 - z, z))
         self.out = place.level(jnp.where(z < 2, 1 - z, 5 - z))
         self.me = 2 * place.y + place.x
+
+    def makes(self, h):
+        return self.p.z == 1 + h
+
+    def helps(self, h):
+        return self.p.z == 2 - h
 
     def copy(self, i, tag, src, dst, peer):
         return pltpu.make_async_remote_copy(
             src_ref=src, dst_ref=dst, send_sem=self.send.at[i, tag], recv_sem=self.recv.at[i, tag], device_id=peer, device_id_type=MESH
         )
 
-    def to_sib(self, i):
+    def first(self, i, h):
+        p, s = self.p, self.slots[i]
+        if h == 0:
+            return [self.copy(i, q, s.ab.at[0, 2 * q + 1 - p.x], s.fr.at[0, q], p.xnb) for q in range(2)]
+        return [self.copy(i, 2 + q, s.ab.at[1, 2 * (1 - p.y) + q], s.fr.at[1, q], p.ynb) for q in range(2)]
+
+    def second(self, i, h):
+        p, s = self.p, self.slots[i]
+        if h == 0:
+            return self.copy(i, 4, s.ab.at[0, 2 * (1 - p.y) + p.x], s.se.at[0], p.ynb)
+        return self.copy(i, 5, s.ab.at[1, 2 * p.y + 1 - p.x], s.se.at[1], p.xnb)
+
+    def up(self, i, h):
         s = self.slots[i]
-        return self.copy(i, 0, s.stage, s.landed, self.p.sib)
-
-    def first(self, i):
+        return self.copy(i, 6 + h, s.ab.at[h, self.me], s.zo.at[h], self.out)
+
+    def across(self, i, h):
+        s = self.slots[i]
+        return self.copy(i, 8 + h, s.ab.at[h, self.me], s.zp, self.peer)
+
+    def down(self, i, h):
+        res = self.slots[i].res.at[h]
+        return self.copy(i, 10 + h, res, res, self.out)
+
+    def over(self, i, h):
+        res = self.slots[i].res.at[h]
+        return self.copy(i, 12 + h, res, res, self.peer)
+
+    def start_first(self, i, h):
+        for cp in self.first(i, h):
+            cp.start()
+
+    def add_first(self, i, h):
         p, s = self.p, self.slots[i]
-        return [
-            self.copy(i, 4, s.ab.at[0, 1 - p.x], s.xr.at[0], p.xnb),
-            self.copy(i, 5, s.ab.at[0, 2 + 1 - p.x], s.xr.at[1], p.xnb),
-            self.copy(i, 6, s.ab.at[1, 2 * (1 - p.y)], s.yr.at[0], p.ynb),
-            self.copy(i, 7, s.ab.at[1, 2 * (1 - p.y) + 1], s.yr.at[1], p.ynb),
-        ]
-
-    def second(self, i):
-        p, s = self.p, self.slots[i]
-        return [
-            self.copy(i, 8, s.ab.at[0, 2 * (1 - p.y) + p.x], s.yr2, p.ynb),
-            self.copy(i, 9, s.ab.at[1, 2 * p.y + 1 - p.x], s.xr2, p.xnb),
-        ]
-
-    def start_first(self, i):
-        for cp in self.first(i):
-            cp.start()
-
-    def add_first(self, i):
-        p, s = self.p, self.slots[i]
-        for cp in self.first(i):
+        for cp in self.first(i, h):
             cp.wait_recv()
         for q in range(2):
-            ja, jb = 2 * q + p.x, 2 * p.y + q
-
-            def body(rows, q=q, ja=ja, jb=jb):
-                s.ab[0, ja, rows, :] = low(wide(s.ab[0, ja, rows, :]) + wide(s.xr[q, rows, :]))
-                s.ab[1, jb, rows, :] = low(wide(s.ab[1, jb, rows, :]) + wide(s.yr[q, rows, :]))
+            j = 2 * q + p.x if h == 0 else 2 * p.y + q
+
+            def body(rows, q=q, j=j):
+                s.ab[h, j, rows, :] = low(wide(s.ab[h, j, rows, :]) + wide(s.fr[h, q, rows, :]))
 
             rows_loop(s.n, body)
-        for cp in self.second(i):
-            cp.start()
-
-    def up(self, i):
-        s = self.slots[i]
-        return [self.copy(i, 10 + k, s.ab.at[k, self.me], s.zo.at[k], self.out) for k in range(2)]
-
-    def across(self, i):
-        s = self.slots[i]
-        return self.copy(i, 12, s.ab.at[1 - self.mine, self.me], s.zp, self.peer)
-
-    def total_out(self, i):
-        res = self.slots[i].res.at[self.mine]
-        return [self.copy(i, 13, res, res, self.out), self.copy(i, 14, res, res, self.peer)]
-
-    def total_on(self, i):
-        res = self.slots[i].res.at[1 - self.mine]
-        return self.copy(i, 15, res, res, self.out)
-
-    def add_second(self, i):
+        self.second(i, h).start()
+
+    def add_second(self, i, h):
         s, me = self.slots[i], self.me
-        for cp in self.second(i):
-            cp.wait_recv()
+        self.second(i, h).wait_recv()
 
         def body(rows):
-            s.ab[0, me, rows, :] = low(wide(s.ab[0, me, rows, :]) + wide(s.yr2[rows, :]))
-            s.ab[1, me, rows, :] = low(wide(s.ab[1, me, rows, :]) + wide(s.xr2[rows, :]))
+            s.ab[h, me, rows, :] = low(wide(s.ab[h, me, rows, :]) + wide(s.se[h, rows, :]))
 
         rows_loop(s.n, body)
 
         @pl.when(self.outer)
         def _():
-            for cp in self.up(i):
-                cp.start()
-
-    def add_outer(self, i):
+            self.up(i, h).start()
+
+    def add_outer(self, i, h):
         s, me = self.slots[i], self.me
 
         @pl.when(self.inner)
         def _():
-            for cp in self.up(i):
-                cp.wait_recv()
+            self.up(i, h).wait_recv()
 
             def body(rows):
-                for k in range(2):
-                    s.ab[k, me, rows, :] = low(wide(s.ab[k, me, rows, :]) + wide(s.zo[k, rows, :]))
+                s.ab[h, me, rows, :] = low(wide(s.ab[h, me, rows, :]) + wide(s.zo[h, rows, :]))
 
             rows_loop(s.n, body)
-            self.across(i).start()
-
-    def add_peer(self, i):
-        s, me, mine = self.slots[i], self.me, self.mine
-
-        @pl.when(self.inner)
+
+        @pl.when(self.helps(h))
         def _():
-            self.across(i).wait_recv()
+            self.across(i, h).start()
+
+    def add_peer(self, i, h):
+        s, me = self.slots[i], self.me
+
+        @pl.when(self.makes(h))
+        def _():
+            self.across(i, h).wait_recv()
 
             def body(rows):
-                s.res[mine, rows, :] = low(wide(s.ab[mine, me, rows, :]) + wide(s.zp[rows, :]))
+                s.res[h, rows, :] = low(wide(s.ab[h, me, rows, :]) + wide(s.zp[rows, :]))
 
             rows_loop(s.n, body)
-            for cp in self.total_out(i):
-                cp.start()
-
-    def pass_on(self, i):
-        @pl.when(self.inner)
+            self.down(i, h).start()
+            self.over(i, h).start()
+
+    def pass_on(self, i, h):
+        @pl.when(self.helps(h))
         def _():
-            other = self.slots[i].res.at[1 - self.mine]
-            self.copy(i, 14, other, other, self.peer).wait_recv()
-            self.total_on(i).start()
-
-    def arrive(self, i):
-        res = self.slots[i].res
-
+            self.over(i, h).wait_recv()
+            self.down(i, h).start()
+
+    def arrive(self, i, h):
         @pl.when(self.outer)
         def _():
-            near = jnp.where(self.p.z == 3, 1, 0)
-            self.copy(i, 13, res.at[near], res.at[near], self.out).wait_recv()
-            self.copy(i, 15, res.at[1 - near], res.at[1 - near], self.out).wait_recv()
+            self.down(i, h).wait_recv()
 
     def drain(self, i):
-        @pl.when(self.outer)
-        def _():
-            for cp in self.up(i):
+        for h in range(2):
+
+            @pl.when(self.outer)
+            def _(h=h):
+                self.up(i, h).wait_send()
+
+            @pl.when(self.inner)
+            def _(h=h):
+                self.down(i, h).wait_send()
+
+            @pl.when(self.makes(h))
+            def _(h=h):
+                self.over(i, h).wait_send()
+
+            @pl.when(self.helps(h))
+            def _(h=h):
+                self.across(i, h).wait_send()
+
+            for cp in self.first(i, h) + [self.second(i, h)]:
                 cp.wait_send()
-
-        @pl.when(self.inner)
-        def _():
-            for cp in [self.across(i), self.total_on(i)] + self.total_out(i):
-                cp.wait_send()
-
-        for cp in [self.to_sib(i)] + self.first(i) + self.second(i):
-            cp.wait_send()
 
 
 class Small:
@@ -463,10 +465,6 @@
     return v * half, half + 0.5 * v * (1.0 - t * t) * (ROOT * (1.0 + 3.0 * CUBE * square))
 
 
-def gelu_value(v):
-    return 0.5 * v * (1.0 + jnp.tanh(ROOT * (v + CUBE * v * (v * v))))
-
-
 def dot(left, right):
     return jnp.dot(left, right, preferred_element_type=jnp.float32)
 
@@ -488,7 +486,7 @@
     return jnp.maximum(-v, 0.0) + jnp.log1p(jnp.exp(-jnp.abs(v)))
 
 
-def strided_scan(decay_ref, value_ref, prod_ref, sum_ref, backward, rows):
+def strided_scan(decay_ref, value_ref, prod_ref, sum_ref, backward, rows, between):
     tiles, _, lanes = sum_ref.shape
     span = rows // 8
 
@@ -514,7 +512,9 @@
 
     ones = [jnp.ones((8, lanes), jnp.float32)] * tiles
     zeros = [jnp.zeros((8, lanes), jnp.float32)] * tiles
-    return lax.fori_loop(0, span, step, (ones, zeros), unroll=2)
+    half = lax.fori_loop(0, span // 2, step, (ones, zeros), unroll=2)
+    between()
+    return lax.fori_loop(span // 2, span, step, half, unroll=2)
 
 
 def segment_ends(ends, backward):
@@ -598,11 +598,13 @@
         n1t=shape((width, rows), bf),
         pre=shape((tiles, rows, LANES), f32),
         lin=shape((tiles, rows + 8, LANES), f32),
-        conv=shape((tiles, rows, LANES), bf),
         convt=shape((tiles, LANES, rows), bf),
-        rgate=shape((tiles, rows, LANES), f32),
-        igate=shape((tiles, rows, LANES), f32),
-        state=shape((tiles, rows + 8, LANES), f32),
+        decay=shape((tiles, rows, LANES), f32),
+        k2=shape((tiles, rows, LANES), f32),
+        k3=shape((tiles, rows, LANES), f32),
+        k6=shape((tiles, rows, LANES), f32),
+        k7=shape((tiles, rows, LANES), f32),
+        slope=shape((tiles, rows, LANES), f32),
         rect=shape((lru, rows), bf),
         resid=shape((rows, width), f32),
         n2t=shape((width, rows), bf),
@@ -619,12 +621,13 @@
         small=pltpu.VMEM((16, lru), f32),
         pre=pltpu.VMEM((tiles, rows, LANES), f32),
         lin=pltpu.VMEM((tiles, rows + 8, LANES), f32),
-        conv=pltpu.VMEM((tiles, rows, LANES), bf),
         convt=pltpu.VMEM((tiles, LANES, rows), bf),
-        rgate=pltpu.VMEM((tiles, rows, LANES), f32),
-        igate=pltpu.VMEM((tiles, rows, LANES), f32),
+        decay=pltpu.VMEM((tiles, rows, LANES), f32),
+        k2=pltpu.VMEM((tiles, rows, LANES), f32),
+        k3=pltpu.VMEM((tiles, rows, LANES), f32),
+        k6=pltpu.VMEM((tiles, rows, LANES), f32),
+        k7=pltpu.VMEM((tiles, rows, LANES), f32),
         prod=pltpu.VMEM((tiles, rows, LANES), f32),
-        state=pltpu.VMEM((tiles, rows + 8, LANES), f32),
         total=pltpu.VMEM((tiles, rows, LANES), f32),
         rec=pltpu.VMEM((rows, lru), bf),
         rect=pltpu.VMEM((lru, rows), bf),
@@ -635,7 +638,7 @@
         ends=pltpu.VMEM((8, 2, tiles, LANES), f32),
         gsend=pltpu.SemaphoreType.DMA((count, len(SENT))),
         grecv=pltpu.SemaphoreType.DMA((count, len(GOT))),
-        gown=pltpu.SemaphoreType.DMA((count,)),
+        gown=pltpu.SemaphoreType.DMA((count, 2)),
         esend=pltpu.SemaphoreType.DMA((7,)),
         erecv=pltpu.SemaphoreType.DMA((7,)),
         hsend=pltpu.SemaphoreType.DMA(()),
@@ -649,10 +652,11 @@
     def kernel(lengths_ref, tokens_ref, *refs):
         ins, outs = refs[:count], refs[count : 2 * count]
         out = named(names, refs[2 * count : 2 * count + len(names)])
-        v = named(keys, refs[2 * count + len(names) :])
+        bounce = refs[-count:]
+        v = named(keys, refs[2 * count + len(names) : -count])
         gelu_w, input_w, gates_w, output_w, mgate_w, mvalue_w, mdown_w = outs[1:]
         place = Place()
-        gather = Gather(place, ins, outs, kinds, v.gsend, v.grecv, v.gown)
+        gather = Gather(place, ins, outs, kinds, v.gsend, v.grecv, v.gown, bounce)
         ends = Ends(place, v.ends, (v.esend, v.erecv), False)
         z, seq = place.z, place.seq
         meet([(z, (seq + d) % 8) for d in range(1, 8)])
@@ -715,7 +719,6 @@
             pltpu.emit_pipeline(body, grid=(tiles // 2,), in_specs=[pl.BlockSpec((width, 2 * LANES), lambda t: (0, t))])(weight)
 
         project(gelu_w, v.pre, 0)
-        keep(v.pre, out.pre)
         gather.relay(4, ("X", "Y"))
         gather.start(6)
         gather.relay(3, ("D1", "D2"))
@@ -758,23 +761,30 @@
                 for k in range(1, 4):
                     acc = acc + taps[k] * v.lin[h, 8 + r - k : 8 + r - k + R, :]
                 cl = low(acc)
-                v.conv[h, r : r + R, :] = cl
                 v.convt[h, :, r : r + R] = cl.T
                 both = dot(cl, w[...])
                 rg = sigmoid(both[:, :LANES] + rb)
                 ig = sigmoid(both[:, LANES:] + ib)
-                v.rgate[h, r : r + R, :] = rg
-                v.igate[h, r : r + R, :] = ig
                 log_decay = rate * rg
-                v.prod[h, r : r + R, :] = jnp.exp(log_decay)
-                v.total[h, r : r + R, :] = jnp.sqrt(minus_expm1(2.0 * log_decay, log_decay)) * ig * wide(cl)
+                decay = jnp.exp(log_decay)
+                mult = jnp.sqrt(minus_expm1(2.0 * log_decay, log_decay))
+                cv = wide(cl)
+                through = mult * ig
+                at = slice(r, r + R)
+                v.prod[h, at, :] = decay
+                v.decay[h, at, :] = decay
+                v.total[h, at, :] = through * cv
+                v.k3[h, at, :] = through
+                v.k2[h, at, :] = through * cv * (1.0 - ig)
+                v.k6[h, at, :] = ig * cv * (decay * decay) / mult
+                v.k7[h, at, :] = rg
 
         pltpu.emit_pipeline(gates, grid=(tiles,), in_specs=[pl.BlockSpec((LANES, 2 * LANES), lambda h: (h, 0))])(gates_w)
-        for src, dst in ((v.conv, out.conv), (v.convt, out.convt), (v.rgate, out.rgate), (v.igate, out.igate)):
+        for src, dst in ((v.convt, out.convt), (v.decay, out.decay), (v.k2, out.k2), (v.k3, out.k3)):
             keep(src, dst)
         gather.relay(6, ("X", "Y"))
         gather.relay(5, ("D1", "D2"))
-        tails = strided_scan(v.prod, v.total, v.prod, v.total, False, rows)
+        tails = strided_scan(v.prod, v.total, v.prod, v.total, False, rows, lambda: None)
         before, whole = segment_ends(tails, False)
         ends.tell(whole)
         gather.relay(7, ("X", "Y"))
@@ -782,7 +792,6 @@
         carry = ends.joined()
         span = rows // 8
         for c in range(tiles):
-            v.state[c, 0:8, :] = jnp.broadcast_to(carry[c : c + 1, :], (8, LANES))
             into = before[c][0] * carry[c : c + 1, :] + before[c][1]
             v.parts[8 * c : 8 * c + 8, 0:LANES] = into
 
@@ -790,14 +799,24 @@
         def _(c):
             lane = pl.ds(pl.multiple_of(c * LANES, LANES), LANES)
             into = v.parts[pl.ds(pl.multiple_of(c * 8, 8), 8), 0:LANES]
+            rate = -cfactor * softplus_minus(small[7:8, lane])
+            first = lax.broadcasted_iota(jnp.int32, (span, LANES), 0) == 0
             for s in range(8):
                 at = slice(s * span, (s + 1) * span)
                 state = v.total[c, at, :] + v.prod[c, at, :] * into[s : s + 1, :]
-                v.state[c, 8 + s * span : 8 + (s + 1) * span, :] = state
-                v.rec[at, lane] = low(state * gelu_value(v.pre[c, at, :]))
+                before_it = jnp.where(first, into[s : s + 1, :], pltpu.roll(state, 1, axis=0))
+                rg = v.k7[c, at, :]
+                k7 = (before_it * v.decay[c, at, :] - v.k6[c, at, :]) * rg
+                v.k7[c, at, :] = k7
+                v.k6[c, at, :] = k7 * rate * (1.0 - rg)
+                value, slope = gelu_parts(v.pre[c, at, :])
+                v.rec[at, lane] = low(state * value)
+                v.pre[c, at, :] = value
+                v.total[c, at, :] = state * slope
             v.rect[lane, :] = v.rec[:, lane].T
 
-        keep(v.state, out.state)
+        for src, dst in ((v.k6, out.k6), (v.k7, out.k7), (v.pre, out.pre), (v.total, out.slope)):
+            keep(src, dst)
         keep(v.rect, out.rect)
         gather.arrive(4)
 
@@ -808,8 +827,6 @@
 
         pltpu.emit_pipeline(back_to_width, grid=(width // 256,), in_specs=[pl.BlockSpec((lru, 256), lambda t: (0, t))])(output_w)
         keep(v.resid, out.resid)
-        gather.relay(7, ("D1", "D2"))
-
         def norm_two(at):
             x = v.resid[at, :]
             scale = lax.rsqrt(jnp.mean(x * x, axis=-1, keepdims=True) + epsilon)
@@ -832,7 +849,11 @@
             mv[...] = dot(v.n2[...], wv[...])
 
             def act(rs):
-                v.hidden[rs, at] = low(gelu_value(mg[rs, :]) * mv[rs, :])
+                value, slope = gelu_parts(mg[rs, :])
+                linear = mv[rs, :]
+                v.hidden[rs, at] = low(value * linear)
+                mg[rs, :] = value
+                mv[rs, :] = linear * slope
 
             rows_loop(rows, act, 64)
             hidt[...] = v.hidden[:, at].T
@@ -844,6 +865,7 @@
             in_specs=[wide_tile, wide_tile],
             out_specs=[pl.BlockSpec((rows, 256), lambda t: (0, t))] * 2 + [pl.BlockSpec((256, rows), lambda t: (t, 0))],
         )(mgate_w, mvalue_w, out.mg, out.mv, out.hidt)
+        gather.relay(7, ("D1", "D2"))
         gather.arrive(7)
         valid_rows = lengths_ref[z] - seq * rows
 
@@ -874,7 +896,7 @@
         out_shape=wholes + [saved[name] for name in names],
         in_specs=[pl.BlockSpec(memory_space=pltpu.SMEM), HBM] + [HBM] * count,
         out_specs=[HBM] * (count + len(names)),
-        scratch_shapes=[scratch[key] for key in keys],
+        scratch_shapes=[scratch[key] for key in keys] + [pltpu.VMEM(s.shape, s.dtype) for s in shards],
         compiler_params=pltpu.CompilerParams(collective_id=1, has_side_effects=True, vmem_limit_bytes=60 << 20),
         name="forward",
     )(lengths, tokens, *shards)
@@ -885,14 +907,71 @@
     bf = jnp.bfloat16
     return dict(
         ab=pltpu.VMEM((2, 4, n, h), bf),
-        xr=pltpu.VMEM((2, n, h), bf),
-        yr=pltpu.VMEM((2, n, h), bf),
-        yr2=pltpu.VMEM((n, h), bf),
-        xr2=pltpu.VMEM((n, h), bf),
+        fr=pltpu.VMEM((2, 2, n, h), bf),
+        se=pltpu.VMEM((2, n, h), bf),
         zo=pltpu.VMEM((2, n, h), bf),
         zp=pltpu.VMEM((n, h), bf),
         res=pltpu.VMEM((2, n, h), bf),
     )
+
+
+PUMPS = (
+    (),
+    (),
+    (),
+    (),
+    (),
+    (),
+    ((6, 0, 0),),
+    ((6, 0, 1),),
+    (),
+    (),
+    (),
+    (),
+    (),
+    ((6, 1, 0),),
+    ((6, 2, 1),),
+    (),
+    (),
+    (),
+    ((0, 0, 0), (0, 0, 1),),
+    (),
+    (),
+    (),
+    (),
+    (),
+    ((0, 1, 0), (6, 2, 0), (0, 2, 1),),
+    (),
+    (),
+    ((1, 0, 1),),
+    ((1, 0, 0), (6, 1, 1),),
+    (),
+    (),
+    (),
+    ((2, 0, 1), (1, 1, 0),),
+    ((0, 2, 0), (6, 3, 0), (2, 0, 0),),
+    (),
+    (),
+    ((3, 0, 1),),
+    ((1, 2, 1),),
+    ((2, 1, 0), (6, 3, 1), (0, 1, 1), (3, 0, 0),),
+    ((0, 3, 0),),
+    ((6, 4, 0),),
+    ((1, 2, 0), (2, 2, 1),),
+    ((4, 0, 1),),
+    ((6, 4, 1),),
+    ((4, 0, 0), (1, 1, 1), (0, 3, 1),),
+    ((3, 1, 0), (2, 2, 0), (1, 3, 0),),
+    ((3, 2, 1), (6, 6, 0), (6, 6, 1), (0, 4, 0),),
+    (),
+    (),
+    ((2, 1, 1), (1, 3, 1), (0, 6, 0), (0, 4, 1), (0, 6, 1), (4, 1, 0), (3, 2, 0), (2, 3, 0),),
+    ((1, 4, 0), (1, 6, 0),),
+    ((2, 3, 1), (6, 5, 0), (1, 4, 1), (1, 6, 1),),
+    ((6, 5, 1),),
+    ((4, 2, 1), (3, 1, 1),),
+    ((2, 4, 0), (2, 6, 0), (3, 3, 0), (2, 4, 1), (2, 6, 1), (0, 5, 0), (4, 2, 0), (0, 5, 1), (3, 3, 1), (4, 1, 1), (1, 5, 0), (1, 5, 1), (4, 3, 0), (3, 4, 0), (3, 6, 0), (2, 5, 0), (3, 4, 1), (3, 6, 1), (4, 3, 1), (2, 5, 1), (4, 4, 0), (3, 5, 0), (4, 6, 0), (4, 4, 1), (3, 5, 1), (4, 6, 1), (4, 5, 0), (4, 5, 1), (5, 0, 0), (5, 0, 1), (5, 1, 0), (5, 2, 0), (5, 2, 1), (5, 3, 0), (5, 1, 1), (5, 4, 0), (5, 6, 0), (5, 3, 1), (5, 5, 0), (5, 4, 1), (5, 6, 1), (5, 5, 1),),
+)
 
 
 def backward_call(lengths, tokens, cotangent, weights, saved):
@@ -900,62 +979,58 @@
     gelu_full, input_full, gates_full, output_full, mgate_full, mvalue_full, mdown_full = weights
     lru, ff = gelu_full.shape[1], mgate_full.shape[1]
     tiles = lru // LANES
+    wide_tile = 2 * LANES
     f32, bf = jnp.float32, jnp.bfloat16
     shape = jax.ShapeDtypeStruct
     DOWN, MGATE, MVALUE, OUTPUT, GELU, INPUT, GATES = range(7)
     full = [mdown_full, mgate_full, mvalue_full, output_full, gelu_full, input_full, gates_full]
     extents = [w.shape for w in full]
-    tile_of = [256, 512, 512, 256, 256, 256, None]
     count = len(full)
     split = lambda v: v.reshape(4, 2, v.shape[0] // 8, v.shape[1])
     inputs = dict(
         tokens=tokens, cot=cotangent, gelu_w=gelu_full, input_w=input_full, gates_w=gates_full, output_w=output_full, mgate_w=mgate_full,
-        mvalue_w=mvalue_full, mdown_w=mdown_full, small=saved.small, n1t=split(saved.n1t), pre=saved.pre, lin=saved.lin, conv=saved.conv,
-        convt=saved.convt, rgate=saved.rgate, igate=saved.igate, state=saved.state, rect=split(saved.rect), resid=saved.resid,
-        n2t=split(saved.n2t), mg=saved.mg, mv=saved.mv, hidt=split(saved.hidt),
+        mvalue_w=mvalue_full, mdown_w=mdown_full, small=saved.small, n1t=split(saved.n1t), pre=saved.pre, lin=saved.lin,
+        convt=saved.convt, decay=saved.decay, k6=saved.k6, k2=saved.k2, k3=saved.k3, k7=saved.k7, slope=saved.slope,
+        rect=split(saved.rect), resid=saved.resid, n2t=split(saved.n2t), mg=saved.mg, mv=saved.mv, hidt=split(saved.hidt),
     )
     slot_keys = list(slot_scratch(8, 256))
+    most = max(4 * (r // 8) * (c // 2) // wide_tile for r, c in extents)
+    passes = 13
     scratch = dict(
         go=pltpu.VMEM((rows, width), bf),
         gm=pltpu.VMEM((rows, width), bf),
         gn=pltpu.VMEM((rows, width), f32),
-        x=pltpu.VMEM((rows, width), bf),
-        resid=pltpu.VMEM((rows, width), f32),
-        gh=pltpu.VMEM((rows, 256), f32),
+        n1t=pltpu.VMEM((4, 2, width // 8, rows), bf),
+        n2t=pltpu.VMEM((4, 2, width // 8, rows), bf),
+        rect=pltpu.VMEM((4, 2, lru // 8, rows), bf),
         small=pltpu.VMEM((16, lru), f32),
         part=pltpu.VMEM((16, lru), f32),
         gain=pltpu.VMEM((8, width), f32),
-        adj=pltpu.VMEM((tiles, rows + 8, LANES), f32),
-        prod=pltpu.VMEM((tiles, rows, LANES), f32),
         into=pltpu.VMEM((tiles, 8, LANES), f32),
-        gg=pltpu.VMEM((rows, lru), bf),
-        gl=pltpu.VMEM((rows, lru), bf),
-        gri=pltpu.VMEM((rows, 2 * LANES), bf),
-        direct=pltpu.VMEM((rows, LANES), f32),
-        gstage=pltpu.VMEM((4, 2, lru // 8, 2 * LANES), bf),
-        glanded=pltpu.VMEM((4, lru // 8, 2 * LANES), bf),
+        halo=pltpu.VMEM((tiles, 8, LANES), f32),
+        edge=pltpu.VMEM((tiles, 8, LANES), f32),
+        stage=pltpu.VMEM((2, most, wide_tile), bf),
+        landed=pltpu.VMEM((2, most, wide_tile), bf),
+        gstage=pltpu.VMEM((4, 2, lru // 8, wide_tile), bf),
         ends=pltpu.VMEM((8, 2, tiles, LANES), f32),
         sslots=pltpu.VMEM((2, 5, 16, lru), f32),
-        rsend=pltpu.SemaphoreType.DMA((count, 16)),
-        rrecv=pltpu.SemaphoreType.DMA((count, 16)),
+        psend=pltpu.SemaphoreType.DMA((passes,)),
+        precv=pltpu.SemaphoreType.DMA((passes,)),
+        rsend=pltpu.SemaphoreType.DMA((count, 14)),
+        rrecv=pltpu.SemaphoreType.DMA((count, 14)),
         esend=pltpu.SemaphoreType.DMA((7,)),
         erecv=pltpu.SemaphoreType.DMA((7,)),
         hsend=pltpu.SemaphoreType.DMA(()),
         hrecv=pltpu.SemaphoreType.DMA(()),
         ssend=pltpu.SemaphoreType.DMA((5,)),
         srecv=pltpu.SemaphoreType.DMA((5,)),
-        load=pltpu.SemaphoreType.DMA((4,)),
+        load=pltpu.SemaphoreType.DMA((8,)),
         keep=pltpu.SemaphoreType.DMA((count + 1, 2)),
+        credit=pltpu.SemaphoreType.REGULAR,
     )
     keys = list(scratch)
-    outs = dict(
-        tokens_grad=shape((rows, width), f32),
-        small_sum=shape((16, lru), f32),
-        gmg=shape((rows, ff), bf),
-        gmv=shape((rows, ff), bf),
-    )
+    outs = dict(tokens_grad=shape((rows, width), f32), small_sum=shape((16, lru), f32))
     out_keys = list(outs)
-    stages = [shape((4, r // 8, c), bf) for r, c in extents[:-1]]
     sums = [shape((r // 8, c), bf) for r, c in extents]
 
     def kernel(lengths_ref, *refs):
@@ -969,344 +1044,461 @@
         w = named(inputs, take(len(inputs)))
         out = named(out_keys, take(len(out_keys)))
         sum_refs = take(count)
-        staged, landed = take(count - 1), take(count - 1)
         v = named(keys, take(len(keys)))
         slots = []
         for i, (r, c) in enumerate(extents):
             s = named(slot_keys, take(len(slot_keys)))
-            s.n, s.h, s.columns, s.tile = r // 8, c // 2, c, tile_of[i]
+            s.n, s.h, s.tiles = r // 8, c // 2, c // 2 // wide_tile
             slots.append(s)
         place = Place()
         z, seq, core = place.z, place.seq, place.core
-        for i in range(count - 1):
-            slots[i].stage, slots[i].landed = staged[i], landed[i]
-        slots[GATES].stage, slots[GATES].landed = v.gstage.at[:, 1 - core], v.glanded
         red = Reduce(place, slots, (v.rsend, v.rrecv))
         ends = Ends(place, v.ends, (v.esend, v.erecv), True)
         tot = Small(place, v.part, v.sslots, (v.ssend, v.srecv))
-        loads = [
-            pltpu.make_async_copy(w.cot, v.go, v.load.at[0]),
-            pltpu.make_async_copy(w.small, v.small, v.load.at[1]),
-            pltpu.make_async_copy(w.resid, v.resid, v.load.at[2]),
-            pltpu.make_async_copy(w.tokens, v.x, v.load.at[3]),
-        ]
-        for cp in loads:
+        small, part = v.small, v.part
+        kept = []
+
+        def load(src, dst, k):
+            cp = pltpu.make_async_copy(src, dst, v.load.at[k])
             cp.start()
-        meet([(z, (seq + d) % 8) for d in range(1, 8)] + [((z + d) % 4, seq) for d in range(1, 4)])
-        loads[0].wait()
-        valid_rows = lengths_ref[z] - seq * rows
-
-        def mask(at):
-            here = lax.broadcasted_iota(jnp.int32, (64, width), 0) + at.start < valid_rows
-            v.go[at, :] = low(jnp.where(here, wide(v.go[at, :]), 0.0))
-
-        rows_loop(rows, mask, 64)
-
-        def spread(s, left, right):
-            return dot(left[...].reshape(4 * s.n, rows), right).reshape(4, s.n, s.tile)
-
-        def right_of(held, s):
-            t = pl.program_id(0)
-            return held[:, pl.ds(pl.multiple_of(t * s.tile, s.tile), s.tile)]
-
-        def weight_pass(i, left, right, streamed, own):
+            return cp
+
+        first_loads = [load(w.cot, v.go, 0)]
+        loads = [load(w.small, v.small, 1), load(w.n2t, v.n2t, 2), load(w.rect, v.rect, 3), load(w.n1t, v.n1t, 4)]
+
+        def arrived(i, h):
+            red.arrive(i, h)
             s = slots[i]
-            steps = s.columns // s.tile
-            in_specs = [pl.BlockSpec((4, None, s.n, rows), lambda t: (0, core if own else 1 - core, 0, 0))]
-            operands = [left]
-            if streamed:
-                in_specs.append(pl.BlockSpec((rows, s.tile), lambda t: (0, t)))
-                operands.append(right)
-            block = pl.BlockSpec((4, s.n, s.tile), lambda t: (0, 0, t))
-
-            def body(*args):
-                value = spread(s, args[0], args[1][...] if streamed else right_of(right, s))
-                if own:
-                    t = pl.program_id(0)
-                    half = steps // 2
-                    at = pl.ds(pl.multiple_of((t % half) * s.tile, s.tile), s.tile)
-                    s.ab[t // half, :, :, at] = low(value + wide(args[-1][...]))
-                else:
-                    args[-1][...] = low(value)
-
-            if own:
-                red.to_sib(i).wait_recv()
-                pltpu.emit_pipeline(body, grid=(steps,), in_specs=in_specs + [block])(*operands, s.landed)
-                red.start_first(i)
-            else:
-                pltpu.emit_pipeline(body, grid=(steps,), in_specs=in_specs, out_specs=[block])(*operands, s.stage)
-                red.to_sib(i).start()
-
-        weight_pass(DOWN, w.hidt, v.go, False, False)
-
-        def mlp(md, mg, mv, wg, wv, gmg, gmv):
-            v.gh[...] = dot_t(v.go[...], md[...])
-
-            def act(at):
-                value, slope = gelu_parts(mg[at, :])
-                gh = v.gh[at, :]
-                gmg[at, :] = low(gh * mv[at, :] * slope)
-                gmv[at, :] = low(gh * value)
-
-            rows_loop(rows, act, 64)
-            more = dot_t(gmg[...], wg[...]) + dot_t(gmv[...], wv[...])
-
-            @pl.when(pl.program_id(0) == 0)
+            cp = pltpu.make_async_copy(s.res.at[h], sum_refs[i].at[:, pl.ds(side(i, h) * s.h, s.h)], v.keep.at[i, h])
+
+            @pl.when(red.outer)
             def _():
-                v.gn[...] = more
-
-            @pl.when(pl.program_id(0) > 0)
+                cp.start()
+
+        def totalled(i, h):
+            s = slots[i]
+            return pltpu.make_async_copy(s.res.at[h], sum_refs[i].at[:, pl.ds(side(i, h) * s.h, s.h)], v.keep.at[i, h])
+
+        def add_peer(i, h):
+            red.add_peer(i, h)
+            cp = totalled(i, h)
+
+            @pl.when(red.makes(h))
             def _():
-                v.gn[...] += more
-
-        across = pl.BlockSpec((rows, 256), lambda t: (0, t))
-        pltpu.emit_pipeline(
-            mlp,
-            grid=(ff // 256,),
-            in_specs=[pl.BlockSpec((256, width), lambda t: (t, 0)), across, across]
-            + [pl.BlockSpec((width, 256), lambda t: (0, t))] * 2,
-            out_specs=[across, across],
-        )(w.mdown_w, w.mg, w.mv, w.mgate_w, w.mvalue_w, out.gmg, out.gmv)
-        weight_pass(DOWN, w.hidt, v.go, False, True)
-        weight_pass(MGATE, w.n2t, out.gmg, True, False)
-        weight_pass(MVALUE, w.n2t, out.gmv, True, False)
-        for cp in loads[1:]:
-            cp.wait()
-        small, part = v.small, v.part
-        part[...] = jnp.zeros_like(part)
+                cp.start()
+
+        def pass_on(i, h):
+            red.pass_on(i, h)
+            cp = totalled(i, h)
+
+            @pl.when(red.helps(h))
+            def _():
+                cp.start()
+
+        steps = (red.add_first, red.add_second, red.add_outer, add_peer, pass_on, arrived, red.start_first)
+        turn = [0]
+
+        def serve(spot):
+            for step, i, h in PUMPS[spot]:
+                steps[step](i, h)
+
+        def pump():
+            serve(turn[0])
+            turn[0] += 1
+
+        def pumps_at(*grid_steps):
+            spots = list(enumerate(grid_steps, turn[0]))
+            turn[0] += len(spots)
+
+            def at_step():
+                for spot, grid_step in spots:
+                    if PUMPS[spot]:
+                        pl.when(pl.program_id(0) == grid_step)(lambda spot=spot: serve(spot))
+
+            return at_step
+
+        def to_sib(k, used):
+            return pltpu.make_async_remote_copy(
+                src_ref=v.stage.at[k % 2, pl.ds(0, used)], dst_ref=v.landed.at[k % 2, pl.ds(0, used)], send_sem=v.psend.at[k],
+                recv_sem=v.precv.at[k], device_id=place.sib, device_id_type=MESH,
+            )
+
+        sent = {}
+
+        def send_blocks(k, used):
+            if k >= 2:
+                pl.semaphore_wait(v.credit, 1)
+            sent[k] = used
+            to_sib(k, used).start()
+
+        def free_stage(k):
+            if k >= 2:
+                to_sib(k - 2, sent[k - 2]).wait_send()
+
+        def give_credit(k):
+            if k + 2 < passes:
+                pl.semaphore_signal(v.credit, inc=1, device_id=place.sib, device_id_type=MESH)
+
+        def side(i, h):
+            return 1 - h if i == MVALUE else h
+
+        def blocks(s):
+            group = max(1, 512 // s.n)
+            return [(j, group) for j in range(0, 4, group)]
+
+        def for_sib(k, i, h, left, right):
+            pump()
+            s = slots[i]
+            free_stage(k)
+
+            @pl.loop(0, s.tiles)
+            def _(t):
+                r = right[:, pl.ds(pl.multiple_of((side(i, h) * s.tiles + t) * wide_tile, wide_tile), wide_tile)]
+                for j, group in blocks(s):
+                    value = dot(left[j : j + group, 1 - core].reshape(group * s.n, rows), r)
+                    at = pl.ds(pl.multiple_of(t * 4 * s.n + j * s.n, s.n), group * s.n)
+                    v.stage[k % 2, at, :] = low(value)
+
+            send_blocks(k, 4 * s.n * s.tiles)
+
+        def for_us(k, i, h, left, right):
+            pump()
+            s = slots[i]
+            to_sib(k, sent[k]).wait_recv()
+
+            @pl.loop(0, s.tiles)
+            def _(t):
+                r = right[:, pl.ds(pl.multiple_of((side(i, h) * s.tiles + t) * wide_tile, wide_tile), wide_tile)]
+                for j, group in blocks(s):
+                    value = dot(left[j : j + group, core].reshape(group * s.n, rows), r)
+                    at = pl.ds(pl.multiple_of(t * 4 * s.n + j * s.n, s.n), group * s.n)
+                    both = low(value + wide(v.landed[k % 2, at, :]))
+                    lane = pl.ds(pl.multiple_of(t * wide_tile, wide_tile), wide_tile)
+                    s.ab[h, j : j + group, :, lane] = both.reshape(group, s.n, wide_tile)
+
+            give_credit(k)
 
         def eight(value):
             return value.reshape(value.shape[0] // 8, 8, value.shape[1]).sum(axis=0)
 
-        def norm_back(read, gain, write):
-            v.gain[...] = jnp.zeros_like(v.gain)
-
-            def chunk(at):
-                x, grad, add = read(at)
-                scale = lax.rsqrt(jnp.mean(x * x, axis=-1, keepdims=True) + epsilon)
-                v.gain[...] += eight(grad * x * scale)
-                scaled = grad * gain
-                m = jnp.mean(scaled * x, axis=-1, keepdims=True)
-                write(at, add + scale * (scaled - x * (scale * scale * m)))
-
-            rows_loop(rows, chunk, 64)
-            return v.gain[...].sum(axis=0, keepdims=True)
-
-        def keep_resid(at, value):
+        def norm_back(x, grad, gain, add):
+            scale = lax.rsqrt(jnp.mean(x * x, axis=-1, keepdims=True) + epsilon)
+            v.gain[...] += eight(grad * x * scale)
+            scaled = grad * gain
+            m = jnp.mean(scaled * x, axis=-1, keepdims=True)
+            return add + scale * (scaled - x * (scale * scale * m))
+
+        def mlp_half(gmg, gmv, half):
+            pump()
+            steps_half = ff // wide_tile // 2
+            inside = pumps_at(steps_half // 3, 2 * steps_half // 3)
+
+            def body(md, value, slope):
+                inside()
+                t = pl.program_id(0) + half * steps_half
+                at = pl.ds(pl.multiple_of(t * wide_tile, wide_tile), wide_tile)
+                gh = dot_t(v.go[...], md[...])
+                gmg[:, at] = low(gh * slope[...])
+                gmv[:, at] = low(gh * value[...])
+
+            across = pl.BlockSpec((rows, wide_tile), lambda t: (0, t + half * steps_half))
+            pltpu.emit_pipeline(
+                body, grid=(steps_half,), in_specs=[pl.BlockSpec((wide_tile, width), lambda t: (t + half * steps_half, 0)), across, across]
+            )(w.mdown_w, w.mg, w.mv)
+
+        def mlp_norm_half(gmg, gmv, half):
+            pump()
+
+            inside = pumps_at(1)
+
+            def body(wg, wv):
+                inside()
+                t = pl.program_id(0) + 2 * half
+                at = pl.ds(pl.multiple_of(t * wide_tile, wide_tile), wide_tile)
+                v.gn[:, at] = dot_t(gmg[...], wg[...]) + dot_t(gmv[...], wv[...])
+
+            pltpu.emit_pipeline(body, grid=(2,), in_specs=[pl.BlockSpec((wide_tile, ff), lambda t: (t + 2 * half, 0))] * 2)(
+                w.mgate_w, w.mvalue_w
+            )
+
+        def mlp_phase(gmg, gmv):
+            def head(hidt):
+                down_loads = load(w.hidt, hidt, 5)
+                meet([(z, (seq + d) % 8) for d in range(1, 8)] + [((z + d) % 4, seq) for d in range(1, 4)])
+                first_loads[0].wait()
+                valid_rows = lengths_ref[z] - seq * rows
+
+                def mask(at):
+                    here = lax.broadcasted_iota(jnp.int32, (64, width), 0) + at.start < valid_rows
+                    v.go[at, :] = low(jnp.where(here, wide(v.go[at, :]), 0.0))
+
+                rows_loop(rows, mask, 64)
+                part[...] = jnp.zeros_like(part)
+                down_loads.wait()
+                for_sib(0, DOWN, 0, hidt, v.go)
+                for_sib(1, DOWN, 1, hidt, v.go)
+                mlp_half(gmg, gmv, 0)
+                for_us(0, DOWN, 0, hidt, v.go)
+                for_us(1, DOWN, 1, hidt, v.go)
+
+            pl.run_scoped(head, pltpu.VMEM((4, 2, ff // 8, rows), bf))
+            for cp in loads:
+                cp.wait()
+            for_sib(2, MGATE, 0, v.n2t, gmg)
+            for_sib(3, MVALUE, 1, v.n2t, gmv)
+            mlp_half(gmg, gmv, 1)
+            for_us(2, MGATE, 0, v.n2t, gmg)
+            for_us(3, MVALUE, 1, v.n2t, gmv)
+            for_sib(4, MGATE, 1, v.n2t, gmg)
+            for_sib(5, MVALUE, 0, v.n2t, gmv)
+            mlp_norm_half(gmg, gmv, 0)
+            for_us(4, MGATE, 1, v.n2t, gmg)
+            for_us(5, MVALUE, 0, v.n2t, gmv)
+            mlp_norm_half(gmg, gmv, 1)
+
+        pl.run_scoped(mlp_phase, pltpu.VMEM((rows, ff), bf), pltpu.VMEM((rows, ff), bf))
+        pump()
+        v.gain[...] = jnp.zeros_like(v.gain)
+
+        inside = pumps_at(rows // 128)
+
+        def norm_two(resid, inside=inside):
+            inside()
+            at = pl.ds(pl.multiple_of(pl.program_id(0) * 64, 64), 64)
+            value = norm_back(resid[...], v.gn[at, :], small[9:10, :width], wide(v.go[at, :]))
             v.gn[at, :] = value
             v.gm[at, :] = low(value)
 
-        part[9:10, :width] = norm_back(lambda at: (v.resid[at, :], v.gn[at, :], wide(v.go[at, :])), small[9:10, :width], keep_resid)
-        weight_pass(MGATE, w.n2t, out.gmg, True, True)
-        weight_pass(MVALUE, w.n2t, out.gmv, True, True)
-        red.add_first(DOWN)
-
-        weight_pass(OUTPUT, w.rect, v.gm, False, False)
-
-        def into_branch(wo, pre, state, rgate):
-            t = pl.program_id(0)
-            v.gh[...] = dot_t(v.gm[...], wo[...])
-            for q in range(2):
-                c = 2 * t + q
+        pltpu.emit_pipeline(norm_two, grid=(rows // 64,), in_specs=[pl.BlockSpec((64, width), lambda t: (t, 0))])(w.resid)
+        part[9:10, :width] = v.gain[...].sum(axis=0, keepdims=True)
+        tokens_load = load(w.tokens, v.go, 6)
+
+        def branch_phase(adj, prod, gg, gl, gri):
+            decay_load = load(w.decay, prod, 7)
+            for_sib(6, OUTPUT, 0, v.rect, v.gm)
+            for_sib(7, OUTPUT, 1, v.rect, v.gm)
+            pump()
+
+            inside = pumps_at(tiles // 6, tiles // 3)
+
+            def into_branch(wo, value, slope, inside=inside):
+                inside()
+                t = pl.program_id(0)
+                gr = dot_t(v.gm[...], wo[...])
+                for q in range(2):
+                    c = 2 * t + q
+                    grad = gr[:, q * LANES : (q + 1) * LANES]
+                    adj[c, pl.ds(0, rows), :] = grad * value[q]
+                    gg[:, pl.ds(pl.multiple_of(c * LANES, LANES), LANES)] = low(grad * slope[q])
+
+            pair = pl.BlockSpec((2, rows, LANES), lambda t: (t, 0, 0))
+            pltpu.emit_pipeline(
+                into_branch, grid=(tiles // 2,), in_specs=[pl.BlockSpec((wide_tile, width), lambda t: (t, 0)), pair, pair]
+            )(w.output_w, w.pre, w.slope)
+            for_us(6, OUTPUT, 0, v.rect, v.gm)
+            for_us(7, OUTPUT, 1, v.rect, v.gm)
+            pump()
+            decay_load.wait()
+            tails = strided_scan(prod, adj, prod, adj, True, rows, pump)
+            before, whole = segment_ends(tails, True)
+            ends.tell(whole)
+            for c in range(tiles):
+                v.into[c] = before[c][1]
+                v.edge[c] = before[c][0]
+            for_sib(8, GELU, 0, v.n1t, gg)
+            for_sib(9, GELU, 1, v.n1t, gg)
+            pump()
+            carry = ends.joined()
+            for c in range(tiles):
+                v.into[c] = v.into[c] + v.edge[c] * carry[c : c + 1, :]
+            span = rows // 8
+
+            inside = pumps_at(tiles // 4, tiles // 2, 3 * tiles // 4)
+
+            def through_gates(k6, k2, k3, k7, convt, wg, inside=inside):
+                inside()
+                c = pl.program_id(0)
                 lane = pl.ds(pl.multiple_of(c * LANES, LANES), LANES)
-                rate = -cfactor * softplus_minus(small[7:8, lane])
-
-                def chunk(at, q=q, c=c, lane=lane, rate=rate):
-                    grad = v.gh[at, q * LANES : (q + 1) * LANES]
-                    value, slope = gelu_parts(pre[q, at, :])
-                    v.adj[c, at, :] = grad * value
-                    v.gg[at, lane] = low(grad * state[q, pl.ds(pl.multiple_of(at.start + 8, 8), 64), :] * slope)
-                    v.prod[c, at, :] = jnp.exp(rate * rgate[q, at, :])
-
-                rows_loop(rows, chunk, 64)
-
-        pair = lambda t: (t, 0, 0)
-        pltpu.emit_pipeline(
-            into_branch,
-            grid=(tiles // 2,),
-            in_specs=[
-                pl.BlockSpec((256, width), lambda t: (t, 0)), pl.BlockSpec((2, rows, LANES), pair),
-                pl.BlockSpec((2, rows + 8, LANES), pair), pl.BlockSpec((2, rows, LANES), pair),
-            ],
-        )(w.output_w, w.pre, w.state, w.rgate)
-        weight_pass(OUTPUT, w.rect, v.gm, False, True)
-        tails = strided_scan(v.prod, v.adj, v.prod, v.adj, True, rows)
-        before, whole = segment_ends(tails, True)
-        ends.tell(whole)
-        weight_pass(GELU, w.n1t, v.gg, False, False)
-        red.add_first(MGATE)
-        carry = ends.joined()
-        for c in range(tiles):
-            v.into[c] = before[c][0] * carry[c : c + 1, :] + before[c][1]
-        span = rows // 8
-
-        def through_gates(rgate, igate, conv, convt, state, wg):
-            c = pl.program_id(0)
-            lane = pl.ds(pl.multiple_of(c * LANES, LANES), LANES)
-            dp = small[7:8, lane]
-            rate = -cfactor * softplus_minus(dp)
-            sums = [jnp.zeros((8, LANES), f32) for _ in range(3)]
-            for k in range(8):
-                at = slice(k * span, (k + 1) * span)
-                adj = v.adj[c, at, :] + v.prod[c, at, :] * v.into[c, k : k + 1, :]
-                rg, ig, cv = rgate[at, :], igate[at, :], wide(conv[at, :])
-                log_decay = rate * rg
-                decay = jnp.exp(log_decay)
-                mult = jnp.sqrt(minus_expm1(2.0 * log_decay, log_decay))
-                grad_decay = adj * state[7 + k * span : 7 + (k + 1) * span, :]
-                grad_log = grad_decay * decay - adj * ig * cv * (decay * decay) / mult
-                grad_r = grad_log * rate * rg * (1.0 - rg)
-                through = adj * mult
-                grad_i = through * cv * ig * (1.0 - ig)
-                v.direct[at, :] = through * ig
-                v.gri[at, :LANES] = low(grad_r)
-                v.gri[at, LANES:] = low(grad_i)
-                for q, value in enumerate((grad_log * rg, grad_r, grad_i)):
-                    sums[q] = sums[q] + eight(value)
-            part[7:8, lane] = sums[0].sum(axis=0, keepdims=True) * (cfactor * sigmoid(-dp))
-            part[5:6, lane] = sums[1].sum(axis=0, keepdims=True)
-            part[6:7, lane] = sums[2].sum(axis=0, keepdims=True)
-            product = low(dot(convt[...], v.gri[...]))
-            for q in range(2):
-                unit = 2 * c + q
-                block = unit // 3
-                at = pl.ds(pl.multiple_of((unit % 3) * 64, 64), 64)
-                v.gstage[block // 2, block % 2, at, :] = product[64 * q : 64 * (q + 1), :]
-            grad_conv = v.direct[...] + dot_t(v.gri[...], wg[...])
-            v.adj[c, pl.ds(0, rows), :] = grad_conv
-            part[4:5, lane] = eight(grad_conv).sum(axis=0, keepdims=True)
-
-        one = lambda t: (t, 0, 0)
-        pltpu.emit_pipeline(
-            through_gates,
-            grid=(tiles,),
-            in_specs=[
-                pl.BlockSpec((None, rows, LANES), one), pl.BlockSpec((None, rows, LANES), one), pl.BlockSpec((None, rows, LANES), one),
-                pl.BlockSpec((None, LANES, rows), one), pl.BlockSpec((None, rows + 8, LANES), one),
-                pl.BlockSpec((LANES, 2 * LANES), lambda t: (t, 0)),
-            ],
-        )(w.rgate, w.igate, w.conv, w.convt, w.state, w.gates_w)
-
-        def halo():
-            return pltpu.make_async_remote_copy(
-                src_ref=v.adj.at[:, pl.ds(0, 8)], dst_ref=v.adj.at[:, pl.ds(rows, 8)], send_sem=v.hsend, recv_sem=v.hrecv,
-                device_id=(z, (seq + 7) % 8), device_id_type=MESH,
-            )
-
-        @pl.when(seq > 0)
-        def _():
-            halo().start()
-
-        red.to_sib(GATES).start()
-        weight_pass(GELU, w.n1t, v.gg, False, True)
-        red.add_first(MVALUE)
-        red.add_second(DOWN)
-
-        @pl.when(seq == 7)
-        def _():
-            v.adj[:, pl.ds(rows, 8), :] = jnp.zeros((tiles, 8, LANES), f32)
-
-        @pl.when(seq < 7)
-        def _():
-            halo().wait_recv()
-
-        def through_conv(lin):
-            c = pl.program_id(0)
-            lane = pl.ds(pl.multiple_of(c * LANES, LANES), LANES)
-            taps = [small[k : k + 1, lane] for k in range(4)]
-            sums = [jnp.zeros((8, LANES), f32) for _ in range(4)]
-            for r in range(0, rows, 128):
-                here = v.adj[c, r : r + 128, :]
-                acc = taps[0] * here
+                sums = [jnp.zeros((8, LANES), f32) for _ in range(3)]
+                for k in range(8):
+                    at = slice(k * span, (k + 1) * span)
+                    here = adj[c, at, :] + prod[c, at, :] * v.into[c, k : k + 1, :]
+                    grad_r = here * k6[at, :]
+                    grad_i = here * k2[at, :]
+                    adj[c, at, :] = here * k3[at, :]
+                    gri[at, :LANES] = low(grad_r)
+                    gri[at, LANES:] = low(grad_i)
+                    for q, value in enumerate((here * k7[at, :], grad_r, grad_i)):
+                        sums[q] = sums[q] + eight(value)
+                part[7:8, lane] = sums[0].sum(axis=0, keepdims=True) * (cfactor * sigmoid(-small[7:8, lane]))
+                part[5:6, lane] = sums[1].sum(axis=0, keepdims=True)
+                part[6:7, lane] = sums[2].sum(axis=0, keepdims=True)
+                product = low(dot(convt[...], gri[...]))
+                for q in range(2):
+                    unit = 2 * c + q
+                    block = unit // 3
+                    at = pl.ds(pl.multiple_of((unit % 3) * 64, 64), 64)
+                    v.gstage[block // 2, block % 2, at, :] = product[64 * q : 64 * (q + 1), :]
+                grad_conv = adj[c, pl.ds(0, rows), :] + dot_t(gri[...], wg[...])
+                adj[c, pl.ds(0, rows), :] = grad_conv
+                part[4:5, lane] = eight(grad_conv).sum(axis=0, keepdims=True)
+
+            one = pl.BlockSpec((None, rows, LANES), lambda t: (t, 0, 0))
+            pltpu.emit_pipeline(
+                through_gates,
+                grid=(tiles,),
+                in_specs=[one] * 4
+                + [pl.BlockSpec((None, LANES, rows), lambda t: (t, 0, 0)), pl.BlockSpec((LANES, wide_tile), lambda t: (t, 0))],
+            )(w.k6, w.k2, w.k3, w.k7, w.convt, w.gates_w)
+
+            def halo():
+                return pltpu.make_async_remote_copy(
+                    src_ref=v.edge, dst_ref=v.halo, send_sem=v.hsend, recv_sem=v.hrecv, device_id=(z, (seq + 7) % 8), device_id_type=MESH
+                )
+
+            v.edge[...] = adj[:, 0:8, :]
+
+            @pl.when(seq > 0)
+            def _():
+                halo().start()
+
+            for_us(8, GELU, 0, v.n1t, gg)
+            pump()
+            s = slots[GATES]
+            free_stage(10)
+            for j in range(4):
+
+                def copy_block(at, j=j):
+                    v.stage[0, pl.ds(pl.multiple_of(j * s.n + at.start, 16), 16), :] = v.gstage[j, 1 - core, at, :]
+
+                rows_loop(s.n, copy_block)
+            send_blocks(10, 4 * s.n)
+            for_us(9, GELU, 1, v.n1t, gg)
+            pump()
+
+            @pl.when(seq == 7)
+            def _():
+                adj[:, pl.ds(rows, 8), :] = jnp.zeros((tiles, 8, LANES), f32)
+
+            @pl.when(seq < 7)
+            def _():
+                halo().wait_recv()
+                adj[:, pl.ds(rows, 8), :] = v.halo[...]
+
+            inside = pumps_at(tiles // 3, 2 * tiles // 3)
+
+            def through_conv(lin, inside=inside):
+                inside()
+                c = pl.program_id(0)
+                lane = pl.ds(pl.multiple_of(c * LANES, LANES), LANES)
+                taps = [small[k : k + 1, lane] for k in range(4)]
+                sums = [jnp.zeros((8, LANES), f32) for _ in range(4)]
+                for r in range(0, rows, 128):
+                    here = adj[c, r : r + 128, :]
+                    acc = taps[0] * here
+                    for k in range(4):
+                        sums[k] = sums[k] + eight(here * lin[8 + r - k : 8 + r - k + 128, :])
+                        if k:
+                            acc = acc + taps[k] * adj[c, r + k : r + k + 128, :]
+                    gl[r : r + 128, lane] = low(acc)
                 for k in range(4):
-                    sums[k] = sums[k] + eight(here * lin[8 + r - k : 8 + r - k + 128, :])
-                    if k:
-                        acc = acc + taps[k] * v.adj[c, r + k : r + k + 128, :]
-                v.gl[r : r + 128, lane] = low(acc)
-            for k in range(4):
-                part[k : k + 1, lane] = sums[k].sum(axis=0, keepdims=True)
-
-        pltpu.emit_pipeline(through_conv, grid=(tiles,), in_specs=[pl.BlockSpec((None, rows + 8, LANES), one)])(w.lin)
-        weight_pass(INPUT, w.n1t, v.gl, False, False)
-
-        def gates_own():
-            s = slots[GATES]
-            red.to_sib(GATES).wait_recv()
+                    part[k : k + 1, lane] = sums[k].sum(axis=0, keepdims=True)
+
+            pltpu.emit_pipeline(
+                through_conv, grid=(tiles,), in_specs=[pl.BlockSpec((None, rows + 8, LANES), lambda t: (t, 0, 0))]
+            )(w.lin)
+            pump()
+            to_sib(10, sent[10]).wait_recv()
             for j in range(4):
 
-                def body(at, j=j):
-                    both = low(wide(v.gstage[j, core, at, :]) + wide(v.glanded[j, at, :]))
+                def fold(at, j=j):
+                    came = v.landed[0, pl.ds(pl.multiple_of(j * s.n + at.start, 16), 16), :]
+                    both = low(wide(v.gstage[j, core, at, :]) + wide(came))
                     s.ab[0, j, at, :] = both[:, : s.h]
                     s.ab[1, j, at, :] = both[:, s.h :]
 
-                rows_loop(s.n, body)
-            red.start_first(GATES)
-
-        def into_norm(wi, wg):
-            t = pl.program_id(0)
-            at = pl.ds(pl.multiple_of(t * 256, 256), 256)
-            v.resid[:, at] = dot_t(v.gl[...], wi[...]) + dot_t(v.gg[...], wg[...])
-
-        pltpu.emit_pipeline(into_norm, grid=(width // 256,), in_specs=[pl.BlockSpec((256, lru), lambda t: (t, 0))] * 2)(w.input_w, w.gelu_w)
-        weight_pass(INPUT, w.n1t, v.gl, False, True)
-        gates_own()
-        red.add_first(OUTPUT)
-        red.add_second(MGATE)
-        red.add_outer(DOWN)
-
-        def keep_tokens(at, value):
-            v.gn[at, :] = value
-
-        part[8:9, :width] = norm_back(lambda at: (wide(v.x[at, :]), v.resid[at, :], v.gn[at, :]), small[8:9, :width], keep_tokens)
+                rows_loop(s.n, fold)
+            give_credit(10)
+            for_sib(11, INPUT, 0, v.n1t, gl)
+            for_sib(12, INPUT, 1, v.n1t, gl)
+            pump()
+
+            inside = pumps_at(width // wide_tile // 2)
+
+            def into_norm(wi, wg, inside=inside):
+                inside()
+                t = pl.program_id(0)
+                value = dot_t(gl[...], wi[...]) + dot_t(gg[...], wg[...])
+                adj[2 * t, pl.ds(0, rows), :] = value[:, :LANES]
+                adj[2 * t + 1, pl.ds(0, rows), :] = value[:, LANES:]
+
+            pltpu.emit_pipeline(into_norm, grid=(width // wide_tile,), in_specs=[pl.BlockSpec((wide_tile, lru), lambda t: (t, 0))] * 2)(
+                w.input_w, w.gelu_w
+            )
+            for_us(11, INPUT, 0, v.n1t, gl)
+            for_us(12, INPUT, 1, v.n1t, gl)
+            pump()
+            v.gain[...] = jnp.zeros_like(v.gain)
+            tokens_load.wait()
+
+            def norm_one(at):
+                grad = jnp.concatenate([adj[c, at, :] for c in range(width // LANES)], axis=1)
+                v.gn[at, :] = norm_back(wide(v.go[at, :]), grad, small[8:9, :width], v.gn[at, :])
+
+            rows_loop(rows // 2, norm_one, 64)
+            pump()
+            rows_loop(rows, norm_one, 64, rows // 2)
+            part[8:9, :width] = v.gain[...].sum(axis=0, keepdims=True)
+
+        pl.run_scoped(
+            branch_phase,
+            pltpu.VMEM((tiles, rows + 8, LANES), f32),
+            pltpu.VMEM((tiles, rows, LANES), f32),
+            pltpu.VMEM((rows, lru), bf),
+            pltpu.VMEM((rows, lru), bf),
+            pltpu.VMEM((rows, wide_tile), bf),
+        )
         tot.begin()
-        kept = [pltpu.make_async_copy(v.gn, out.tokens_grad, v.keep.at[count, 0])]
-        kept[0].start()
-
-        def finish(i):
-            s = slots[i]
-            red.arrive(i)
-            for k in range(2):
-                cp = pltpu.make_async_copy(s.res.at[k], sum_refs[i].at[:, pl.ds(k * s.h, s.h)], v.keep.at[i, k])
-                cp.start()
-                kept.append(cp)
-
-        steps = [
-            (red.add_first, GELU), (red.add_second, MVALUE), (red.add_outer, MGATE), (red.add_peer, DOWN), (tot.step, 0),
-            (red.add_first, INPUT), (red.add_second, OUTPUT), (red.add_outer, MVALUE), (red.add_peer, MGATE), (red.pass_on, DOWN), (tot.step, 1),
-            (red.add_first, GATES), (red.add_second, GELU), (red.add_outer, OUTPUT), (red.add_peer, MVALUE), (red.pass_on, MGATE), (finish, DOWN),
-            (tot.step, 2),
-            (red.add_second, INPUT), (red.add_outer, GELU), (red.add_peer, OUTPUT), (red.pass_on, MVALUE), (finish, MGATE), (tot.step, 3),
-            (red.add_second, GATES), (red.add_outer, INPUT), (red.add_peer, GELU), (red.pass_on, OUTPUT), (finish, MVALUE), (tot.step, 4),
-            (red.add_outer, GATES), (red.add_peer, INPUT), (red.pass_on, GELU), (finish, OUTPUT),
-            (red.add_peer, GATES), (red.pass_on, INPUT), (finish, GELU), (red.pass_on, GATES), (finish, INPUT), (finish, GATES),
-        ]
-        for act, i in steps:
-            act(i)
+        cp = pltpu.make_async_copy(v.gn, out.tokens_grad, v.keep.at[count, 0])
+        cp.start()
+        kept.append(cp)
+        last = PUMPS[turn[0]]
+        for k, (step, i, h) in enumerate(last):
+            steps[step](i, h)
+            if k % 4 == 3 and k < 20:
+                tot.step(k // 4)
         cp = pltpu.make_async_copy(part, out.small_sum, v.keep.at[count, 1])
         cp.start()
         kept.append(cp)
+        for i in range(count):
+            for h in range(2):
+                kept.append(totalled(i, h))
         for cp in kept:
             cp.wait()
         for i in range(count):
             red.drain(i)
+        for k in (passes - 2, passes - 1):
+            to_sib(k, sent[k]).wait_send()
         tot.drain()
         ends.drain()
 
         @pl.when(seq > 0)
         def _():
-            halo().wait_send()
+            pltpu.make_async_remote_copy(
+                src_ref=v.edge, dst_ref=v.halo, send_sem=v.hsend, recv_sem=v.hrecv, device_id=(z, (seq + 7) % 8), device_id_type=MESH
+            ).wait_send()
 
     slot_list = [value for r, c in extents for value in slot_scratch(r, c).values()]
     result = pl.pallas_call(
         kernel,
-        out_shape=list(outs.values()) + sums + stages + stages,
+        out_shape=list(outs.values()) + sums,
         in_specs=[pl.BlockSpec(memory_space=pltpu.SMEM)] + [HBM] * len(inputs),
-        out_specs=[HBM] * (len(outs) + count + 2 * (count - 1)),
+        out_specs=[HBM] * (len(outs) + count),
         scratch_shapes=list(scratch.values()) + slot_list,
         compiler_params=pltpu.CompilerParams(collective_id=2, has_side_effects=True, vmem_limit_bytes=62 << 20),
         name="backward",
     )(lengths, *inputs.values())
-    return result[0], result[1], result[len(outs) : len(outs) + count]
+    return result[0], result[1], result[len(outs) :]
 
 
 def local(

time: 461 us -> 378 us (0.82)
  Pallas kernels: 434 us -> 348 us
    pallas_call x1, Pallas kernels: 276 us -> 185 us  [backward_call(): pl.pallas_call(kernel, out_shape=list(outs.values()) + sums, in_specs=[pl...]
    pallas_call x1, Pallas kernels: 157 us -> 163 us  [forward_call(): pl.pallas_call(kernel, out_shape=wholes + [saved[name] for name in names]...]
where the time goes in v3:
time: 378 us; the launch traced here: 372 us
  Pallas kernels  348 us (92%)
  other arithmetic  12.1 us (3%)
  local copies, waits for them, and re-layouts  12 us (3%)
    pallas_call x1, Pallas kernels, backward_call(): pl.pallas_call(kernel, out_shape=list(outs.values()) + sums, in_specs=[pl...  185 us
    pallas_call x1, Pallas kernels, forward_call(): pl.pallas_call(kernel, out_shape=wholes + [saved[name] for name in names]...  163 us
    convert_element_type x6, other arithmetic, local_fast(): value.astype(jnp.float32)  9.85 us

profile of v3, /device:TPU:0, one launch (start us, length us, event | category | flops | bytes accessed | tf_op | source)
XLA Modules:
  0.0 372.3 jit_solution(12111583702438970384)
XLA Ops:
  0.7 0.7 broadcast_in_dim.16
  1.3 0.7 broadcast_in_dim.17
  2.0 0.7 broadcast_in_dim.18
  2.6 0.7 broadcast_in_dim.19
  3.3 0.7 concatenate.6
  4.0 0.6 dynamic_update_slice.6
  4.6 0.7 convert_dynamic-update-slice_fusion.refs_0_
  5.3 0.0 copy-start.5
  5.3 1.5 pad_maximum_fusion.refs_3_
  6.8 0.0 copy-done.5
  6.8 162.6 %forward.1 = (f32[128,1536]{1,0:T(8,128)}, bf16[1024,1536]{1,0:T(8,128)(2,1)}, bf16[1024,1536]{1,0:T(8,128)(2,1)}, bf16[1536,256]{1,0:T(8,128)(2,1)}, bf16[1536,...) custom-call(s32[4]{0:T(128)} %lengths_ref.3, ...), custom_call_target="tpu_custom_call" | custom-call | tf_op jit(solution)/shard_map/forward/pallas_call | solution.py:894
  169.4 185.0 %backward.1 = (f32[512,1024]{1,0:T(8,128)}, f32[16,1536]{1,0:T(8,128)}, bf16[384,1024]{1,0:T(8,128)(2,1)}, bf16[128,3072]{1,0:T(8,128)(2,1)}, bf16[128,3072]{1,0...) custom-call(s32[4]{0:T(128)} %lengths_ref.3, ...), custom_call_target="tpu_custom_call" | custom-call | tf_op jit(solution)/shard_map/backward/pallas_call | solution.py:1492
  354.4 0.0 copy-start.4
  354.4 0.7 constant_dynamic-slice_fusion
  355.2 0.5 slice_bitcast_fusion
  355.7 0.0 copy-start.3
  355.7 2.0 convert_element_type.29
  357.7 2.0 convert_element_type.30
  359.7 1.4 dynamic-slice_bitcast_fusion
  361.1 1.5 fusion
  362.6 0.0 copy-start.2
  362.6 1.6 fusion.1
  364.1 2.0 convert_element_type.32
  366.1 0.0 copy-done.4
  366.1 0.0 copy-start.1
  366.1 1.3 convert_element_type.33
  367.4 0.0 copy-done.3
  367.4 0.0 copy-start
  367.4 1.3 convert_element_type.34
  368.7 0.0 copy-done.2
  368.7 1.3 convert_element_type.35
  370.0 0.0 copy-done.1
  370.0 1.0 copy.39
  371.0 0.0 copy-done
  371.0 1.3 copy.40
  (2 shorter events, 0.0 us)
Async XLA Ops:
  5.3 1.5 copy-start.5
  354.4 11.7 %copy-start.4 = (bf16[128,3072]{1,0:T(8,128)(2,1)S(1)}, bf16[128,3072]{1,0:T(8,128)(2,1)}, u32[]{:S(2)}) copy-start(bf16[128,3072]{1,0:T(8,128)(2,1)} %get-tuple-element.82) | copy-start | bytes 2359300
  355.7 11.7 %copy-start.3 = (bf16[128,3072]{1,0:T(8,128)(2,1)S(1)}, bf16[128,3072]{1,0:T(8,128)(2,1)}, u32[]{:S(2)}) copy-start(bf16[128,3072]{1,0:T(8,128)(2,1)} %get-tuple-element.83) | copy-start | bytes 2359300
  362.6 6.1 %copy-start.2 = (bf16[384,1024]{1,0:T(8,128)(2,1)S(1)}, bf16[384,1024]{1,0:T(8,128)(2,1)}, u32[]{:S(2)}) copy-start(bf16[384,1024]{1,0:T(8,128)(2,1)} %get-tuple-element.84) | copy-start | bytes 2359300
  366.1 3.9 %copy-start.1 = (bf16[512,1024]{1,0:T(8,128)(2,1)S(1)}, bf16[512,1024]{1,0:T(8,128)(2,1)}, u32[]{:S(2)}) copy-start(bf16[512,1024]{1,0:T(8,128)(2,1)} %get-tuple-element.110) | copy-start | bytes 3145732
  367.4 3.6 copy-start

commit v4 on v3

--- a/solution.py
+++ b/solution.py
@@ -129,47 +129,42 @@
     pl.semaphore_wait(barrier, len(peers))
 
 
-def when(cond, body):
-    if cond is None:
-        body()
-    else:
-        pl.when(cond)(body)
-
-
 GOT = ("X", "Y", "D1", "D2", "SO", "SX", "SY", "S1", "S2")
 SENT = ("ox", "oy", "os", "fy", "fx", "zX", "zY", "zD1", "zD2", "SX", "SY", "S1", "S2")
+OVER_LINKS = GOT[:4]
+TO_SIB = dict(zip(OVER_LINKS, GOT[5:]))
 
 
 class Gather:
     def __init__(self, place, shards, fulls, kinds, send, recv, own, bounce):
-        self.p, self.shards, self.fulls, self.bounce = place, shards, fulls, bounce
+        self.p, self.shards, self.fulls, self.bounce, self.kinds = place, shards, fulls, bounce, kinds
         self.send, self.recv, self.own = send, recv, own
-        even = place.z % 2 == 0
-        odd = place.z % 2 == 1
-        self.fetch = [(None, even, odd)[kind] for kind in kinds]
-        self.shared = [kind > 0 for kind in kinds]
         self.znb = place.level(place.z + 1 - 2 * (place.z % 2))
+
+    def fetched(self, i, odd):
+        return self.kinds[i] != 2 - odd
 
     def part(self, i, name):
         p = self.p
         n = self.shards[i].shape[0]
-        spot = {
-            "O": (p.y, p.x, p.core), "X": (p.y, 1 - p.x, p.core), "Y": (1 - p.y, p.x, p.core),
-            "D1": (1 - p.y, 1 - p.x, p.core), "D2": (1 - p.y, 1 - p.x, p.core),
-            "SO": (p.y, p.x, 1 - p.core), "SX": (p.y, 1 - p.x, 1 - p.core), "SY": (1 - p.y, p.x, 1 - p.core),
-            "S1": (1 - p.y, 1 - p.x, 1 - p.core), "S2": (1 - p.y, 1 - p.x, 1 - p.core),
-        }[name]
-        first = pl.multiple_of(p.at(*spot) * n, n)
-        if name in ("D1", "S1"):
+        y, x = p.y, p.x
+        if name[-1] == "X":
+            x = 1 - x
+        elif name[-1] == "Y":
+            y = 1 - y
+        elif name[-1] in "12":
+            x, y = 1 - x, 1 - y
+        core = 1 - p.core if name[0] == "S" else p.core
+        first = pl.multiple_of(p.at(y, x, core) * n, n)
+        if name[-1] == "1":
             return pl.ds(first, n // 2)
-        if name in ("D2", "S2"):
+        if name[-1] == "2":
             return pl.ds(pl.multiple_of(first + n // 2, n // 2), n // 2)
         return pl.ds(first, n)
 
     def half(self, i, name, which):
         n = self.shards[i].shape[0]
-        first = self.part(i, name).start
-        return pl.ds(pl.multiple_of(first + which * (n // 2), n // 2), n // 2)
+        return pl.ds(pl.multiple_of(self.part(i, name).start + which * (n // 2), n // 2), n // 2)
 
     def copy(self, i, how, got, peer, rows, src=None):
         full = self.fulls[i]
@@ -197,66 +192,47 @@
             return pltpu.make_async_copy(self.shards[i], self.bounce[i], self.own.at[i, 0])
         return pltpu.make_async_copy(self.bounce[i], self.fulls[i].at[self.part(i, "O")], self.own.at[i, 1])
 
-    def start(self, i):
-        def far():
+    def start(self, i, odd):
+        if self.fetched(i, odd):
             for c in self.own_far(i):
                 c.start()
-
-        when(self.fetch[i], far)
         self.own_near(i).start()
         self.own_kept(i, 0).start()
 
-    def onward_far(self, i, name):
+    def onward(self, i, name, odd):
         p = self.p
-        far = []
+        copies = []
+        if self.fetched(i, odd):
+            if name == "X":
+                copies.append(self.copy(i, "fy", "D1", p.ynb, self.half(i, "X", 0)))
+            if name == "Y":
+                copies.append(self.copy(i, "fx", "D2", p.xnb, self.half(i, "Y", 1)))
+            if self.kinds[i]:
+                copies.append(self.copy(i, "z" + name, name, self.znb, self.part(i, name)))
+        copies.append(self.copy(i, TO_SIB[name], TO_SIB[name], p.sib, self.part(i, name)))
+        return copies
+
+    def relay(self, i, name, odd):
+        self.wait(i, name)
+        for c in self.onward(i, name, odd):
+            c.start()
         if name == "X":
-            far.append(self.copy(i, "fy", "D1", p.ynb, self.half(i, "X", 0)))
-        if name == "Y":
-            far.append(self.copy(i, "fx", "D2", p.xnb, self.half(i, "Y", 1)))
-        if self.shared[i]:
-            far.append(self.copy(i, "z" + name, name, self.znb, self.part(i, name)))
-        return far
-
-    def onward_near(self, i, name):
-        to_sib = {"X": "SX", "Y": "SY", "D1": "S1", "D2": "S2"}[name]
-        return self.copy(i, to_sib, to_sib, self.p.sib, self.part(i, name))
-
-    def relay(self, i, names):
-        for name in names:
-            self.wait(i, name)
-
-            def far(name=name):
-                for c in self.onward_far(i, name):
-                    c.start()
-
-            if name in ("X", "Y") or self.shared[i]:
-                when(self.fetch[i], far)
-            self.onward_near(i, name).start()
-            if name == "X":
-                self.own_kept(i, 0).wait()
-                self.own_kept(i, 1).start()
+            self.own_kept(i, 0).wait()
+            self.own_kept(i, 1).start()
 
     def arrive(self, i):
-        for name in ("SO", "SX", "SY", "S1", "S2"):
+        for name in GOT[4:]:
             self.wait(i, name)
         self.own_kept(i, 1).wait()
 
-    def drain(self, i):
-        self.own_near(i).wait_send()
-        for name in ("X", "Y", "D1", "D2"):
-            self.onward_near(i, name).wait_send()
-
-        def far():
+    def drain(self, i, odd):
+        if self.fetched(i, odd):
             for c in self.own_far(i):
                 c.wait_send()
-            for name in ("X", "Y", "D1", "D2"):
-                for c in self.onward_far(i, name):
-                    c.wait_send()
-
-        when(self.fetch[i], far)
-
-    def peers(self):
-        return [self.p.sib, self.p.xnb, self.p.ynb, self.znb]
+        self.own_near(i).wait_send()
+        for name in OVER_LINKS:
+            for c in self.onward(i, name, odd):
+                c.wait_send()
 
 
 def rows_loop(total, body, step=16, start=0):
@@ -556,12 +532,18 @@
         for c, (prod, total) in enumerate(whole):
             self.slots[self.p.seq, 0, c : c + 1, :] = prod
             self.slots[self.p.seq, 1, c : c + 1, :] = total
+        self.share()
+
+    def share(self):
         for d in range(1, 8):
             self.copy(d).start()
 
-    def joined(self):
+    def shared(self):
         for d in range(1, 8):
             self.come(d).wait_recv()
+
+    def joined(self):
+        self.shared()
         carry = jnp.zeros(self.slots.shape[2:], jnp.float32)
         for k in range(7, 0, -1) if self.backward else range(7):
             further = self.slots[k, 0] * carry + self.slots[k, 1]
@@ -582,12 +564,87 @@
 VMEM = pl.BlockSpec(memory_space=pltpu.VMEM)
 
 
-def forward_call(lengths, tokens, shards):
+KINDS = (0, 1, 0, 0, 2, 1, 0)
+FETCHES = (
+    (
+        ((0, 1),),
+        ((0, 0),),
+        ((0, 2), (1, 1), (2, 1), (1, 0), (2, 0), (1, 2), (2, 2), (3, 1), (4, 1), (0, 5), (0, 4), (3, 0), (4, 0), (3, 2), (4, 2),),
+        (),
+        (),
+        (),
+        ((0, 3),),
+        ((1, 4), (1, 5), (2, 5),),
+        (),
+        (),
+        ((1, 3), (2, 3),),
+        ((0, 6), (2, 4),),
+        ((3, 5), (4, 5),),
+        ((3, 3), (4, 3),),
+        ((3, 4),),
+        (),
+        (),
+        ((4, 4),),
+        (),
+        (),
+        ((1, 6), (2, 6),),
+        (),
+        (),
+        (),
+        (),
+        ((3, 6), (4, 6),),
+        (),
+        (),
+        (),
+        (),
+        (),
+        (),
+        (),
+    ),
+    (
+        ((0, 0), (0, 1), (0, 4),),
+        (),
+        ((1, 0), (2, 0), (1, 1), (0, 2), (0, 5), (1, 4), (2, 4), (2, 1), (3, 0), (4, 0), (3, 1), (1, 2), (2, 2),),
+        ((4, 1), (0, 3),),
+        (),
+        ((3, 4), (4, 4), (3, 2), (4, 2),),
+        ((0, 6),),
+        (),
+        ((1, 3), (2, 3),),
+        (),
+        (),
+        ((1, 5),),
+        ((1, 6), (2, 6),),
+        (),
+        ((3, 3), (4, 3),),
+        (),
+        ((3, 6), (4, 6),),
+        ((2, 5),),
+        (),
+        (),
+        (),
+        ((3, 5),),
+        (),
+        (),
+        (),
+        ((4, 5),),
+        (),
+        (),
+        (),
+        (),
+        (),
+        (),
+        (),
+    ),
+)
+
+
+def forward_call(lengths, tokens, small_own, shards):
     rows, width = tokens.shape
-    lru = shards[1].shape[1]
-    ff = shards[5].shape[1]
+    lru = shards[0].shape[1]
+    ff = shards[4].shape[1]
     tiles = lru // LANES
-    kinds = (0,) * 8
+    kinds = KINDS
     count = len(shards)
     f32, bf = jnp.float32, jnp.bfloat16
     shape = jax.ShapeDtypeStruct
@@ -609,6 +666,7 @@
         resid=shape((rows, width), f32),
         n2t=shape((width, rows), bf),
         mg=shape((rows, ff), f32),
+        bend=shape((rows, ff), f32),
         mv=shape((rows, ff), f32),
         hidt=shape((ff, rows), bf),
     )
@@ -617,7 +675,8 @@
         x=pltpu.VMEM((rows, width), bf),
         n1=pltpu.VMEM((rows, width), bf),
         n1t=pltpu.VMEM((width, rows), bf),
-        parts=pltpu.VMEM((8 * 16, lru), f32),
+        parts=pltpu.VMEM((8,) + small_own.shape, f32),
+        into=pltpu.VMEM((8 * tiles, LANES), f32),
         small=pltpu.VMEM((16, lru), f32),
         pre=pltpu.VMEM((tiles, rows, LANES), f32),
         lin=pltpu.VMEM((tiles, rows + 8, LANES), f32),
@@ -641,6 +700,8 @@
         gown=pltpu.SemaphoreType.DMA((count, 2)),
         esend=pltpu.SemaphoreType.DMA((7,)),
         erecv=pltpu.SemaphoreType.DMA((7,)),
+        ssend=pltpu.SemaphoreType.DMA((7,)),
+        srecv=pltpu.SemaphoreType.DMA((7,)),
         hsend=pltpu.SemaphoreType.DMA(()),
         hrecv=pltpu.SemaphoreType.DMA(()),
         load=pltpu.SemaphoreType.DMA((2,)),
@@ -649,17 +710,24 @@
     keys = list(scratch)
     R = 128
 
-    def kernel(lengths_ref, tokens_ref, *refs):
+    def kernel(lengths_ref, tokens_ref, small_ref, *refs):
         ins, outs = refs[:count], refs[count : 2 * count]
         out = named(names, refs[2 * count : 2 * count + len(names)])
         bounce = refs[-count:]
         v = named(keys, refs[2 * count + len(names) : -count])
-        gelu_w, input_w, gates_w, output_w, mgate_w, mvalue_w, mdown_w = outs[1:]
+        gelu_w, input_w, gates_w, output_w, mgate_w, mvalue_w, mdown_w = outs
         place = Place()
         gather = Gather(place, ins, outs, kinds, v.gsend, v.grecv, v.gown, bounce)
         ends = Ends(place, v.ends, (v.esend, v.erecv), False)
+        packs = Ends(place, v.parts, (v.ssend, v.srecv), False)
         z, seq = place.z, place.seq
-        meet([(z, (seq + d) % 8) for d in range(1, 8)])
+        loads = [
+            pltpu.make_async_copy(tokens_ref, v.x, v.load.at[0]),
+            pltpu.make_async_copy(small_ref, v.parts.at[seq], v.load.at[1]),
+        ]
+        for cp in loads:
+            cp.start()
+        meet([(z, (seq + d) % 8) for d in range(1, 8)] + [gather.znb])
         kept = []
 
         def keep(src, dst):
@@ -667,25 +735,55 @@
             cp.start()
             kept.append(cp)
 
-        load = pltpu.make_async_copy(tokens_ref, v.x, v.load.at[0])
-        load.start()
-        for i in range(4):
-            gather.start(i)
-        load.wait()
-        gather.relay(0, ("X", "Y"))
-        gather.start(4)
-        gather.relay(0, ("D1", "D2"))
-        gather.arrive(0)
-        load = pltpu.make_async_copy(outs[0], v.parts, v.load.at[1])
-        load.start()
-        gather.relay(1, ("X", "Y"))
-        load.wait()
+        def by_level(act):
+            for odd in range(2):
+                pl.when(z % 2 == odd)(lambda odd=odd: act(odd))
+
+        turn_of = [0]
+
+        def serve(spot):
+            def act(odd):
+                for step, i in FETCHES[odd][spot]:
+                    if step == 0:
+                        gather.start(i, odd)
+                    else:
+                        gather.relay(i, OVER_LINKS[step - 1], odd)
+
+            if FETCHES[0][spot] or FETCHES[1][spot]:
+                by_level(act)
+
+        def pump():
+            serve(turn_of[0])
+            turn_of[0] += 1
+
+        def pumps_at(*places):
+            spots = list(enumerate(places, turn_of[0]))
+            turn_of[0] += len(spots)
+
+            def at_place(here):
+                for spot, there in spots:
+                    if FETCHES[0][spot] or FETCHES[1][spot]:
+                        pl.when(here == there)(lambda spot=spot: serve(spot))
+
+            return at_place
+
+        loads[1].wait()
+        packs.share()
+        pump()
+        packs.shared()
         small = v.small
-        total = v.parts[0:16, :]
-        for k in range(1, 8):
-            total = total + v.parts[16 * k : 16 * (k + 1), :]
-        small[...] = total
+        lane = lax.broadcasted_iota(jnp.int32, (8, LANES), 1)
+        for k in range(4):
+            left, right = v.parts[2 * k, 0:8, :], pltpu.roll(v.parts[2 * k + 1, 0:8, :], 64, axis=1)
+            first = 3 * k * LANES
+            small[0:8, first : first + LANES] = left[:, :LANES]
+            small[0:8, first + LANES : first + 2 * LANES] = jnp.where(lane < 64, left[:, LANES:], right[:, :LANES])
+            small[0:8, first + 2 * LANES : first + 3 * LANES] = right[:, LANES:]
+        for k in range(8):
+            small[8:16, k * LANES : (k + 1) * LANES] = v.parts[k, 8:16, :LANES]
+        small[8:16, width:] = jnp.zeros((8, lru - width), f32)
         keep(v.small, out.small)
+        loads[0].wait()
 
         def norm_one(at):
             x = wide(v.x[at, :])
@@ -693,9 +791,7 @@
             v.n1[at, :] = low(x * scale * small[8:9, :width])
 
         rows_loop(rows, norm_one, 64)
-        gather.relay(2, ("X", "Y"))
-        gather.start(5)
-        gather.relay(1, ("D1", "D2"))
+        pump()
 
         def turn(src, dst, at):
             dst[at, :] = src[:, at].T
@@ -705,24 +801,24 @@
             turn(v.n1, v.n1t, pl.ds(pl.multiple_of(k * 256, 256), 256))
 
         keep(v.n1t, out.n1t)
-        gather.relay(3, ("X", "Y"))
-        gather.relay(2, ("D1", "D2"))
-        gather.arrive(1)
 
         def project(weight, dst, first):
+            inside = pumps_at(tiles // 4)
+
             def body(w):
                 t = pl.program_id(0)
+                inside(t)
                 both = dot(v.n1[...], w[...])
                 dst[2 * t, pl.ds(first, rows), :] = both[:, :LANES]
                 dst[2 * t + 1, pl.ds(first, rows), :] = both[:, LANES:]
 
             pltpu.emit_pipeline(body, grid=(tiles // 2,), in_specs=[pl.BlockSpec((width, 2 * LANES), lambda t: (0, t))])(weight)
 
+        pump()
+        gather.arrive(0)
         project(gelu_w, v.pre, 0)
-        gather.relay(4, ("X", "Y"))
-        gather.start(6)
-        gather.relay(3, ("D1", "D2"))
-        gather.arrive(2)
+        pump()
+        gather.arrive(1)
         project(input_w, v.lin, 8)
 
         def halo():
@@ -735,10 +831,8 @@
         def _():
             halo().start()
 
-        gather.relay(5, ("X", "Y"))
-        gather.relay(4, ("D1", "D2"))
-        gather.start(7)
-        gather.arrive(3)
+        pump()
+        gather.arrive(2)
 
         @pl.when(seq == 0)
         def _():
@@ -750,8 +844,11 @@
 
         keep(v.lin, out.lin)
 
+        gates_inside = pumps_at(tiles // 3, 2 * tiles // 3)
+
         def gates(w):
             h = pl.program_id(0)
+            gates_inside(h)
             lane = pl.ds(pl.multiple_of(h * LANES, LANES), LANES)
             taps = [small[k : k + 1, lane] for k in range(4)]
             cb, rb, ib, dp = [small[k : k + 1, lane] for k in range(4, 8)]
@@ -782,23 +879,25 @@
         pltpu.emit_pipeline(gates, grid=(tiles,), in_specs=[pl.BlockSpec((LANES, 2 * LANES), lambda h: (h, 0))])(gates_w)
         for src, dst in ((v.convt, out.convt), (v.decay, out.decay), (v.k2, out.k2), (v.k3, out.k3)):
             keep(src, dst)
-        gather.relay(6, ("X", "Y"))
-        gather.relay(5, ("D1", "D2"))
-        tails = strided_scan(v.prod, v.total, v.prod, v.total, False, rows, lambda: None)
+        pump()
+        tails = strided_scan(v.prod, v.total, v.prod, v.total, False, rows, pump)
         before, whole = segment_ends(tails, False)
         ends.tell(whole)
-        gather.relay(7, ("X", "Y"))
-        gather.relay(6, ("D1", "D2"))
+        pump()
         carry = ends.joined()
         span = rows // 8
         for c in range(tiles):
             into = before[c][0] * carry[c : c + 1, :] + before[c][1]
-            v.parts[8 * c : 8 * c + 8, 0:LANES] = into
+            v.into[8 * c : 8 * c + 8, :] = into
+
+        pump()
+        state_inside = pumps_at(tiles // 3, 2 * tiles // 3)
 
         @pl.loop(0, tiles)
         def _(c):
+            state_inside(c)
             lane = pl.ds(pl.multiple_of(c * LANES, LANES), LANES)
-            into = v.parts[pl.ds(pl.multiple_of(c * 8, 8), 8), 0:LANES]
+            into = v.into[pl.ds(pl.multiple_of(c * 8, 8), 8), :]
             rate = -cfactor * softplus_minus(small[7:8, lane])
             first = lax.broadcasted_iota(jnp.int32, (span, LANES), 0) == 0
             for s in range(8):
@@ -818,55 +917,72 @@
         for src, dst in ((v.k6, out.k6), (v.k7, out.k7), (v.pre, out.pre), (v.total, out.slope)):
             keep(src, dst)
         keep(v.rect, out.rect)
-        gather.arrive(4)
+        pump()
+        gather.arrive(3)
+        width_inside = pumps_at(width // 512)
 
         def back_to_width(w):
             t = pl.program_id(0)
+            width_inside(t)
             at = pl.ds(pl.multiple_of(t * 256, 256), 256)
             v.resid[:, at] = wide(v.x[:, at]) + dot(v.rec[...], w[...])
 
         pltpu.emit_pipeline(back_to_width, grid=(width // 256,), in_specs=[pl.BlockSpec((lru, 256), lambda t: (0, t))])(output_w)
         keep(v.resid, out.resid)
+        pump()
         def norm_two(at):
             x = v.resid[at, :]
             scale = lax.rsqrt(jnp.mean(x * x, axis=-1, keepdims=True) + epsilon)
             v.n2[at, :] = low(x * scale * small[9:10, :width])
 
         rows_loop(rows, norm_two, 64)
+        pump()
 
         @pl.loop(0, width // 256)
         def _(k):
             turn(v.n2, v.n2t, pl.ds(pl.multiple_of(k * 256, 256), 256))
 
         keep(v.n2t, out.n2t)
+        steps = ff // 256
+        sixths = [k * steps // 6 for k in range(1, 6)]
+        across = pl.BlockSpec((rows, 256), lambda t: (0, t))
+        columns = pl.BlockSpec((width, 256), lambda t: (0, t))
+        pump()
+        gather.arrive(4)
+        gate_inside = pumps_at(*sixths)
+
+        def mlp_gate(wg, value, slope):
+            gate_inside(pl.program_id(0))
+            value[...] = dot(v.n2[...], wg[...])
+
+            def act(rs):
+                value[rs, :], slope[rs, :] = gelu_parts(value[rs, :])
+
+            rows_loop(rows, act, 64)
+
+        pltpu.emit_pipeline(mlp_gate, grid=(steps,), in_specs=[columns], out_specs=[across, across])(mgate_w, out.mg, out.bend)
+        pump()
         gather.arrive(5)
+        value_inside = pumps_at(*sixths)
+
+        def mlp_value(wv, value, slope, mv, hidt):
+            t = pl.program_id(0)
+            value_inside(t)
+            at = pl.ds(pl.multiple_of(t * 256, 256), 256)
+            linear = dot(v.n2[...], wv[...])
+            mv[...] = linear * slope[...]
+            hidden = low(linear * value[...])
+            v.hidden[:, at] = hidden
+            hidt[...] = hidden.T
+
+        pltpu.emit_pipeline(
+            mlp_value,
+            grid=(steps,),
+            in_specs=[columns, across, across],
+            out_specs=[across, pl.BlockSpec((256, rows), lambda t: (t, 0))],
+        )(mvalue_w, out.mg, out.bend, out.mv, out.hidt)
+        pump()
         gather.arrive(6)
-
-        def mlp(wg, wv, mg, mv, hidt):
-            t = pl.program_id(0)
-            at = pl.ds(pl.multiple_of(t * 256, 256), 256)
-            mg[...] = dot(v.n2[...], wg[...])
-            mv[...] = dot(v.n2[...], wv[...])
-
-            def act(rs):
-                value, slope = gelu_parts(mg[rs, :])
-                linear = mv[rs, :]
-                v.hidden[rs, at] = low(value * linear)
-                mg[rs, :] = value
-                mv[rs, :] = linear * slope
-
-            rows_loop(rows, act, 64)
-            hidt[...] = v.hidden[:, at].T
-
-        wide_tile = pl.BlockSpec((width, 256), lambda t: (0, t))
-        pltpu.emit_pipeline(
-            mlp,
-            grid=(ff // 256,),
-            in_specs=[wide_tile, wide_tile],
-            out_specs=[pl.BlockSpec((rows, 256), lambda t: (0, t))] * 2 + [pl.BlockSpec((256, rows), lambda t: (t, 0))],
-        )(mgate_w, mvalue_w, out.mg, out.mv, out.hidt)
-        gather.relay(7, ("D1", "D2"))
-        gather.arrive(7)
         valid_rows = lengths_ref[z] - seq * rows
 
         def down(w, mixed):
@@ -883,9 +999,15 @@
         )(mdown_w, out.mixed)
         for cp in kept:
             cp.wait()
-        for i in range(count):
-            gather.drain(i)
+        pump()
+
+        def drain(odd):
+            for i in range(count):
+                gather.drain(i, odd)
+
+        by_level(drain)
         ends.drain()
+        packs.drain()
 
         @pl.when(seq < 7)
         def _():
@@ -894,12 +1016,12 @@
     result = pl.pallas_call(
         kernel,
         out_shape=wholes + [saved[name] for name in names],
-        in_specs=[pl.BlockSpec(memory_space=pltpu.SMEM), HBM] + [HBM] * count,
+        in_specs=[pl.BlockSpec(memory_space=pltpu.SMEM), HBM, HBM] + [HBM] * count,
         out_specs=[HBM] * (count + len(names)),
         scratch_shapes=[scratch[key] for key in keys] + [pltpu.VMEM(s.shape, s.dtype) for s in shards],
         compiler_params=pltpu.CompilerParams(collective_id=1, has_side_effects=True, vmem_limit_bytes=60 << 20),
         name="forward",
-    )(lengths, tokens, *shards)
+    )(lengths, tokens, small_own, *shards)
     return result[:count], named(names, result[count:])
 
 def slot_scratch(rows, columns):
@@ -1788,14 +1910,13 @@
     ).astype(jnp.float32)
     model_rows = jnp.stack([mixer_gain, mlp_gain]).astype(jnp.float32)
     mine = lax.axis_index("seq")
-    small = jnp.zeros((16, width_lru), jnp.float32)
-    small = lax.dynamic_update_slice(small, lru_rows, (0, mine * lru_rows.shape[1]))
-    small = lax.dynamic_update_slice(small, model_rows, (8, mine * model_rows.shape[1]))
+    across = lambda value, columns: jnp.pad(value, ((0, 0), (0, columns - value.shape[1])))
+    small = jnp.concatenate([across(lru_rows, 256), across(model_rows, 256), jnp.zeros((6, 256), jnp.float32)], axis=0)
     gates = jnp.concatenate([rgate_weight, igate_weight], axis=1)
     weights, saved = forward_call(
-        lengths, tokens, [small, gelu_weight, input_weight, gates, output_weight, mlp_gate, mlp_value, mlp_down]
-    )
-    tokens_grad, small_sum, big = backward_call(lengths, tokens, cotangent, weights[1:], saved)
+        lengths, tokens, small, [gelu_weight, input_weight, gates, output_weight, mlp_gate, mlp_value, mlp_down]
+    )
+    tokens_grad, small_sum, big = backward_call(lengths, tokens, cotangent, weights, saved)
     down, mgate, mvalue, out_w, gelu_w, input_w, gates = [value.astype(jnp.float32) for value in big]
     lru_own = lax.dynamic_slice(small_sum, (0, mine * conv_bias.shape[0]), (8, conv_bias.shape[0]))
     model_own = lax.dynamic_slice(small_sum, (8, mine * mixer_gain.shape[0]), (2, mixer_gain.shape[0]))

time: 378 us -> 351 us (0.929)
  Pallas kernels: 348 us -> 325 us
    pallas_call x1, Pallas kernels: 163 us -> 131 us  [forward_call(): pl.pallas_call(kernel, out_shape=wholes + [saved[name] for name in names]...]
    pallas_call x1, Pallas kernels: 185 us -> 194 us  [backward_call(): pl.pallas_call(kernel, out_shape=list(outs.values()) + sums, in_specs=[pl...]
where the time goes in v4:
time: 351 us; the launch traced here: 348 us
  Pallas kernels  325 us (93%)
  other arithmetic  12.1 us (3%)
  local copies, waits for them, and re-layouts  10.5 us (3%)
    pallas_call x1, Pallas kernels, backward_call(): pl.pallas_call(kernel, out_shape=list(outs.values()) + sums, in_specs=[pl...  194 us
    pallas_call x1, Pallas kernels, forward_call(): pl.pallas_call(kernel, out_shape=wholes + [saved[name] for name in names]...  131 us
    convert_element_type x6, other arithmetic, local_fast(): value.astype(jnp.float32)  9.22 us

profile of v4, /device:TPU:0, one launch (start us, length us, event | category | flops | bytes accessed | tf_op | source)
XLA Modules:
  0.0 348.1 jit_solution(8097099318770836685)
XLA Ops:
  0.7 1.5 pad_maximum_fusion.refs_2_
  2.1 0.7 broadcast_in_dim.15
  2.8 0.7 broadcast_in_dim.16
  3.4 0.7 broadcast_in_dim.17
  4.1 0.7 broadcast_in_dim.18
  4.8 0.7 concatenate.9
  5.5 0.7 fusion.3
  6.2 0.1 pad.22.clone
  6.2 0.7 maximum_maximum_fusion.small_ref
  6.9 130.7 %forward.1 = (bf16[1024,1536]{1,0:T(8,128)(2,1)}, bf16[1024,1536]{1,0:T(8,128)(2,1)}, bf16[1536,256]{1,0:T(8,128)(2,1)}, bf16[1536,1024]{1,0:T(8,128)(2,1)}, bf1...) custom-call(s32[4]{0:T(128)} %lengths_ref.3, ...), custom_call_target="tpu_custom_call" | custom-call | tf_op jit(solution)/shard_map/forward/pallas_call | solution.py:1016
  137.7 194.1 %backward.1 = (f32[512,1024]{1,0:T(8,128)}, f32[16,1536]{1,0:T(8,128)}, bf16[384,1024]{1,0:T(8,128)(2,1)}, bf16[128,3072]{1,0:T(8,128)(2,1)}, bf16[128,3072]{1,0...) custom-call(s32[4]{0:T(128)} %lengths_ref.3, ...), custom_call_target="tpu_custom_call" | custom-call | tf_op jit(solution)/shard_map/backward/pallas_call | solution.py:1614
  331.8 0.0 copy-start.2
  331.8 0.0 copy-start.6
  331.8 2.5 convert_element_type.31
  334.3 0.0 copy-start.5
  334.3 0.0 copy-start.4
  334.3 2.5 convert_element_type.32
  336.9 0.0 copy-start.3
  336.9 0.0 copy-done.2
  336.9 0.0 copy-start.1
  336.9 1.3 convert_element_type.33
  338.2 0.0 copy-start
  338.2 0.0 copy-done.6
  338.2 1.0 convert_element_type.27
  339.1 0.0 copy-done.5
  339.1 1.0 convert_element_type.28
  340.1 0.0 copy-done.4
  340.1 1.0 convert_element_type.30
  341.1 0.0 copy-done.3
  341.1 0.7 fusion.5
  341.8 1.5 fusion.4
  343.3 1.4 dynamic-slice_bitcast_fusion
  344.6 0.7 constant_dynamic-slice_fusion
  345.3 0.5 slice_bitcast_fusion
  345.8 0.0 copy-done.1
  345.8 1.0 copy.37
  346.8 0.0 copy-done
  346.8 1.3 copy.38
  (2 shorter events, 0.0 us)
Async XLA Ops:
  331.8 5.1 %copy-start.2 = (bf16[384,1024]{1,0:T(8,128)(2,1)S(1)}, bf16[384,1024]{1,0:T(8,128)(2,1)}, u32[]{:S(2)}) copy-start(bf16[384,1024]{1,0:T(8,128)(2,1)} %get-tuple-element.84) | copy-start | bytes 2359300
  331.8 6.4 %copy-start.6 = (bf16[128,1536]{1,0:T(8,128)(2,1)S(1)}, bf16[128,1536]{1,0:T(8,128)(2,1)}, u32[]{:S(2)}) copy-start(bf16[128,1536]{1,0:T(8,128)(2,1)} %get-tuple-element.78) | copy-start | bytes 1179652
  334.3 4.8 %copy-start.5 = (bf16[128,1536]{1,0:T(8,128)(2,1)S(1)}, bf16[128,1536]{1,0:T(8,128)(2,1)}, u32[]{:S(2)}) copy-start(bf16[128,1536]{1,0:T(8,128)(2,1)} %get-tuple-element.79) | copy-start | bytes 1179652
  334.3 5.8 %copy-start.4 = (bf16[192,1024]{1,0:T(8,128)(2,1)S(1)}, bf16[192,1024]{1,0:T(8,128)(2,1)}, u32[]{:S(2)}) copy-start(bf16[192,1024]{1,0:T(8,128)(2,1)} %get-tuple-element.81) | copy-start | bytes 1179652
  336.9 4.2 %copy-start.3 = (bf16[192,256]{1,0:T(8,128)(2,1)S(1)}, bf16[192,256]{1,0:T(8,128)(2,1)}, u32[]{:S(2)}) copy-start(bf16[192,256]{1,0:T(8,128)(2,1)} %get-tuple-element.80) | copy-start | bytes 294916
  336.9 9.0 %copy-start.1 = (bf16[512,1024]{1,0:T(8,128)(2,1)S(1)}, bf16[512,1024]{1,0:T(8,128)(2,1)}, u32[]{:S(2)}) copy-start(bf16[512,1024]{1,0:T(8,128)(2,1)} %get-tuple-element.110) | copy-start | bytes 3145732
  338.2 8.6 %copy-start = (f32[512,1024]{1,0:T(8,128)S(1)}, f32[512,1024]{1,0:T(8,128)}, u32[]{:S(2)}) copy-start(f32[512,1024]{1,0:T(8,128)} %get-tuple-element.111) | copy-start | bytes 6291460

commit v5 on v4

--- a/solution.py
+++ b/solution.py
@@ -122,11 +122,14 @@
         return (z, self.seq)
 
 
-def meet(peers):
+def greet(peers):
     barrier = pltpu.get_barrier_semaphore()
     for peer in peers:
         pl.semaphore_signal(barrier, inc=1, device_id=peer, device_id_type=MESH)
-    pl.semaphore_wait(barrier, len(peers))
+
+
+def met(count):
+    pl.semaphore_wait(pltpu.get_barrier_semaphore(), count)
 
 
 GOT = ("X", "Y", "D1", "D2", "SO", "SX", "SY", "S1", "S2")
@@ -567,32 +570,32 @@
 KINDS = (0, 1, 0, 0, 2, 1, 0)
 FETCHES = (
     (
-        ((0, 1),),
-        ((0, 0),),
-        ((0, 2), (1, 1), (2, 1), (1, 0), (2, 0), (1, 2), (2, 2), (3, 1), (4, 1), (0, 5), (0, 4), (3, 0), (4, 0), (3, 2), (4, 2),),
+        ((0, 1), (0, 0),),
+        ((0, 2),),
+        ((1, 1), (2, 1), (1, 0), (2, 0), (1, 2), (2, 2), (3, 1), (4, 1), (0, 5), (0, 4), (3, 0), (4, 0), (3, 2), (4, 2),),
         (),
         (),
         (),
         ((0, 3),),
-        ((1, 4), (1, 5), (2, 5),),
-        (),
-        (),
+        ((1, 5), (2, 5),),
+        (),
+        ((1, 4),),
         ((1, 3), (2, 3),),
-        ((0, 6), (2, 4),),
+        (),
         ((3, 5), (4, 5),),
-        ((3, 3), (4, 3),),
+        ((3, 3), (4, 3), (0, 6),),
+        ((2, 4),),
+        (),
         ((3, 4),),
         (),
         (),
-        ((4, 4),),
-        (),
-        (),
-        ((1, 6), (2, 6),),
+        ((4, 4), (1, 6), (2, 6),),
         (),
         (),
         (),
         (),
         ((3, 6), (4, 6),),
+        (),
         (),
         (),
         (),
@@ -602,29 +605,29 @@
         (),
     ),
     (
-        ((0, 0), (0, 1), (0, 4),),
-        (),
-        ((1, 0), (2, 0), (1, 1), (0, 2), (0, 5), (1, 4), (2, 4), (2, 1), (3, 0), (4, 0), (3, 1), (1, 2), (2, 2),),
-        ((4, 1), (0, 3),),
-        (),
-        ((3, 4), (4, 4), (3, 2), (4, 2),),
-        ((0, 6),),
-        (),
+        ((0, 0), (0, 2), (0, 1),),
+        (),
+        ((1, 0), (2, 0), (1, 2), (2, 2), (0, 4), (0, 5), (3, 0), (4, 0), (3, 2), (4, 2), (1, 1),),
+        (),
+        ((2, 1), (0, 3), (3, 1), (1, 4), (2, 4), (4, 1),),
         ((1, 3), (2, 3),),
         (),
         (),
+        ((3, 4), (4, 4),),
+        ((3, 3), (4, 3), (0, 6),),
+        (),
+        (),
         ((1, 5),),
+        (),
+        (),
         ((1, 6), (2, 6),),
         (),
-        ((3, 3), (4, 3),),
-        (),
+        (),
+        ((2, 5),),
         ((3, 6), (4, 6),),
-        ((2, 5),),
-        (),
         (),
         (),
         ((3, 5),),
-        (),
         (),
         (),
         ((4, 5),),
@@ -639,7 +642,7 @@
 )
 
 
-def forward_call(lengths, tokens, small_own, shards):
+def forward_call(tokens, small_own, shards):
     rows, width = tokens.shape
     lru = shards[0].shape[1]
     ff = shards[4].shape[1]
@@ -650,7 +653,7 @@
     shape = jax.ShapeDtypeStruct
     wholes = [shape((8 * s.shape[0], s.shape[1]), s.dtype) for s in shards]
     saved = dict(
-        mixed=shape((rows, width), bf),
+        hidden=shape((rows, ff), bf),
         small=shape((16, lru), f32),
         n1t=shape((width, rows), bf),
         pre=shape((tiles, rows, LANES), f32),
@@ -710,7 +713,7 @@
     keys = list(scratch)
     R = 128
 
-    def kernel(lengths_ref, tokens_ref, small_ref, *refs):
+    def kernel(tokens_ref, small_ref, *refs):
         ins, outs = refs[:count], refs[count : 2 * count]
         out = named(names, refs[2 * count : 2 * count + len(names)])
         bounce = refs[-count:]
@@ -725,9 +728,9 @@
             pltpu.make_async_copy(tokens_ref, v.x, v.load.at[0]),
             pltpu.make_async_copy(small_ref, v.parts.at[seq], v.load.at[1]),
         ]
+        greet([(z, (seq + d) % 8) for d in range(1, 8)] + [gather.znb])
         for cp in loads:
             cp.start()
-        meet([(z, (seq + d) % 8) for d in range(1, 8)] + [gather.znb])
         kept = []
 
         def keep(src, dst):
@@ -768,6 +771,7 @@
             return at_place
 
         loads[1].wait()
+        met(8)
         packs.share()
         pump()
         packs.shared()
@@ -983,20 +987,7 @@
         )(mvalue_w, out.mg, out.bend, out.mv, out.hidt)
         pump()
         gather.arrive(6)
-        valid_rows = lengths_ref[z] - seq * rows
-
-        def down(w, mixed):
-            t = pl.program_id(0)
-            at = pl.ds(pl.multiple_of(t * 256, 256), 256)
-            valid = (lax.broadcasted_iota(jnp.int32, (rows, 256), 0) < valid_rows).astype(f32)
-            mixed[...] = low((v.resid[:, at] + dot(v.hidden[...], w[...])) * valid)
-
-        pltpu.emit_pipeline(
-            down,
-            grid=(width // 256,),
-            in_specs=[pl.BlockSpec((ff, 256), lambda t: (0, t))],
-            out_specs=[pl.BlockSpec((rows, 256), lambda t: (0, t))],
-        )(mdown_w, out.mixed)
+        keep(v.hidden, out.hidden)
         for cp in kept:
             cp.wait()
         pump()
@@ -1016,16 +1007,15 @@
     result = pl.pallas_call(
         kernel,
         out_shape=wholes + [saved[name] for name in names],
-        in_specs=[pl.BlockSpec(memory_space=pltpu.SMEM), HBM, HBM] + [HBM] * count,
+        in_specs=[HBM] * (2 + count),
         out_specs=[HBM] * (count + len(names)),
         scratch_shapes=[scratch[key] for key in keys] + [pltpu.VMEM(s.shape, s.dtype) for s in shards],
         compiler_params=pltpu.CompilerParams(collective_id=1, has_side_effects=True, vmem_limit_bytes=60 << 20),
         name="forward",
-    )(lengths, tokens, small_own, *shards)
+    )(tokens, small_own, *shards)
     return result[:count], named(names, result[count:])
 
-def slot_scratch(rows, columns):
-    n, h = rows // 8, columns // 2
+def slot_scratch(n, h):
     bf = jnp.bfloat16
     return dict(
         ab=pltpu.VMEM((2, 4, n, h), bf),
@@ -1042,57 +1032,79 @@
     (),
     (),
     (),
-    (),
-    (),
     ((6, 0, 0),),
     ((6, 0, 1),),
     (),
     (),
     (),
     (),
-    (),
     ((6, 1, 0),),
+    ((6, 1, 1),),
+    (),
+    ((0, 0, 0), (0, 0, 1),),
+    (),
+    (),
+    (),
+    (),
+    ((0, 1, 0), (0, 1, 1),),
+    ((6, 2, 0),),
     ((6, 2, 1),),
-    (),
-    (),
-    (),
-    ((0, 0, 0), (0, 0, 1),),
-    (),
-    (),
-    (),
-    (),
-    (),
-    ((0, 1, 0), (6, 2, 0), (0, 2, 1),),
-    (),
-    (),
-    ((1, 0, 1),),
-    ((1, 0, 0), (6, 1, 1),),
-    (),
-    (),
-    (),
+    ((1, 0, 1), (6, 4, 0),),
+    ((1, 0, 0), (6, 4, 1),),
+    (),
+    (),
+    (),
+    ((1, 1, 1),),
     ((2, 0, 1), (1, 1, 0),),
-    ((0, 2, 0), (6, 3, 0), (2, 0, 0),),
-    (),
-    (),
-    ((3, 0, 1),),
-    ((1, 2, 1),),
-    ((2, 1, 0), (6, 3, 1), (0, 1, 1), (3, 0, 0),),
-    ((0, 3, 0),),
-    ((6, 4, 0),),
-    ((1, 2, 0), (2, 2, 1),),
-    ((4, 0, 1),),
-    ((6, 4, 1),),
-    ((4, 0, 0), (1, 1, 1), (0, 3, 1),),
-    ((3, 1, 0), (2, 2, 0), (1, 3, 0),),
-    ((3, 2, 1), (6, 6, 0), (6, 6, 1), (0, 4, 0),),
-    (),
-    (),
-    ((2, 1, 1), (1, 3, 1), (0, 6, 0), (0, 4, 1), (0, 6, 1), (4, 1, 0), (3, 2, 0), (2, 3, 0),),
-    ((1, 4, 0), (1, 6, 0),),
-    ((2, 3, 1), (6, 5, 0), (1, 4, 1), (1, 6, 1),),
-    ((6, 5, 1),),
-    ((4, 2, 1), (3, 1, 1),),
-    ((2, 4, 0), (2, 6, 0), (3, 3, 0), (2, 4, 1), (2, 6, 1), (0, 5, 0), (4, 2, 0), (0, 5, 1), (3, 3, 1), (4, 1, 1), (1, 5, 0), (1, 5, 1), (4, 3, 0), (3, 4, 0), (3, 6, 0), (2, 5, 0), (3, 4, 1), (3, 6, 1), (4, 3, 1), (2, 5, 1), (4, 4, 0), (3, 5, 0), (4, 6, 0), (4, 4, 1), (3, 5, 1), (4, 6, 1), (4, 5, 0), (4, 5, 1), (5, 0, 0), (5, 0, 1), (5, 1, 0), (5, 2, 0), (5, 2, 1), (5, 3, 0), (5, 1, 1), (5, 4, 0), (5, 6, 0), (5, 3, 1), (5, 5, 0), (5, 4, 1), (5, 6, 1), (5, 5, 1),),
+    ((2, 0, 0),),
+    ((6, 3, 0),),
+    ((0, 2, 0), (6, 3, 1), (3, 0, 1), (0, 2, 1), (2, 1, 1),),
+    (),
+    (),
+    ((2, 1, 0), (3, 0, 0),),
+    ((4, 0, 1), (6, 5, 0), (6, 5, 1), (0, 4, 0), (0, 4, 1), (3, 1, 1),),
+    ((4, 0, 0), (1, 2, 0), (3, 1, 0),),
+    ((4, 1, 1), (0, 3, 0),),
+    (),
+    ((2, 2, 0), (4, 1, 0), (1, 2, 1), (0, 3, 1),),
+    (),
+    ((3, 2, 0), (2, 2, 1),),
+    ((0, 5, 0), (0, 5, 1),),
+    (),
+    ((4, 2, 0), (1, 4, 1), (1, 4, 0),),
+    ((1, 3, 1), (6, 6, 0), (6, 6, 1), (1, 3, 0), (3, 2, 1), (2, 4, 1),),
+    ((2, 4, 0), (1, 5, 1), (1, 5, 0), (4, 2, 1), (3, 4, 1),),
+    (),
+    (),
+    ((2, 3, 1), (0, 6, 0), (0, 6, 1), (3, 4, 0), (2, 3, 0),),
+    ((4, 4, 1),),
+    ((2, 5, 1), (1, 6, 0), (1, 6, 1), (3, 3, 1),),
+    ((4, 4, 0), (2, 5, 0), (3, 3, 0),),
+    ((6, 7, 0),),
+    ((6, 7, 1),),
+    ((4, 3, 1), (3, 5, 1), (2, 6, 0),),
+    (),
+    ((4, 3, 0), (2, 6, 1), (3, 5, 0),),
+    ((4, 5, 1), (0, 7, 0), (0, 7, 1),),
+    ((6, 10, 0), (6, 10, 1),),
+    ((3, 6, 1),),
+    ((3, 6, 0),),
+    (),
+    (),
+    ((1, 7, 0), (6, 8, 0), (4, 5, 0), (1, 7, 1), (0, 10, 1),),
+    ((0, 10, 0), (6, 8, 1),),
+    ((4, 6, 1), (6, 9, 0),),
+    ((6, 9, 1),),
+    ((4, 6, 0), (1, 10, 0),),
+    ((2, 7, 0),),
+    ((1, 10, 1), (0, 8, 0),),
+    ((2, 7, 1), (2, 10, 0), (0, 8, 1), (2, 10, 1), (0, 9, 0),),
+    ((0, 9, 1), (3, 7, 0), (3, 10, 0),),
+    ((1, 8, 0), (1, 8, 1), (3, 7, 1), (1, 9, 0), (1, 9, 1), (3, 10, 1),),
+    (),
+    ((4, 7, 0), (2, 8, 0), (4, 10, 0),),
+    ((4, 7, 1), (4, 10, 1), (2, 8, 1), (2, 9, 0),),
+    ((2, 9, 1), (3, 8, 0), (3, 9, 0), (3, 8, 1), (3, 9, 1), (4, 8, 0), (4, 8, 1), (4, 9, 0), (4, 9, 1), (5, 0, 0), (5, 0, 1), (5, 1, 0), (5, 1, 1), (5, 2, 0), (5, 2, 1), (5, 4, 0), (5, 4, 1), (5, 3, 0), (5, 3, 1), (5, 5, 0), (5, 5, 1), (5, 6, 0), (5, 6, 1), (5, 7, 0), (5, 10, 0), (5, 7, 1), (5, 10, 1), (5, 8, 0), (5, 9, 0), (5, 8, 1), (5, 9, 1),),
 )
 
 
@@ -1104,20 +1116,22 @@
     wide_tile = 2 * LANES
     f32, bf = jnp.float32, jnp.bfloat16
     shape = jax.ShapeDtypeStruct
-    DOWN, MGATE, MVALUE, OUTPUT, GELU, INPUT, GATES = range(7)
     full = [mdown_full, mgate_full, mvalue_full, output_full, gelu_full, input_full, gates_full]
-    extents = [w.shape for w in full]
-    count = len(full)
+    cut = lambda k, *shares: [(k, full[k].shape[1] * a // 6, full[k].shape[1] * (b - a) // 6) for a, b in zip((0,) + shares, shares + (6,))]
+    pieces = cut(0, 3) + cut(1, 3) + cut(2, 3) + cut(3) + cut(4) + cut(5, 4) + cut(6)
+    DOWN, DOWN2, MGATE, MGATE2, MVALUE, MVALUE2, OUTPUT, GELU, INPUT, INPUT2, GATES = range(11)
+    extents = [(full[k].shape[0] // 8, columns // 2) for k, _, columns in pieces]
+    count = len(pieces)
     split = lambda v: v.reshape(4, 2, v.shape[0] // 8, v.shape[1])
     inputs = dict(
         tokens=tokens, cot=cotangent, gelu_w=gelu_full, input_w=input_full, gates_w=gates_full, output_w=output_full, mgate_w=mgate_full,
         mvalue_w=mvalue_full, mdown_w=mdown_full, small=saved.small, n1t=split(saved.n1t), pre=saved.pre, lin=saved.lin,
         convt=saved.convt, decay=saved.decay, k6=saved.k6, k2=saved.k2, k3=saved.k3, k7=saved.k7, slope=saved.slope,
-        rect=split(saved.rect), resid=saved.resid, n2t=split(saved.n2t), mg=saved.mg, mv=saved.mv, hidt=split(saved.hidt),
-    )
-    slot_keys = list(slot_scratch(8, 256))
-    most = max(4 * (r // 8) * (c // 2) // wide_tile for r, c in extents)
-    passes = 13
+        rect=split(saved.rect), resid=saved.resid, n2t=split(saved.n2t), mg=saved.mg, mv=saved.mv, hidt=split(saved.hidt), hidden=saved.hidden,
+    )
+    slot_keys = list(slot_scratch(8, 128))
+    most = max(4 * n * h // wide_tile for n, h in extents)
+    passes, depth = 2 * count - 1, 4
     scratch = dict(
         go=pltpu.VMEM((rows, width), bf),
         gm=pltpu.VMEM((rows, width), bf),
@@ -1127,12 +1141,13 @@
         rect=pltpu.VMEM((4, 2, lru // 8, rows), bf),
         small=pltpu.VMEM((16, lru), f32),
         part=pltpu.VMEM((16, lru), f32),
+        own=pltpu.VMEM((16, wide_tile), f32),
         gain=pltpu.VMEM((8, width), f32),
         into=pltpu.VMEM((tiles, 8, LANES), f32),
         halo=pltpu.VMEM((tiles, 8, LANES), f32),
         edge=pltpu.VMEM((tiles, 8, LANES), f32),
-        stage=pltpu.VMEM((2, most, wide_tile), bf),
-        landed=pltpu.VMEM((2, most, wide_tile), bf),
+        stage=pltpu.VMEM((depth, most, wide_tile), bf),
+        landed=pltpu.VMEM((depth, most, wide_tile), bf),
         gstage=pltpu.VMEM((4, 2, lru // 8, wide_tile), bf),
         ends=pltpu.VMEM((8, 2, tiles, LANES), f32),
         sslots=pltpu.VMEM((2, 5, 16, lru), f32),
@@ -1147,13 +1162,13 @@
         ssend=pltpu.SemaphoreType.DMA((5,)),
         srecv=pltpu.SemaphoreType.DMA((5,)),
         load=pltpu.SemaphoreType.DMA((8,)),
-        keep=pltpu.SemaphoreType.DMA((count + 1, 2)),
+        keep=pltpu.SemaphoreType.DMA((count + 2, 2)),
         credit=pltpu.SemaphoreType.REGULAR,
     )
     keys = list(scratch)
-    outs = dict(tokens_grad=shape((rows, width), f32), small_sum=shape((16, lru), f32))
+    outs = dict(mixed=shape((rows, width), bf), tokens_grad=shape((rows, width), f32), small_sum=shape((16, wide_tile), f32))
     out_keys = list(outs)
-    sums = [shape((r // 8, c), bf) for r, c in extents]
+    sums = [shape((w.shape[0] // 8, w.shape[1]), bf) for w in full]
 
     def kernel(lengths_ref, *refs):
         refs = list(refs)
@@ -1165,12 +1180,12 @@
 
         w = named(inputs, take(len(inputs)))
         out = named(out_keys, take(len(out_keys)))
-        sum_refs = take(count)
+        sum_refs = take(len(full))
         v = named(keys, take(len(keys)))
         slots = []
-        for i, (r, c) in enumerate(extents):
+        for (k, first, _), (n, h) in zip(pieces, extents):
             s = named(slot_keys, take(len(slot_keys)))
-            s.n, s.h, s.tiles = r // 8, c // 2, c // 2 // wide_tile
+            s.n, s.h, s.tiles, s.first, s.sum = n, h, h // wide_tile, first, sum_refs[k]
             slots.append(s)
         place = Place()
         z, seq, core = place.z, place.seq, place.core
@@ -1185,13 +1200,13 @@
             cp.start()
             return cp
 
+        greet([(z, (seq + d) % 8) for d in range(1, 8)] + [((z + d) % 4, seq) for d in range(1, 4)])
         first_loads = [load(w.cot, v.go, 0)]
         loads = [load(w.small, v.small, 1), load(w.n2t, v.n2t, 2), load(w.rect, v.rect, 3), load(w.n1t, v.n1t, 4)]
 
         def arrived(i, h):
             red.arrive(i, h)
-            s = slots[i]
-            cp = pltpu.make_async_copy(s.res.at[h], sum_refs[i].at[:, pl.ds(side(i, h) * s.h, s.h)], v.keep.at[i, h])
+            cp = totalled(i, h)
 
             @pl.when(red.outer)
             def _():
@@ -1199,7 +1214,7 @@
 
         def totalled(i, h):
             s = slots[i]
-            return pltpu.make_async_copy(s.res.at[h], sum_refs[i].at[:, pl.ds(side(i, h) * s.h, s.h)], v.keep.at[i, h])
+            return pltpu.make_async_copy(s.res.at[h], s.sum.at[:, pl.ds(s.first + h * s.h, s.h)], v.keep.at[i, h])
 
         def add_peer(i, h):
             red.add_peer(i, h)
@@ -1239,66 +1254,76 @@
 
             return at_step
 
-        def to_sib(k, used):
+        sent = []
+        pass_of = {}
+
+        def to_sib(k):
             return pltpu.make_async_remote_copy(
-                src_ref=v.stage.at[k % 2, pl.ds(0, used)], dst_ref=v.landed.at[k % 2, pl.ds(0, used)], send_sem=v.psend.at[k],
-                recv_sem=v.precv.at[k], device_id=place.sib, device_id_type=MESH,
+                src_ref=v.stage.at[k % depth, pl.ds(0, sent[k])], dst_ref=v.landed.at[k % depth, pl.ds(0, sent[k])],
+                send_sem=v.psend.at[k], recv_sem=v.precv.at[k], device_id=place.sib, device_id_type=MESH,
             )
 
-        sent = {}
-
-        def send_blocks(k, used):
-            if k >= 2:
+        def next_pass():
+            k = len(sent)
+            if k >= depth:
+                to_sib(k - depth).wait_send()
+            return k
+
+        def send_blocks(used):
+            k = len(sent)
+            sent.append(used)
+            if k == 0:
+                met(10)
+            if k >= depth:
                 pl.semaphore_wait(v.credit, 1)
-            sent[k] = used
-            to_sib(k, used).start()
-
-        def free_stage(k):
-            if k >= 2:
-                to_sib(k - 2, sent[k - 2]).wait_send()
+            to_sib(k).start()
 
         def give_credit(k):
-            if k + 2 < passes:
+            if k + depth < passes:
                 pl.semaphore_signal(v.credit, inc=1, device_id=place.sib, device_id_type=MESH)
-
-        def side(i, h):
-            return 1 - h if i == MVALUE else h
 
         def blocks(s):
             group = max(1, 512 // s.n)
             return [(j, group) for j in range(0, 4, group)]
 
-        def for_sib(k, i, h, left, right):
-            pump()
+        def right_tile(s, h, right, t):
+            return right[:, pl.ds(pl.multiple_of(s.first + h * s.h + t * wide_tile, wide_tile), wide_tile)]
+
+        def for_sib(i, left, right):
             s = slots[i]
-            free_stage(k)
-
-            @pl.loop(0, s.tiles)
-            def _(t):
-                r = right[:, pl.ds(pl.multiple_of((side(i, h) * s.tiles + t) * wide_tile, wide_tile), wide_tile)]
-                for j, group in blocks(s):
-                    value = dot(left[j : j + group, 1 - core].reshape(group * s.n, rows), r)
-                    at = pl.ds(pl.multiple_of(t * 4 * s.n + j * s.n, s.n), group * s.n)
-                    v.stage[k % 2, at, :] = low(value)
-
-            send_blocks(k, 4 * s.n * s.tiles)
-
-        def for_us(k, i, h, left, right):
-            pump()
+            for h in range(2):
+                pump()
+                k = next_pass()
+                pass_of[i, h] = k
+
+                @pl.loop(0, s.tiles)
+                def _(t, h=h, k=k):
+                    r = right_tile(s, h, right, t)
+                    for j, group in blocks(s):
+                        value = dot(left[j : j + group, 1 - core].reshape(group * s.n, rows), r)
+                        at = pl.ds(pl.multiple_of(t * 4 * s.n + j * s.n, s.n), group * s.n)
+                        v.stage[k % depth, at, :] = low(value)
+
+                send_blocks(4 * s.n * s.tiles)
+
+        def for_us(i, left, right):
             s = slots[i]
-            to_sib(k, sent[k]).wait_recv()
-
-            @pl.loop(0, s.tiles)
-            def _(t):
-                r = right[:, pl.ds(pl.multiple_of((side(i, h) * s.tiles + t) * wide_tile, wide_tile), wide_tile)]
-                for j, group in blocks(s):
-                    value = dot(left[j : j + group, core].reshape(group * s.n, rows), r)
-                    at = pl.ds(pl.multiple_of(t * 4 * s.n + j * s.n, s.n), group * s.n)
-                    both = low(value + wide(v.landed[k % 2, at, :]))
-                    lane = pl.ds(pl.multiple_of(t * wide_tile, wide_tile), wide_tile)
-                    s.ab[h, j : j + group, :, lane] = both.reshape(group, s.n, wide_tile)
-
-            give_credit(k)
+            for h in range(2):
+                pump()
+                k = pass_of[i, h]
+                to_sib(k).wait_recv()
+
+                @pl.loop(0, s.tiles)
+                def _(t, h=h, k=k):
+                    r = right_tile(s, h, right, t)
+                    for j, group in blocks(s):
+                        value = dot(left[j : j + group, core].reshape(group * s.n, rows), r)
+                        at = pl.ds(pl.multiple_of(t * 4 * s.n + j * s.n, s.n), group * s.n)
+                        both = low(value + wide(v.landed[k % depth, at, :]))
+                        lane = pl.ds(pl.multiple_of(t * wide_tile, wide_tile), wide_tile)
+                        s.ab[h, j : j + group, :, lane] = both.reshape(group, s.n, wide_tile)
+
+                give_credit(k)
 
         def eight(value):
             return value.reshape(value.shape[0] // 8, 8, value.shape[1]).sum(axis=0)
@@ -1310,22 +1335,20 @@
             m = jnp.mean(scaled * x, axis=-1, keepdims=True)
             return add + scale * (scaled - x * (scale * scale * m))
 
-        def mlp_half(gmg, gmv, half):
+        def mlp_steps(gmg, gmv, first, count_of, *inner):
             pump()
-            steps_half = ff // wide_tile // 2
-            inside = pumps_at(steps_half // 3, 2 * steps_half // 3)
+            inside = pumps_at(*inner)
 
             def body(md, value, slope):
                 inside()
-                t = pl.program_id(0) + half * steps_half
-                at = pl.ds(pl.multiple_of(t * wide_tile, wide_tile), wide_tile)
+                at = pl.ds(pl.multiple_of((pl.program_id(0) + first) * wide_tile, wide_tile), wide_tile)
                 gh = dot_t(v.go[...], md[...])
                 gmg[:, at] = low(gh * slope[...])
                 gmv[:, at] = low(gh * value[...])
 
-            across = pl.BlockSpec((rows, wide_tile), lambda t: (0, t + half * steps_half))
+            across = pl.BlockSpec((rows, wide_tile), lambda t: (0, t + first))
             pltpu.emit_pipeline(
-                body, grid=(steps_half,), in_specs=[pl.BlockSpec((wide_tile, width), lambda t: (t + half * steps_half, 0)), across, across]
+                body, grid=(count_of,), in_specs=[pl.BlockSpec((wide_tile, width), lambda t: (t + first, 0)), across, across]
             )(w.mdown_w, w.mg, w.mv)
 
         def mlp_norm_half(gmg, gmv, half):
@@ -1343,12 +1366,13 @@
                 w.mgate_w, w.mvalue_w
             )
 
+        valid_rows = lengths_ref[z] - seq * rows
+        third = ff // wide_tile // 6
+
         def mlp_phase(gmg, gmv):
             def head(hidt):
                 down_loads = load(w.hidt, hidt, 5)
-                meet([(z, (seq + d) % 8) for d in range(1, 8)] + [((z + d) % 4, seq) for d in range(1, 4)])
                 first_loads[0].wait()
-                valid_rows = lengths_ref[z] - seq * rows
 
                 def mask(at):
                     here = lax.broadcasted_iota(jnp.int32, (64, width), 0) + at.start < valid_rows
@@ -1357,25 +1381,26 @@
                 rows_loop(rows, mask, 64)
                 part[...] = jnp.zeros_like(part)
                 down_loads.wait()
-                for_sib(0, DOWN, 0, hidt, v.go)
-                for_sib(1, DOWN, 1, hidt, v.go)
-                mlp_half(gmg, gmv, 0)
-                for_us(0, DOWN, 0, hidt, v.go)
-                for_us(1, DOWN, 1, hidt, v.go)
+                for_sib(DOWN, hidt, v.go)
+                mlp_steps(gmg, gmv, 0, third)
+                for_us(DOWN, hidt, v.go)
+                for_sib(DOWN2, hidt, v.go)
+                mlp_steps(gmg, gmv, third, 2 * third, third)
+                for_us(DOWN2, hidt, v.go)
 
             pl.run_scoped(head, pltpu.VMEM((4, 2, ff // 8, rows), bf))
             for cp in loads:
                 cp.wait()
-            for_sib(2, MGATE, 0, v.n2t, gmg)
-            for_sib(3, MVALUE, 1, v.n2t, gmv)
-            mlp_half(gmg, gmv, 1)
-            for_us(2, MGATE, 0, v.n2t, gmg)
-            for_us(3, MVALUE, 1, v.n2t, gmv)
-            for_sib(4, MGATE, 1, v.n2t, gmg)
-            for_sib(5, MVALUE, 0, v.n2t, gmv)
+            for_sib(MGATE, v.n2t, gmg)
+            for_sib(MVALUE, v.n2t, gmv)
+            mlp_steps(gmg, gmv, 3 * third, 3 * third, third, 2 * third)
+            for_us(MGATE, v.n2t, gmg)
+            for_us(MVALUE, v.n2t, gmv)
+            for_sib(MGATE2, v.n2t, gmg)
+            for_sib(MVALUE2, v.n2t, gmv)
             mlp_norm_half(gmg, gmv, 0)
-            for_us(4, MGATE, 1, v.n2t, gmg)
-            for_us(5, MVALUE, 0, v.n2t, gmv)
+            for_us(MGATE2, v.n2t, gmg)
+            for_us(MVALUE2, v.n2t, gmv)
             mlp_norm_half(gmg, gmv, 1)
 
         pl.run_scoped(mlp_phase, pltpu.VMEM((rows, ff), bf), pltpu.VMEM((rows, ff), bf))
@@ -1397,8 +1422,7 @@
 
         def branch_phase(adj, prod, gg, gl, gri):
             decay_load = load(w.decay, prod, 7)
-            for_sib(6, OUTPUT, 0, v.rect, v.gm)
-            for_sib(7, OUTPUT, 1, v.rect, v.gm)
+            for_sib(OUTPUT, v.rect, v.gm)
             pump()
 
             inside = pumps_at(tiles // 6, tiles // 3)
@@ -1417,8 +1441,7 @@
             pltpu.emit_pipeline(
                 into_branch, grid=(tiles // 2,), in_specs=[pl.BlockSpec((wide_tile, width), lambda t: (t, 0)), pair, pair]
             )(w.output_w, w.pre, w.slope)
-            for_us(6, OUTPUT, 0, v.rect, v.gm)
-            for_us(7, OUTPUT, 1, v.rect, v.gm)
+            for_us(OUTPUT, v.rect, v.gm)
             pump()
             decay_load.wait()
             tails = strided_scan(prod, adj, prod, adj, True, rows, pump)
@@ -1427,8 +1450,7 @@
             for c in range(tiles):
                 v.into[c] = before[c][1]
                 v.edge[c] = before[c][0]
-            for_sib(8, GELU, 0, v.n1t, gg)
-            for_sib(9, GELU, 1, v.n1t, gg)
+            for_sib(GELU, v.n1t, gg)
             pump()
             carry = ends.joined()
             for c in range(tiles):
@@ -1484,18 +1506,17 @@
             def _():
                 halo().start()
 
-            for_us(8, GELU, 0, v.n1t, gg)
+            for_us(GELU, v.n1t, gg)
             pump()
             s = slots[GATES]
-            free_stage(10)
+            gates_pass = next_pass()
             for j in range(4):
 
                 def copy_block(at, j=j):
-                    v.stage[0, pl.ds(pl.multiple_of(j * s.n + at.start, 16), 16), :] = v.gstage[j, 1 - core, at, :]
+                    v.stage[gates_pass % depth, pl.ds(pl.multiple_of(j * s.n + at.start, 16), 16), :] = v.gstage[j, 1 - core, at, :]
 
                 rows_loop(s.n, copy_block)
-            send_blocks(10, 4 * s.n)
-            for_us(9, GELU, 1, v.n1t, gg)
+            send_blocks(4 * s.n)
             pump()
 
             @pl.when(seq == 7)
@@ -1530,22 +1551,23 @@
                 through_conv, grid=(tiles,), in_specs=[pl.BlockSpec((None, rows + 8, LANES), lambda t: (t, 0, 0))]
             )(w.lin)
             pump()
-            to_sib(10, sent[10]).wait_recv()
+            to_sib(gates_pass).wait_recv()
             for j in range(4):
 
                 def fold(at, j=j):
-                    came = v.landed[0, pl.ds(pl.multiple_of(j * s.n + at.start, 16), 16), :]
+                    came = v.landed[gates_pass % depth, pl.ds(pl.multiple_of(j * s.n + at.start, 16), 16), :]
                     both = low(wide(v.gstage[j, core, at, :]) + wide(came))
                     s.ab[0, j, at, :] = both[:, : s.h]
                     s.ab[1, j, at, :] = both[:, s.h :]
 
                 rows_loop(s.n, fold)
-            give_credit(10)
-            for_sib(11, INPUT, 0, v.n1t, gl)
-            for_sib(12, INPUT, 1, v.n1t, gl)
+            give_credit(gates_pass)
+            for_sib(INPUT, v.n1t, gl)
+            for_sib(INPUT2, v.n1t, gl)
+            for_us(INPUT, v.n1t, gl)
+            for_us(INPUT2, v.n1t, gl)
             pump()
-
-            inside = pumps_at(width // wide_tile // 2)
+            inside = pumps_at(*range(1, width // wide_tile))
 
             def into_norm(wi, wg, inside=inside):
                 inside()
@@ -1557,8 +1579,6 @@
             pltpu.emit_pipeline(into_norm, grid=(width // wide_tile,), in_specs=[pl.BlockSpec((wide_tile, lru), lambda t: (t, 0))] * 2)(
                 w.input_w, w.gelu_w
             )
-            for_us(11, INPUT, 0, v.n1t, gl)
-            for_us(12, INPUT, 1, v.n1t, gl)
             pump()
             v.gain[...] = jnp.zeros_like(v.gain)
             tokens_load.wait()
@@ -1584,12 +1604,35 @@
         cp = pltpu.make_async_copy(v.gn, out.tokens_grad, v.keep.at[count, 0])
         cp.start()
         kept.append(cp)
-        last = PUMPS[turn[0]]
-        for k, (step, i, h) in enumerate(last):
+
+        def mixed_phase(hidden):
+            hidden_load = load(w.hidden, hidden, 7)
+            pump()
+            inside = pumps_at(*range(1, width // wide_tile))
+            hidden_load.wait()
+
+            def body(wd, resid, mixed):
+                inside()
+                valid = lax.broadcasted_iota(jnp.int32, (rows, wide_tile), 0) < valid_rows
+                mixed[...] = low(jnp.where(valid, resid[...] + dot(hidden[...], wd[...]), 0.0))
+
+            across = pl.BlockSpec((rows, wide_tile), lambda t: (0, t))
+            pltpu.emit_pipeline(
+                body, grid=(width // wide_tile,), in_specs=[pl.BlockSpec((ff, wide_tile), lambda t: (0, t)), across], out_specs=[across]
+            )(w.mdown_w, w.resid, out.mixed)
+
+        pl.run_scoped(mixed_phase, pltpu.VMEM((rows, ff), bf))
+        summed = 0
+        for k, (step, i, h) in enumerate(PUMPS[turn[0]]):
             steps[step](i, h)
-            if k % 4 == 3 and k < 20:
-                tot.step(k // 4)
-        cp = pltpu.make_async_copy(part, out.small_sum, v.keep.at[count, 1])
+            if k % 4 == 3 and summed < 5:
+                tot.step(summed)
+                summed += 1
+        for k in range(summed, 5):
+            tot.step(k)
+        v.own[0:8, :] = pltpu.roll(part[0:8, :], (8 - seq) % 8 * (lru // 8), axis=1)[:, :wide_tile]
+        v.own[8:16, :] = pltpu.roll(part[8:16, :], (lru - seq * (width // 8)) % lru, axis=1)[:, :wide_tile]
+        cp = pltpu.make_async_copy(v.own, out.small_sum, v.keep.at[count, 1])
         cp.start()
         kept.append(cp)
         for i in range(count):
@@ -1599,8 +1642,8 @@
             cp.wait()
         for i in range(count):
             red.drain(i)
-        for k in (passes - 2, passes - 1):
-            to_sib(k, sent[k]).wait_send()
+        for k in range(passes - depth, passes):
+            to_sib(k).wait_send()
         tot.drain()
         ends.drain()
 
@@ -1610,17 +1653,43 @@
                 src_ref=v.edge, dst_ref=v.halo, send_sem=v.hsend, recv_sem=v.hrecv, device_id=(z, (seq + 7) % 8), device_id_type=MESH
             ).wait_send()
 
-    slot_list = [value for r, c in extents for value in slot_scratch(r, c).values()]
+    slot_list = [value for n, h in extents for value in slot_scratch(n, h).values()]
     result = pl.pallas_call(
         kernel,
         out_shape=list(outs.values()) + sums,
         in_specs=[pl.BlockSpec(memory_space=pltpu.SMEM)] + [HBM] * len(inputs),
-        out_specs=[HBM] * (len(outs) + count),
+        out_specs=[HBM] * (len(outs) + len(full)),
         scratch_shapes=list(scratch.values()) + slot_list,
         compiler_params=pltpu.CompilerParams(collective_id=2, has_side_effects=True, vmem_limit_bytes=62 << 20),
         name="backward",
     )(lengths, *inputs.values())
-    return result[0], result[1], result[len(outs) :]
+    return result[: len(outs)], result[len(outs) :]
+
+
+def finish_call(plain, sums):
+    parts = 4
+    block = lambda v: pl.BlockSpec((v.shape[0] // parts, v.shape[1]), lambda t: (t, 0))
+    half = sums[-1].shape[1] // 2
+    ins = list(plain) + list(sums)
+    outs = [jax.ShapeDtypeStruct(v.shape, v.dtype) for v in plain] + [jax.ShapeDtypeStruct(v.shape, jnp.float32) for v in sums[:-1]]
+    outs += [jax.ShapeDtypeStruct((sums[-1].shape[0], half), jnp.float32)] * 2
+
+    def kernel(*refs):
+        src, dst = refs[: len(ins)], refs[len(ins) :]
+        for a, b in zip(src[:-1], dst):
+            b[...] = a[...].astype(b.dtype)
+        dst[-2][...] = wide(src[-1][:, :half])
+        dst[-1][...] = wide(src[-1][:, half:])
+
+    return pl.pallas_call(
+        kernel,
+        grid=(parts,),
+        out_shape=outs,
+        in_specs=[block(v) for v in ins],
+        out_specs=[block(v) for v in outs],
+        compiler_params=pltpu.CompilerParams(vmem_limit_bytes=60 << 20),
+        name="finish",
+    )(*ins)
 
 
 def local(
@@ -1903,34 +1972,30 @@
     mlp_down,
     cotangent,
 ):
-    block = rgate_weight.shape[1]
-    width_lru = input_weight.shape[1]
     lru_rows = jnp.concatenate(
         [conv_taps.T, conv_bias[None], rgate_bias[None], igate_bias[None], decay_param[None]], axis=0
     ).astype(jnp.float32)
     model_rows = jnp.stack([mixer_gain, mlp_gain]).astype(jnp.float32)
-    mine = lax.axis_index("seq")
     across = lambda value, columns: jnp.pad(value, ((0, 0), (0, columns - value.shape[1])))
     small = jnp.concatenate([across(lru_rows, 256), across(model_rows, 256), jnp.zeros((6, 256), jnp.float32)], axis=0)
     gates = jnp.concatenate([rgate_weight, igate_weight], axis=1)
     weights, saved = forward_call(
-        lengths, tokens, small, [gelu_weight, input_weight, gates, output_weight, mlp_gate, mlp_value, mlp_down]
-    )
-    tokens_grad, small_sum, big = backward_call(lengths, tokens, cotangent, weights, saved)
-    down, mgate, mvalue, out_w, gelu_w, input_w, gates = [value.astype(jnp.float32) for value in big]
-    lru_own = lax.dynamic_slice(small_sum, (0, mine * conv_bias.shape[0]), (8, conv_bias.shape[0]))
-    model_own = lax.dynamic_slice(small_sum, (8, mine * mixer_gain.shape[0]), (2, mixer_gain.shape[0]))
+        tokens, small, [gelu_weight, input_weight, gates, output_weight, mlp_gate, mlp_value, mlp_down]
+    )
+    (mixed, tokens_grad, small_sum), sums = backward_call(lengths, tokens, cotangent, weights, saved)
+    mixed, tokens_grad, down, mgate, mvalue, out_w, gelu_w, input_w, rgates, igates = finish_call([mixed, tokens_grad], sums)
+    lru_own, model_own = small_sum[:8, : conv_bias.shape[0]], small_sum[8:10, : mixer_gain.shape[0]]
     return (
-        saved.mixed,
+        mixed,
         tokens_grad,
         model_own[0],
         gelu_w,
         input_w,
         lru_own[:4].T,
         lru_own[4],
-        gates[:, :block],
+        rgates,
         lru_own[5],
-        gates[:, block:],
+        igates,
         lru_own[6],
         lru_own[7],
         out_w,

time: 351 us -> 334 us (0.952)
  other arithmetic: 12.1 us -> 2.84 us
  Pallas kernels: 325 us -> 320 us
    pallas_call x1, Pallas kernels: 194 us -> 179 us  [backward_call(): pl.pallas_call(kernel, out_shape=list(outs.values()) + sums, in_specs=[pl...]
    convert_element_type x6 -> x0, other arithmetic: 9.22 us -> none  [local_fast(): value.astype(jnp.float32)]
    pallas_call x0 -> x1, Pallas kernels: none -> 6.95 us  [finish_call(): pl.pallas_call(kernel, grid=(parts,), out_shape=outs, in_specs=[block(v)...]
where the time goes in v5:
time: 334 us; the launch traced here: 331 us
  Pallas kernels  320 us (96%)
  local copies, waits for them, and re-layouts  7.4 us (2%)
    pallas_call x1, Pallas kernels, backward_call(): pl.pallas_call(kernel, out_shape=list(outs.values()) + sums, in_specs=[pl...  179 us
    pallas_call x1, Pallas kernels, forward_call(): pl.pallas_call(kernel, out_shape=wholes + [saved[name] for name in names]...  133 us
    pallas_call x1, Pallas kernels, finish_call(): pl.pallas_call(kernel, grid=(parts,), out_shape=outs, in_specs=[block(v)...  6.95 us

profile of v5, /device:TPU:0, one launch (start us, length us, event | category | flops | bytes accessed | tf_op | source)
XLA Modules:
  0.0 330.6 jit_solution(10550241090530043132)
XLA Ops:
  0.7 0.1 pad.22.clone
  0.7 0.7 broadcast_in_dim.15
  1.4 0.7 broadcast_in_dim.16
  2.1 0.7 broadcast_in_dim.17
  2.7 0.7 broadcast_in_dim.18
  3.4 0.7 concatenate.9
  4.1 0.7 fusion.3
  4.8 0.7 maximum_maximum_fusion.small_ref
  5.4 1.5 pad_maximum_fusion.refs_2_
  6.9 133.2 %forward.1 = (bf16[1024,1536]{1,0:T(8,128)(2,1)}, bf16[1024,1536]{1,0:T(8,128)(2,1)}, bf16[1536,256]{1,0:T(8,128)(2,1)}, bf16[1536,1024]{1,0:T(8,128)(2,1)}, bf1...) custom-call(bf16[512,1024]{1,0:T(8,128)(2,1)} %refs_0_.3, ...), custom_call_target="tpu_custom_call" | custom-call | tf_op jit(solution)/shard_map/forward/pallas_call | solution.py:1007
  140.1 179.3 %backward.1 = (bf16[512,1024]{1,0:T(8,128)(2,1)}, f32[512,1024]{1,0:T(8,128)}, f32[16,256]{1,0:T(8,128)}, bf16[384,1024]{1,0:T(8,128)(2,1)}, bf16[128,3072]{1,0:...) custom-call(s32[4]{0:T(128)} %lengths_ref.1, ...), custom_call_target="tpu_custom_call" | custom-call | tf_op jit(solution)/shard_map/backward/pallas_call | solution.py:1657
  319.5 1.3 slice_bitcast_fusion.1
  320.8 1.3 slice_bitcast_fusion
  322.1 1.4 fusion.4
  323.5 6.9 %finish.1 = (bf16[512,1024]{1,0:T(8,128)(2,1)}, f32[512,1024]{1,0:T(8,128)}, f32[384,1024]{1,0:T(8,128)}, f32[128,3072]{1,0:T(8,128)}, f32[128,3072]{1,0:T(8,128...) custom-call(bf16[512,1024]{1,0:T(8,128)(2,1)} %get-tuple-element.87., ...), custom_call_target="tpu_custom_call" | custom-call | tf_op jit(solution)/shard_map/finish/pallas_call | solution.py:1684
  (2 shorter events, 0.0 us)

commit v6 on v5

--- a/solution.py
+++ b/solution.py
@@ -142,6 +142,7 @@
     def __init__(self, place, shards, fulls, kinds, send, recv, own, bounce):
         self.p, self.shards, self.fulls, self.bounce, self.kinds = place, shards, fulls, bounce, kinds
         self.send, self.recv, self.own = send, recv, own
+        self.held = [shard is buffer for shard, buffer in zip(shards, bounce)]
         self.znb = place.level(place.z + 1 - 2 * (place.z % 2))
 
     def fetched(self, i, odd):
@@ -200,7 +201,8 @@
             for c in self.own_far(i):
                 c.start()
         self.own_near(i).start()
-        self.own_kept(i, 0).start()
+        if not self.held[i]:
+            self.own_kept(i, 0).start()
 
     def onward(self, i, name, odd):
         p = self.p
@@ -220,7 +222,8 @@
         for c in self.onward(i, name, odd):
             c.start()
         if name == "X":
-            self.own_kept(i, 0).wait()
+            if not self.held[i]:
+                self.own_kept(i, 0).wait()
             self.own_kept(i, 1).start()
 
     def arrive(self, i):
@@ -465,14 +468,26 @@
     return jnp.maximum(-v, 0.0) + jnp.log1p(jnp.exp(-jnp.abs(v)))
 
 
-def strided_scan(decay_ref, value_ref, prod_ref, sum_ref, backward, rows, between):
+def interleave(rows, back):
+    span = rows // 8
+    shape = (8, span, rows) if back else (span, 8, rows)
+    major, minor, of = [lax.broadcasted_iota(jnp.int32, shape, d).astype(jnp.float32) for d in range(3)]
+    source = minor * (8.0 if back else float(span)) + major
+    return low(jnp.where(of == source, 1.0, 0.0)).reshape(rows, rows)
+
+
+def over_segments(value, tile):
+    return (value.reshape(value.shape[0] // 8, 8, value.shape[1]) * tile[None]).reshape(value.shape)
+
+
+def segment_scan(decay_ref, value_ref, prod_ref, sum_ref, backward, rows, between):
     tiles, _, lanes = sum_ref.shape
     span = rows // 8
 
     def step(k, carry):
         prod, total = carry
         t = span - 1 - k if backward else k
-        spot = pl.ds(t, 8, stride=span)
+        spot = pl.ds(pl.multiple_of(t * 8, 8), 8)
         new_prod, new_total = [], []
         for c in range(tiles):
             d, v = decay_ref[c, spot, :], value_ref[c, spot, :]
@@ -563,6 +578,7 @@
     return SimpleNamespace(**dict(zip(keys, refs)))
 
 
+RIM = 24
 HBM = pl.BlockSpec(memory_space=pl.ANY)
 VMEM = pl.BlockSpec(memory_space=pltpu.VMEM)
 
@@ -570,26 +586,26 @@
 KINDS = (0, 1, 0, 0, 2, 1, 0)
 FETCHES = (
     (
-        ((0, 1), (0, 0),),
-        ((0, 2),),
-        ((1, 1), (2, 1), (1, 0), (2, 0), (1, 2), (2, 2), (3, 1), (4, 1), (0, 5), (0, 4), (3, 0), (4, 0), (3, 2), (4, 2),),
+        ((0, 1),),
+        (),
+        ((0, 0), (0, 2), (1, 1), (2, 1), (1, 0), (2, 0), (1, 2), (2, 2), (3, 1), (4, 1), (0, 5), (0, 4), (3, 0), (4, 0), (3, 2), (4, 2),),
         (),
         (),
         (),
         ((0, 3),),
-        ((1, 5), (2, 5),),
-        (),
-        ((1, 4),),
+        ((1, 5), (2, 5), (1, 4),),
+        (),
+        (),
         ((1, 3), (2, 3),),
-        (),
+        ((2, 4), (0, 6),),
         ((3, 5), (4, 5),),
-        ((3, 3), (4, 3), (0, 6),),
-        ((2, 4),),
-        (),
+        ((3, 3), (4, 3),),
         ((3, 4),),
         (),
         (),
-        ((4, 4), (1, 6), (2, 6),),
+        ((4, 4),),
+        (),
+        ((1, 6), (2, 6),),
         (),
         (),
         (),
@@ -605,29 +621,29 @@
         (),
     ),
     (
-        ((0, 0), (0, 2), (0, 1),),
-        (),
-        ((1, 0), (2, 0), (1, 2), (2, 2), (0, 4), (0, 5), (3, 0), (4, 0), (3, 2), (4, 2), (1, 1),),
-        (),
-        ((2, 1), (0, 3), (3, 1), (1, 4), (2, 4), (4, 1),),
+        ((0, 0), (0, 1),),
+        (),
+        ((0, 4), (1, 0), (2, 0), (1, 1), (0, 2), (0, 5), (1, 4), (2, 4), (2, 1), (3, 0), (4, 0), (3, 1), (1, 2), (2, 2),),
+        ((4, 1),),
+        ((0, 3),),
+        ((3, 4), (4, 4), (3, 2), (4, 2),),
+        ((0, 6),),
+        (),
         ((1, 3), (2, 3),),
         (),
         (),
-        ((3, 4), (4, 4),),
-        ((3, 3), (4, 3), (0, 6),),
-        (),
-        (),
-        ((1, 5),),
-        (),
-        (),
-        ((1, 6), (2, 6),),
-        (),
-        (),
+        (),
+        ((1, 5), (1, 6), (2, 6),),
+        (),
+        ((3, 3), (4, 3),),
+        (),
+        ((3, 6), (4, 6),),
         ((2, 5),),
-        ((3, 6), (4, 6),),
+        (),
         (),
         (),
         ((3, 5),),
+        (),
         (),
         (),
         ((4, 5),),
@@ -642,22 +658,27 @@
 )
 
 
-def forward_call(tokens, small_own, shards):
+def forward_call(tokens, small_own, gate_weights, shards):
     rows, width = tokens.shape
     lru = shards[0].shape[1]
-    ff = shards[4].shape[1]
+    ff = shards[3].shape[1]
+    own = lambda v: jax.ShapeDtypeStruct(v.shape, v.dtype)
+    gates_own = jax.ShapeDtypeStruct((gate_weights[0].shape[0], 2 * LANES), gate_weights[0].dtype)
+    inputs = len(gate_weights) + len(shards)
+    shapes = [own(v) for v in shards[:2]] + [gates_own] + [own(v) for v in shards[2:]]
     tiles = lru // LANES
     kinds = KINDS
-    count = len(shards)
+    count = len(shapes)
     f32, bf = jnp.float32, jnp.bfloat16
     shape = jax.ShapeDtypeStruct
-    wholes = [shape((8 * s.shape[0], s.shape[1]), s.dtype) for s in shards]
+    wholes = [shape((8 * s.shape[0], s.shape[1]), s.dtype) for s in shapes]
     saved = dict(
         hidden=shape((rows, ff), bf),
+        x=shape((rows, width), bf),
         small=shape((16, lru), f32),
         n1t=shape((width, rows), bf),
         pre=shape((tiles, rows, LANES), f32),
-        lin=shape((tiles, rows + 8, LANES), f32),
+        lin=shape((tiles, rows + RIM, LANES), f32),
         convt=shape((tiles, LANES, rows), bf),
         decay=shape((tiles, rows, LANES), f32),
         k2=shape((tiles, rows, LANES), f32),
@@ -679,10 +700,12 @@
         n1=pltpu.VMEM((rows, width), bf),
         n1t=pltpu.VMEM((width, rows), bf),
         parts=pltpu.VMEM((8,) + small_own.shape, f32),
-        into=pltpu.VMEM((8 * tiles, LANES), f32),
+        into=pltpu.VMEM((tiles, 8, LANES), f32),
+        edge=pltpu.VMEM((tiles, 8, LANES), f32),
+        halo=pltpu.VMEM((tiles, 8, LANES), f32),
         small=pltpu.VMEM((16, lru), f32),
         pre=pltpu.VMEM((tiles, rows, LANES), f32),
-        lin=pltpu.VMEM((tiles, rows + 8, LANES), f32),
+        lin=pltpu.VMEM((tiles, rows + RIM, LANES), f32),
         convt=pltpu.VMEM((tiles, LANES, rows), bf),
         decay=pltpu.VMEM((tiles, rows, LANES), f32),
         k2=pltpu.VMEM((tiles, rows, LANES), f32),
@@ -707,17 +730,18 @@
         srecv=pltpu.SemaphoreType.DMA((7,)),
         hsend=pltpu.SemaphoreType.DMA(()),
         hrecv=pltpu.SemaphoreType.DMA(()),
-        load=pltpu.SemaphoreType.DMA((2,)),
+        load=pltpu.SemaphoreType.DMA((4,)),
         keep=pltpu.SemaphoreType.DMA((len(names),)),
     )
     keys = list(scratch)
     R = 128
 
     def kernel(tokens_ref, small_ref, *refs):
-        ins, outs = refs[:count], refs[count : 2 * count]
-        out = named(names, refs[2 * count : 2 * count + len(names)])
-        bounce = refs[-count:]
-        v = named(keys, refs[2 * count + len(names) : -count])
+        pair, given, refs = refs[:2], refs[2:inputs], refs[inputs:]
+        outs, bounce = refs[:count], refs[-count:]
+        ins = list(given[:2]) + [bounce[2]] + list(given[2:])
+        out = named(names, refs[count : count + len(names)])
+        v = named(keys, refs[count + len(names) : -count])
         gelu_w, input_w, gates_w, output_w, mgate_w, mvalue_w, mdown_w = outs
         place = Place()
         gather = Gather(place, ins, outs, kinds, v.gsend, v.grecv, v.gown, bounce)
@@ -725,9 +749,9 @@
         packs = Ends(place, v.parts, (v.ssend, v.srecv), False)
         z, seq = place.z, place.seq
         loads = [
-            pltpu.make_async_copy(tokens_ref, v.x, v.load.at[0]),
+            pltpu.make_async_copy(tokens_ref, v.n2, v.load.at[0]),
             pltpu.make_async_copy(small_ref, v.parts.at[seq], v.load.at[1]),
-        ]
+        ] + [pltpu.make_async_copy(pair[k], bounce[2].at[:, pl.ds(k * LANES, LANES)], v.load.at[2 + k]) for k in range(2)]
         greet([(z, (seq + d) % 8) for d in range(1, 8)] + [gather.znb])
         for cp in loads:
             cp.start()
@@ -770,10 +794,13 @@
 
             return at_place
 
-        loads[1].wait()
+        for cp in loads[1:]:
+            cp.wait()
         met(8)
         packs.share()
         pump()
+        loads[0].wait()
+        v.x[...] = low(dot(interleave(rows, False), v.n2[...]))
         packs.shared()
         small = v.small
         lane = lax.broadcasted_iota(jnp.int32, (8, LANES), 1)
@@ -787,7 +814,7 @@
             small[8:16, k * LANES : (k + 1) * LANES] = v.parts[k, 8:16, :LANES]
         small[8:16, width:] = jnp.zeros((8, lru - width), f32)
         keep(v.small, out.small)
-        loads[0].wait()
+        keep(v.x, out.x)
 
         def norm_one(at):
             x = wide(v.x[at, :])
@@ -823,13 +850,15 @@
         project(gelu_w, v.pre, 0)
         pump()
         gather.arrive(1)
-        project(input_w, v.lin, 8)
+        project(input_w, v.lin, RIM)
 
         def halo():
             return pltpu.make_async_remote_copy(
-                src_ref=v.lin.at[:, pl.ds(rows, 8)], dst_ref=v.lin.at[:, pl.ds(0, 8)], send_sem=v.hsend, recv_sem=v.hrecv,
-                device_id=(z, (seq + 1) % 8), device_id_type=MESH,
+                src_ref=v.edge, dst_ref=v.halo, send_sem=v.hsend, recv_sem=v.hrecv, device_id=(z, (seq + 1) % 8), device_id_type=MESH
             )
+
+        for k in range(3):
+            v.edge[:, k : k + 1, :] = v.lin[:, RIM + rows - 8 * k - 1 : RIM + rows - 8 * k, :]
 
         @pl.when(seq < 7)
         def _():
@@ -840,11 +869,19 @@
 
         @pl.when(seq == 0)
         def _():
-            v.lin[:, 0:8, :] = jnp.zeros((tiles, 8, LANES), f32)
+            v.halo[...] = jnp.zeros((tiles, 8, LANES), f32)
 
         @pl.when(seq > 0)
         def _():
             halo().wait_recv()
+
+        lowest = lax.broadcasted_iota(jnp.int32, (8, LANES), 0) == 0
+
+        @pl.loop(0, tiles)
+        def _(c):
+            for k in range(3):
+                tile = pltpu.roll(v.lin[c, RIM + rows - 8 * (k + 1) : RIM + rows - 8 * k, :], 1, axis=0)
+                v.lin[c, RIM - 8 * (k + 1) : RIM - 8 * k, :] = jnp.where(lowest, v.halo[c, k : k + 1, :], tile)
 
         keep(v.lin, out.lin)
 
@@ -858,9 +895,9 @@
             cb, rb, ib, dp = [small[k : k + 1, lane] for k in range(4, 8)]
             rate = -cfactor * softplus_minus(dp)
             for r in range(0, rows, R):
-                acc = cb + taps[0] * v.lin[h, 8 + r : 8 + r + R, :]
+                acc = cb + taps[0] * v.lin[h, RIM + r : RIM + r + R, :]
                 for k in range(1, 4):
-                    acc = acc + taps[k] * v.lin[h, 8 + r - k : 8 + r - k + R, :]
+                    acc = acc + taps[k] * v.lin[h, RIM + r - 8 * k : RIM + r - 8 * k + R, :]
                 cl = low(acc)
                 v.convt[h, :, r : r + R] = cl.T
                 both = dot(cl, w[...])
@@ -884,7 +921,7 @@
         for src, dst in ((v.convt, out.convt), (v.decay, out.decay), (v.k2, out.k2), (v.k3, out.k3)):
             keep(src, dst)
         pump()
-        tails = strided_scan(v.prod, v.total, v.prod, v.total, False, rows, pump)
+        tails = segment_scan(v.prod, v.total, v.prod, v.total, False, rows, pump)
         before, whole = segment_ends(tails, False)
         ends.tell(whole)
         pump()
@@ -892,7 +929,7 @@
         span = rows // 8
         for c in range(tiles):
             into = before[c][0] * carry[c : c + 1, :] + before[c][1]
-            v.into[8 * c : 8 * c + 8, :] = into
+            v.into[c] = into
 
         pump()
         state_inside = pumps_at(tiles // 3, 2 * tiles // 3)
@@ -901,13 +938,14 @@
         def _(c):
             state_inside(c)
             lane = pl.ds(pl.multiple_of(c * LANES, LANES), LANES)
-            into = v.into[pl.ds(pl.multiple_of(c * 8, 8), 8), :]
+            into = v.into[c]
             rate = -cfactor * softplus_minus(small[7:8, lane])
-            first = lax.broadcasted_iota(jnp.int32, (span, LANES), 0) == 0
+            last = into
             for s in range(8):
                 at = slice(s * span, (s + 1) * span)
-                state = v.total[c, at, :] + v.prod[c, at, :] * into[s : s + 1, :]
-                before_it = jnp.where(first, into[s : s + 1, :], pltpu.roll(state, 1, axis=0))
+                state = v.total[c, at, :] + over_segments(v.prod[c, at, :], into)
+                before_it = jnp.concatenate([last, state[:-8]], axis=0)
+                last = state[-8:]
                 rg = v.k7[c, at, :]
                 k7 = (before_it * v.decay[c, at, :] - v.k6[c, at, :]) * rg
                 v.k7[c, at, :] = k7
@@ -1007,12 +1045,12 @@
     result = pl.pallas_call(
         kernel,
         out_shape=wholes + [saved[name] for name in names],
-        in_specs=[HBM] * (2 + count),
+        in_specs=[HBM] * (2 + inputs),
         out_specs=[HBM] * (count + len(names)),
-        scratch_shapes=[scratch[key] for key in keys] + [pltpu.VMEM(s.shape, s.dtype) for s in shards],
+        scratch_shapes=[scratch[key] for key in keys] + [pltpu.VMEM(s.shape, s.dtype) for s in shapes],
         compiler_params=pltpu.CompilerParams(collective_id=1, has_side_effects=True, vmem_limit_bytes=60 << 20),
         name="forward",
-    )(tokens, small_own, *shards)
+    )(tokens, small_own, *gate_weights, *shards)
     return result[:count], named(names, result[count:])
 
 def slot_scratch(n, h):
@@ -1041,75 +1079,75 @@
     ((6, 1, 0),),
     ((6, 1, 1),),
     (),
+    (),
+    (),
     ((0, 0, 0), (0, 0, 1),),
     (),
     (),
     (),
-    (),
-    ((0, 1, 0), (0, 1, 1),),
     ((6, 2, 0),),
-    ((6, 2, 1),),
-    ((1, 0, 1), (6, 4, 0),),
-    ((1, 0, 0), (6, 4, 1),),
-    (),
-    (),
-    (),
-    ((1, 1, 1),),
+    ((0, 1, 0), (6, 2, 1), (0, 1, 1),),
+    ((6, 4, 0),),
+    ((6, 4, 1),),
+    (),
+    ((1, 0, 1),),
+    ((1, 0, 0),),
+    (),
+    (),
     ((2, 0, 1), (1, 1, 0),),
+    ((0, 2, 0),),
+    (),
+    ((6, 5, 0),),
     ((2, 0, 0),),
+    ((3, 0, 1), (6, 5, 1), (1, 1, 1), (0, 2, 1), (2, 1, 0),),
+    ((3, 0, 0),),
+    ((2, 1, 1), (0, 4, 0), (4, 0, 1), (0, 4, 1),),
+    ((4, 0, 0), (1, 2, 0), (3, 1, 0),),
+    (),
     ((6, 3, 0),),
-    ((0, 2, 0), (6, 3, 1), (3, 0, 1), (0, 2, 1), (2, 1, 1),),
-    (),
-    (),
-    ((2, 1, 0), (3, 0, 0),),
-    ((4, 0, 1), (6, 5, 0), (6, 5, 1), (0, 4, 0), (0, 4, 1), (3, 1, 1),),
-    ((4, 0, 0), (1, 2, 0), (3, 1, 0),),
-    ((4, 1, 1), (0, 3, 0),),
-    (),
-    ((2, 2, 0), (4, 1, 0), (1, 2, 1), (0, 3, 1),),
-    (),
-    ((3, 2, 0), (2, 2, 1),),
-    ((0, 5, 0), (0, 5, 1),),
-    (),
-    ((4, 2, 0), (1, 4, 1), (1, 4, 0),),
-    ((1, 3, 1), (6, 6, 0), (6, 6, 1), (1, 3, 0), (3, 2, 1), (2, 4, 1),),
-    ((2, 4, 0), (1, 5, 1), (1, 5, 0), (4, 2, 1), (3, 4, 1),),
-    (),
-    (),
-    ((2, 3, 1), (0, 6, 0), (0, 6, 1), (3, 4, 0), (2, 3, 0),),
-    ((4, 4, 1),),
-    ((2, 5, 1), (1, 6, 0), (1, 6, 1), (3, 3, 1),),
-    ((4, 4, 0), (2, 5, 0), (3, 3, 0),),
+    ((3, 1, 1), (6, 3, 1), (0, 5, 0),),
+    ((2, 2, 0), (1, 2, 1), (4, 1, 0), (0, 5, 1),),
+    ((1, 4, 1), (1, 4, 0), (4, 1, 1),),
+    (),
+    ((2, 2, 1), (3, 2, 0),),
+    (),
+    (),
+    ((2, 4, 1), (6, 6, 0), (0, 3, 0), (0, 3, 1), (3, 2, 1),),
+    (),
+    ((2, 4, 0), (6, 6, 1), (1, 5, 1), (1, 5, 0), (4, 2, 0),),
+    (),
+    ((1, 3, 0), (3, 4, 1), (4, 2, 1),),
+    ((2, 5, 1), (3, 4, 0), (0, 6, 0),),
     ((6, 7, 0),),
-    ((6, 7, 1),),
-    ((4, 3, 1), (3, 5, 1), (2, 6, 0),),
-    (),
-    ((4, 3, 0), (2, 6, 1), (3, 5, 0),),
-    ((4, 5, 1), (0, 7, 0), (0, 7, 1),),
+    ((2, 5, 0), (6, 7, 1), (1, 3, 1), (4, 4, 1), (0, 6, 1),),
+    ((3, 5, 1),),
+    ((2, 3, 0), (1, 6, 0),),
+    ((3, 5, 0), (4, 4, 0), (2, 3, 1),),
+    ((0, 7, 0), (4, 5, 1),),
     ((6, 10, 0), (6, 10, 1),),
-    ((3, 6, 1),),
-    ((3, 6, 0),),
-    (),
-    (),
-    ((1, 7, 0), (6, 8, 0), (4, 5, 0), (1, 7, 1), (0, 10, 1),),
-    ((0, 10, 0), (6, 8, 1),),
-    ((4, 6, 1), (6, 9, 0),),
-    ((6, 9, 1),),
-    ((4, 6, 0), (1, 10, 0),),
-    ((2, 7, 0),),
-    ((1, 10, 1), (0, 8, 0),),
-    ((2, 7, 1), (2, 10, 0), (0, 8, 1), (2, 10, 1), (0, 9, 0),),
-    ((0, 9, 1), (3, 7, 0), (3, 10, 0),),
-    ((1, 8, 0), (1, 8, 1), (3, 7, 1), (1, 9, 0), (1, 9, 1), (3, 10, 1),),
-    (),
-    ((4, 7, 0), (2, 8, 0), (4, 10, 0),),
-    ((4, 7, 1), (4, 10, 1), (2, 8, 1), (2, 9, 0),),
-    ((2, 9, 1), (3, 8, 0), (3, 9, 0), (3, 8, 1), (3, 9, 1), (4, 8, 0), (4, 8, 1), (4, 9, 0), (4, 9, 1), (5, 0, 0), (5, 0, 1), (5, 1, 0), (5, 1, 1), (5, 2, 0), (5, 2, 1), (5, 4, 0), (5, 4, 1), (5, 3, 0), (5, 3, 1), (5, 5, 0), (5, 5, 1), (5, 6, 0), (5, 6, 1), (5, 7, 0), (5, 10, 0), (5, 7, 1), (5, 10, 1), (5, 8, 0), (5, 9, 0), (5, 8, 1), (5, 9, 1),),
+    ((2, 6, 0),),
+    ((1, 6, 1), (4, 5, 0), (0, 7, 1), (3, 3, 0), (0, 10, 0),),
+    (),
+    (),
+    ((6, 8, 0),),
+    ((1, 7, 0), (6, 8, 1), (3, 3, 1), (3, 6, 0), (1, 10, 0), (0, 10, 1),),
+    ((2, 6, 1), (6, 9, 0),),
+    ((1, 7, 1), (6, 9, 1),),
+    ((4, 3, 0),),
+    ((2, 7, 0), (2, 10, 0), (4, 3, 1),),
+    ((4, 6, 0), (0, 8, 1), (1, 10, 1), (0, 8, 0),),
+    ((2, 7, 1), (2, 10, 1), (3, 6, 1), (3, 7, 0), (3, 10, 0), (0, 9, 1), (0, 9, 0), (1, 8, 1), (1, 8, 0),),
+    (),
+    ((3, 7, 1), (3, 10, 1), (1, 9, 1), (1, 9, 0), (4, 6, 1),),
+    ((2, 8, 1),),
+    ((2, 8, 0), (4, 7, 0), (4, 10, 0), (2, 9, 1), (4, 7, 1), (4, 10, 1), (2, 9, 0),),
+    ((3, 8, 1), (3, 9, 1), (3, 8, 0),),
+    ((3, 9, 0), (4, 8, 1), (4, 8, 0), (4, 9, 1), (4, 9, 0), (5, 0, 0), (5, 0, 1), (5, 1, 0), (5, 1, 1), (5, 2, 0), (5, 2, 1), (5, 4, 0), (5, 4, 1), (5, 5, 0), (5, 5, 1), (5, 3, 0), (5, 6, 0), (5, 3, 1), (5, 7, 0), (5, 10, 0), (5, 6, 1), (5, 7, 1), (5, 10, 1), (5, 8, 0), (5, 9, 0), (5, 8, 1), (5, 9, 1),),
 )
 
 
-def backward_call(lengths, tokens, cotangent, weights, saved):
-    rows, width = tokens.shape
+def backward_call(lengths, cotangent, weights, saved):
+    rows, width = cotangent.shape
     gelu_full, input_full, gates_full, output_full, mgate_full, mvalue_full, mdown_full = weights
     lru, ff = gelu_full.shape[1], mgate_full.shape[1]
     tiles = lru // LANES
@@ -1124,7 +1162,7 @@
     count = len(pieces)
     split = lambda v: v.reshape(4, 2, v.shape[0] // 8, v.shape[1])
     inputs = dict(
-        tokens=tokens, cot=cotangent, gelu_w=gelu_full, input_w=input_full, gates_w=gates_full, output_w=output_full, mgate_w=mgate_full,
+        x=saved.x, cot=cotangent, gelu_w=gelu_full, input_w=input_full, gates_w=gates_full, output_w=output_full, mgate_w=mgate_full,
         mvalue_w=mvalue_full, mdown_w=mdown_full, small=saved.small, n1t=split(saved.n1t), pre=saved.pre, lin=saved.lin,
         convt=saved.convt, decay=saved.decay, k6=saved.k6, k2=saved.k2, k3=saved.k3, k7=saved.k7, slope=saved.slope,
         rect=split(saved.rect), resid=saved.resid, n2t=split(saved.n2t), mg=saved.mg, mv=saved.mv, hidt=split(saved.hidt), hidden=saved.hidden,
@@ -1136,8 +1174,7 @@
         go=pltpu.VMEM((rows, width), bf),
         gm=pltpu.VMEM((rows, width), bf),
         gn=pltpu.VMEM((rows, width), f32),
-        n1t=pltpu.VMEM((4, 2, width // 8, rows), bf),
-        n2t=pltpu.VMEM((4, 2, width // 8, rows), bf),
+        normt=pltpu.VMEM((4, 2, width // 8, rows), bf),
         rect=pltpu.VMEM((4, 2, lru // 8, rows), bf),
         small=pltpu.VMEM((16, lru), f32),
         part=pltpu.VMEM((16, lru), f32),
@@ -1201,8 +1238,8 @@
             return cp
 
         greet([(z, (seq + d) % 8) for d in range(1, 8)] + [((z + d) % 4, seq) for d in range(1, 4)])
-        first_loads = [load(w.cot, v.go, 0)]
-        loads = [load(w.small, v.small, 1), load(w.n2t, v.n2t, 2), load(w.rect, v.rect, 3), load(w.n1t, v.n1t, 4)]
+        first_loads = [load(w.cot, v.gm, 0)]
+        loads = [load(w.small, v.small, 1), load(w.n2t, v.normt, 2), load(w.rect, v.rect, 3)]
 
         def arrived(i, h):
             red.arrive(i, h)
@@ -1374,11 +1411,9 @@
                 down_loads = load(w.hidt, hidt, 5)
                 first_loads[0].wait()
 
-                def mask(at):
-                    here = lax.broadcasted_iota(jnp.int32, (64, width), 0) + at.start < valid_rows
-                    v.go[at, :] = low(jnp.where(here, wide(v.go[at, :]), 0.0))
-
-                rows_loop(rows, mask, 64)
+                here = lax.broadcasted_iota(jnp.int32, (rows, width), 0) < valid_rows
+                v.gm[...] = low(jnp.where(here, wide(v.gm[...]), 0.0))
+                v.go[...] = low(dot(interleave(rows, False), v.gm[...]))
                 part[...] = jnp.zeros_like(part)
                 down_loads.wait()
                 for_sib(DOWN, hidt, v.go)
@@ -1391,16 +1426,16 @@
             pl.run_scoped(head, pltpu.VMEM((4, 2, ff // 8, rows), bf))
             for cp in loads:
                 cp.wait()
-            for_sib(MGATE, v.n2t, gmg)
-            for_sib(MVALUE, v.n2t, gmv)
+            for_sib(MGATE, v.normt, gmg)
+            for_sib(MVALUE, v.normt, gmv)
             mlp_steps(gmg, gmv, 3 * third, 3 * third, third, 2 * third)
-            for_us(MGATE, v.n2t, gmg)
-            for_us(MVALUE, v.n2t, gmv)
-            for_sib(MGATE2, v.n2t, gmg)
-            for_sib(MVALUE2, v.n2t, gmv)
+            for_us(MGATE, v.normt, gmg)
+            for_us(MVALUE, v.normt, gmv)
+            for_sib(MGATE2, v.normt, gmg)
+            for_sib(MVALUE2, v.normt, gmv)
             mlp_norm_half(gmg, gmv, 0)
-            for_us(MGATE2, v.n2t, gmg)
-            for_us(MVALUE2, v.n2t, gmv)
+            for_us(MGATE2, v.normt, gmg)
+            for_us(MVALUE2, v.normt, gmv)
             mlp_norm_half(gmg, gmv, 1)
 
         pl.run_scoped(mlp_phase, pltpu.VMEM((rows, ff), bf), pltpu.VMEM((rows, ff), bf))
@@ -1418,7 +1453,9 @@
 
         pltpu.emit_pipeline(norm_two, grid=(rows // 64,), in_specs=[pl.BlockSpec((64, width), lambda t: (t, 0))])(w.resid)
         part[9:10, :width] = v.gain[...].sum(axis=0, keepdims=True)
-        tokens_load = load(w.tokens, v.go, 6)
+        tokens_load = load(w.x, v.go, 6)
+
+        norm_load = load(w.n1t, v.normt, 4)
 
         def branch_phase(adj, prod, gg, gl, gri):
             decay_load = load(w.decay, prod, 7)
@@ -1444,13 +1481,14 @@
             for_us(OUTPUT, v.rect, v.gm)
             pump()
             decay_load.wait()
-            tails = strided_scan(prod, adj, prod, adj, True, rows, pump)
+            tails = segment_scan(prod, adj, prod, adj, True, rows, pump)
             before, whole = segment_ends(tails, True)
             ends.tell(whole)
             for c in range(tiles):
                 v.into[c] = before[c][1]
                 v.edge[c] = before[c][0]
-            for_sib(GELU, v.n1t, gg)
+            norm_load.wait()
+            for_sib(GELU, v.normt, gg)
             pump()
             carry = ends.joined()
             for c in range(tiles):
@@ -1466,7 +1504,7 @@
                 sums = [jnp.zeros((8, LANES), f32) for _ in range(3)]
                 for k in range(8):
                     at = slice(k * span, (k + 1) * span)
-                    here = adj[c, at, :] + prod[c, at, :] * v.into[c, k : k + 1, :]
+                    here = adj[c, at, :] + over_segments(prod[c, at, :], v.into[c])
                     grad_r = here * k6[at, :]
                     grad_i = here * k2[at, :]
                     adj[c, at, :] = here * k3[at, :]
@@ -1500,13 +1538,14 @@
                     src_ref=v.edge, dst_ref=v.halo, send_sem=v.hsend, recv_sem=v.hrecv, device_id=(z, (seq + 7) % 8), device_id_type=MESH
                 )
 
-            v.edge[...] = adj[:, 0:8, :]
+            for k in range(3):
+                v.edge[:, k : k + 1, :] = adj[:, 8 * k : 8 * k + 1, :]
 
             @pl.when(seq > 0)
             def _():
                 halo().start()
 
-            for_us(GELU, v.n1t, gg)
+            for_us(GELU, v.normt, gg)
             pump()
             s = slots[GATES]
             gates_pass = next_pass()
@@ -1521,12 +1560,19 @@
 
             @pl.when(seq == 7)
             def _():
-                adj[:, pl.ds(rows, 8), :] = jnp.zeros((tiles, 8, LANES), f32)
+                v.halo[...] = jnp.zeros((tiles, 8, LANES), f32)
 
             @pl.when(seq < 7)
             def _():
                 halo().wait_recv()
-                adj[:, pl.ds(rows, 8), :] = v.halo[...]
+
+            highest = lax.broadcasted_iota(jnp.int32, (8, LANES), 0) == 7
+
+            @pl.loop(0, tiles)
+            def _(c):
+                for k in range(3):
+                    tile = adj[c, 8 * k + 1 : 8 * k + 9, :]
+                    adj[c, rows + 8 * k : rows + 8 * (k + 1), :] = jnp.where(highest, v.halo[c, k : k + 1, :], tile)
 
             inside = pumps_at(tiles // 3, 2 * tiles // 3)
 
@@ -1540,15 +1586,15 @@
                     here = adj[c, r : r + 128, :]
                     acc = taps[0] * here
                     for k in range(4):
-                        sums[k] = sums[k] + eight(here * lin[8 + r - k : 8 + r - k + 128, :])
+                        sums[k] = sums[k] + eight(here * lin[RIM + r - 8 * k : RIM + r - 8 * k + 128, :])
                         if k:
-                            acc = acc + taps[k] * adj[c, r + k : r + k + 128, :]
+                            acc = acc + taps[k] * adj[c, r + 8 * k : r + 8 * k + 128, :]
                     gl[r : r + 128, lane] = low(acc)
                 for k in range(4):
                     part[k : k + 1, lane] = sums[k].sum(axis=0, keepdims=True)
 
             pltpu.emit_pipeline(
-                through_conv, grid=(tiles,), in_specs=[pl.BlockSpec((None, rows + 8, LANES), lambda t: (t, 0, 0))]
+                through_conv, grid=(tiles,), in_specs=[pl.BlockSpec((None, rows + RIM, LANES), lambda t: (t, 0, 0))]
             )(w.lin)
             pump()
             to_sib(gates_pass).wait_recv()
@@ -1562,10 +1608,10 @@
 
                 rows_loop(s.n, fold)
             give_credit(gates_pass)
-            for_sib(INPUT, v.n1t, gl)
-            for_sib(INPUT2, v.n1t, gl)
-            for_us(INPUT, v.n1t, gl)
-            for_us(INPUT2, v.n1t, gl)
+            for_sib(INPUT, v.normt, gl)
+            for_sib(INPUT2, v.normt, gl)
+            for_us(INPUT, v.normt, gl)
+            for_us(INPUT2, v.normt, gl)
             pump()
             inside = pumps_at(*range(1, width // wide_tile))
 
@@ -1594,34 +1640,49 @@
 
         pl.run_scoped(
             branch_phase,
-            pltpu.VMEM((tiles, rows + 8, LANES), f32),
+            pltpu.VMEM((tiles, rows + RIM, LANES), f32),
             pltpu.VMEM((tiles, rows, LANES), f32),
             pltpu.VMEM((rows, lru), bf),
             pltpu.VMEM((rows, lru), bf),
             pltpu.VMEM((rows, wide_tile), bf),
         )
         tot.begin()
-        cp = pltpu.make_async_copy(v.gn, out.tokens_grad, v.keep.at[count, 0])
-        cp.start()
-        kept.append(cp)
-
-        def mixed_phase(hidden):
+
+        def tokens_out():
+            return pltpu.make_async_copy(v.gn, out.tokens_grad, v.keep.at[count, 0])
+
+        def last_phase(hidden, order):
             hidden_load = load(w.hidden, hidden, 7)
+            order[...] = interleave(rows, True)
+
+            @pl.loop(0, width // wide_tile)
+            def _(t):
+                at = pl.ds(pl.multiple_of(t * wide_tile, wide_tile), wide_tile)
+                value = v.gn[:, at]
+                high = low(value)
+                rest = value - wide(high)
+                middle = low(rest)
+                lowest = low(rest - wide(middle))
+                v.gn[:, at] = (dot(order[...], high) + dot(order[...], middle)) + dot(order[...], lowest)
+
+            tokens_out().start()
             pump()
             inside = pumps_at(*range(1, width // wide_tile))
             hidden_load.wait()
 
             def body(wd, resid, mixed):
                 inside()
-                valid = lax.broadcasted_iota(jnp.int32, (rows, wide_tile), 0) < valid_rows
-                mixed[...] = low(jnp.where(valid, resid[...] + dot(hidden[...], wd[...]), 0.0))
+                value = dot(order[...], low(resid[...] + dot(hidden[...], wd[...])))
+                here = lax.broadcasted_iota(jnp.int32, (rows, wide_tile), 0) < valid_rows
+                mixed[...] = low(jnp.where(here, value, 0.0))
 
             across = pl.BlockSpec((rows, wide_tile), lambda t: (0, t))
             pltpu.emit_pipeline(
                 body, grid=(width // wide_tile,), in_specs=[pl.BlockSpec((ff, wide_tile), lambda t: (0, t)), across], out_specs=[across]
             )(w.mdown_w, w.resid, out.mixed)
 
-        pl.run_scoped(mixed_phase, pltpu.VMEM((rows, ff), bf))
+        kept.append(tokens_out())
+        pl.run_scoped(last_phase, pltpu.VMEM((rows, ff), bf), pltpu.VMEM((rows, rows), bf))
         summed = 0
         for k, (step, i, h) in enumerate(PUMPS[turn[0]]):
             steps[step](i, h)
@@ -1978,11 +2039,10 @@
     model_rows = jnp.stack([mixer_gain, mlp_gain]).astype(jnp.float32)
     across = lambda value, columns: jnp.pad(value, ((0, 0), (0, columns - value.shape[1])))
     small = jnp.concatenate([across(lru_rows, 256), across(model_rows, 256), jnp.zeros((6, 256), jnp.float32)], axis=0)
-    gates = jnp.concatenate([rgate_weight, igate_weight], axis=1)
     weights, saved = forward_call(
-        tokens, small, [gelu_weight, input_weight, gates, output_weight, mlp_gate, mlp_value, mlp_down]
-    )
-    (mixed, tokens_grad, small_sum), sums = backward_call(lengths, tokens, cotangent, weights, saved)
+        tokens, small, [rgate_weight, igate_weight], [gelu_weight, input_weight, output_weight, mlp_gate, mlp_value, mlp_down]
+    )
+    (mixed, tokens_grad, small_sum), sums = backward_call(lengths, cotangent, weights, saved)
     mixed, tokens_grad, down, mgate, mvalue, out_w, gelu_w, input_w, rgates, igates = finish_call([mixed, tokens_grad], sums)
     lru_own, model_own = small_sum[:8, : conv_bias.shape[0]], small_sum[8:10, : mixer_gain.shape[0]]
     return (

time: 334 us -> 318 us (0.952)
  Pallas kernels: 320 us -> 303 us
    pallas_call x1, Pallas kernels: 179 us -> 170 us  [backward_call(): pl.pallas_call(kernel, out_shape=list(outs.values()) + sums, in_specs=[pl...]
    pallas_call x1, Pallas kernels: 133 us -> 126 us  [forward_call(): pl.pallas_call(kernel, out_shape=wholes + [saved[name] for name in names]...]
where the time goes in v6:
time: 318 us; the launch traced here: 313 us
  Pallas kernels  303 us (95%)
  local copies, waits for them, and re-layouts  7.39 us (2%)
    pallas_call x1, Pallas kernels, backward_call(): pl.pallas_call(kernel, out_shape=list(outs.values()) + sums, in_specs=[pl...  170 us
    pallas_call x1, Pallas kernels, forward_call(): pl.pallas_call(kernel, out_shape=wholes + [saved[name] for name in names]...  126 us
    pallas_call x1, Pallas kernels, finish_call(): pl.pallas_call(kernel, grid=(parts,), out_shape=outs, in_specs=[block(v)...  6.95 us

profile of v6, /device:TPU:0, one launch (start us, length us, event | category | flops | bytes accessed | tf_op | source)
XLA Modules:
  0.0 312.6 jit_solution(11341103692645328561)
XLA Ops:
  0.7 0.1 pad.20.clone
  0.7 0.7 broadcast_in_dim.15
  1.4 0.7 broadcast_in_dim.16
  2.1 0.7 broadcast_in_dim.17
  2.7 0.7 broadcast_in_dim.18
  3.4 0.7 concatenate.6
  4.1 0.7 fusion.3
  4.8 0.7 maximum_maximum_fusion.small_ref
  5.4 126.4 %forward.1 = (bf16[1024,1536]{1,0:T(8,128)(2,1)}, bf16[1024,1536]{1,0:T(8,128)(2,1)}, bf16[1536,256]{1,0:T(8,128)(2,1)}, bf16[1536,1024]{1,0:T(8,128)(2,1)}, bf1...) custom-call(bf16[512,1024]{1,0:T(8,128)(2,1)} %tokens_ref.1, ...), custom_call_target="tpu_custom_call" | custom-call | tf_op jit(solution)/shard_map/forward/pallas_call | solution.py:1045
  131.8 169.7 %backward.1 = (bf16[512,1024]{1,0:T(8,128)(2,1)}, f32[512,1024]{1,0:T(8,128)}, f32[16,256]{1,0:T(8,128)}, bf16[384,1024]{1,0:T(8,128)(2,1)}, bf16[128,3072]{1,0:...) custom-call(s32[4]{0:T(128)} %lengths_ref.1, ...), custom_call_target="tpu_custom_call" | custom-call | tf_op jit(solution)/shard_map/backward/pallas_call | solution.py:1718
  301.6 1.3 slice_bitcast_fusion.1
  302.8 1.3 slice_bitcast_fusion
  304.1 1.4 fusion.4
  305.5 6.9 %finish.1 = (bf16[512,1024]{1,0:T(8,128)(2,1)}, f32[512,1024]{1,0:T(8,128)}, f32[384,1024]{1,0:T(8,128)}, f32[128,3072]{1,0:T(8,128)}, f32[128,3072]{1,0:T(8,128...) custom-call(bf16[512,1024]{1,0:T(8,128)(2,1)} %get-tuple-element.89., ...), custom_call_target="tpu_custom_call" | custom-call | tf_op jit(solution)/shard_map/finish/pallas_call | solution.py:1745
  (2 shorter events, 0.0 us)
